TPU v7x, 32 devices: a whole 2x2x4 slice. The times are simulated.
32 devices in a mesh: gx: 8 (over z, y), gy: 4 (over x, core).
Axes of the slice: x: 2, y: 2, z: 4, core: 2. Of those that a mesh axis runs over, the one named last changes fastest.
Arguments:
- tokens: bfloat16 [48, 24, 8, 384], P('gx', 'gy'), may hold values from -6 to 6
- upstream: bfloat16 [48, 24, 8, 384], P('gx', 'gy'), may hold values from -41 to 41
- window_labels: int32 [48, 24, 8], P('gx', 'gy'), may hold values from 0 to 2
- ln1_gain: float32 [384], replicated, may hold values from 0.5 to 1.5
- w_qkv: bfloat16 [384, 1152], replicated, as said below
- w_proj: bfloat16 [384, 384], replicated, may hold values from -0.3125 to 0.3125
- ln2_gain: float32 [384], replicated, may hold values from 0.5 to 1.5
- w_fc1: bfloat16 [384, 1536], replicated, may hold values from -0.3125 to 0.3125
- b_fc1: float32 [1536], replicated, may hold values from -3 to 3
- w_fc2: bfloat16 [1536, 384], replicated, may hold values from -0.15625 to 0.15625
Outputs:
- d_tokens: bfloat16 [48, 24, 8, 384], P('gx', 'gy')
- g_ln1: float32 [384], replicated
- g_qkv: bfloat16 [384, 1152], replicated
- g_proj: bfloat16 [384, 384], replicated
- g_ln2: float32 [384], replicated
- g_fc1: bfloat16 [384, 1536], replicated
- g_bfc1: float32 [1536], replicated
- g_fc2: bfloat16 [1536, 384], replicated
Inputs may be any that keep to these rules, and one draw needn't show every extreme that they name: `w_qkv`: entries at most 28 / sqrt(384) in magnitude.
All inputs are finite; a program needn't handle non-finite values.
Results may differ from a plain program's by a relative error of at most 0.019.
Values may be sent and summed in bfloat16 or wider, within the bound.
No kernel may reach another device: no remote copies, remote signals or barrier semaphores. Data moves between devices by JAX's collectives and lax.ppermute only.
A program may use at most 128 MiB of HBM per device.

v0:
```python
import math

import jax
import jax.numpy as jnp
from jax import lax
from jax.sharding import PartitionSpec as P

HD = 32
WZ = 8


EPS = 1e-05
CUBIC = 0.044715
ROOT_TWO_PI = math.sqrt(2.0 / math.pi)


def shifted(shard, axis, by):
    size = lax.axis_size(axis)
    return lax.ppermute(shard, axis, [(i, (i + by) % size) for i in range(size)])


def row_stats(values):
    row_mean = jnp.mean(values, axis=-1, keepdims=True)
    center = values - row_mean
    variance = jnp.mean(center * center, axis=-1, keepdims=True)
    inv_std = lax.rsqrt(variance + EPS)
    return (center * inv_std, inv_std)


def norm_back(incoming, normed, inv_std, gain_vec):
    scaled = incoming * gain_vec
    first_mean = jnp.mean(scaled, axis=-1, keepdims=True)
    second_mean = jnp.mean(scaled * normed, axis=-1, keepdims=True)
    flat_terms = (incoming * normed).reshape(-1, incoming.shape[-1])
    return (inv_std * (scaled - first_mean - normed * second_mean), jnp.sum(flat_terms, axis=0))


def gelu_pair(preact):
    cubic_arg = ROOT_TWO_PI * (preact + CUBIC * preact * preact * preact)
    tanh_value = jnp.tanh(cubic_arg)
    gelu_value = 0.5 * preact * (1.0 + tanh_value)
    gelu_slope = 0.5 * (1.0 + tanh_value) + 0.5 * preact * (
        1.0 - tanh_value * tanh_value
    ) * ROOT_TWO_PI * (1.0 + 3.0 * CUBIC * preact * preact)
    return (gelu_value, gelu_slope)


def to_windows(grid_tile, win_depth):
    tile_x, tile_y, tile_z = grid_tile.shape[:3]
    trailing = grid_tile.shape[3:]
    blocks = tile_z // win_depth
    shaped = grid_tile.reshape((tile_x, tile_y, blocks, win_depth) + trailing)
    axes_order = (2, 0, 1, 3) + tuple(range(4, 4 + len(trailing)))
    return shaped.transpose(axes_order).reshape((blocks, tile_x * tile_y * win_depth) + trailing)


def from_windows(win_rows, tile_x, tile_y, win_depth):
    blocks = win_rows.shape[0]
    trailing = win_rows.shape[2:]
    shaped = win_rows.reshape((blocks, tile_x, tile_y, win_depth) + trailing)
    axes_order = (1, 2, 0, 3) + tuple(range(4, 4 + len(trailing)))
    return shaped.transpose(axes_order).reshape((tile_x, tile_y, blocks * win_depth) + trailing)


def roll_ahead(grid_tile, dim_x):
    half_size = grid_tile.shape[dim_x] // 2
    arrived = shifted(lax.slice_in_dim(grid_tile, 0, half_size, axis=dim_x), "gx", -1)
    grid_tile = jnp.concatenate(
        (lax.slice_in_dim(grid_tile, half_size, grid_tile.shape[dim_x], axis=dim_x), arrived),
        axis=dim_x,
    )
    dim_y = dim_x + 1
    half_size = grid_tile.shape[dim_y] // 2
    arrived = shifted(lax.slice_in_dim(grid_tile, 0, half_size, axis=dim_y), "gy", -1)
    grid_tile = jnp.concatenate(
        (lax.slice_in_dim(grid_tile, half_size, grid_tile.shape[dim_y], axis=dim_y), arrived),
        axis=dim_y,
    )
    return jnp.roll(grid_tile, -(WZ // 2), axis=dim_x + 2)


def unroll_wide(grid_tile):
    grid_tile = jnp.roll(grid_tile, WZ // 2, axis=2)
    size_x = grid_tile.shape[0]
    keep_x = size_x - size_x // 2
    arrived = shifted(grid_tile[keep_x:].astype(jnp.bfloat16), "gx", 1).astype(jnp.float32)
    grid_tile = jnp.concatenate((arrived, grid_tile[:keep_x]), axis=0)
    size_y = grid_tile.shape[1]
    keep_y = size_y - size_y // 2
    arrived = shifted(grid_tile[:, keep_y:].astype(jnp.bfloat16), "gy", 1).astype(jnp.float32)
    return jnp.concatenate((arrived, grid_tile[:, :keep_y]), axis=1)


def attend_forward(h_rows, region_codes, w_qkv, w_proj):
    blocks, length, model_width = h_rows.shape
    head_count = model_width // HD
    score_scale = HD ** (-0.5)
    packed = jnp.dot(
        h_rows.reshape(-1, model_width), w_qkv, preferred_element_type=jnp.float32
    ).astype(jnp.bfloat16)
    packed = packed.reshape(blocks, length, 3, head_count, HD)
    queries = packed[:, :, 0]
    key_part = packed[:, :, 1]
    val_part = packed[:, :, 2]
    allowed = (region_codes[:, :, None] == region_codes[:, None, :])[:, None]
    scores = (
        jnp.einsum("bqhe,bkhe->bhqk", queries, key_part, preferred_element_type=jnp.float32)
        * score_scale
    )
    scores = jnp.where(allowed, scores, -1e30)
    highest = jnp.max(scores, axis=-1, keepdims=True)
    exp_scores = jnp.exp(scores - highest)
    probs = exp_scores / jnp.sum(exp_scores, axis=-1, keepdims=True)
    probs_low = probs.astype(jnp.bfloat16)
    head_mix = jnp.einsum(
        "bhqk,bkhe->bqhe", probs_low, val_part, preferred_element_type=jnp.float32
    ).astype(jnp.bfloat16)
    head_mix = head_mix.reshape(blocks * length, model_width)
    attn_out = jnp.dot(head_mix, w_proj, preferred_element_type=jnp.float32).reshape(
        blocks, length, model_width
    )
    return (attn_out, (queries, key_part, val_part, probs, probs_low, head_mix))


def attend_backward(grad_rows, saved, h_rows, w_qkv, w_proj):
    queries, key_part, val_part, probs, probs_low, head_mix = saved
    blocks, length, model_width = grad_rows.shape
    head_count = model_width // HD
    score_scale = HD ** (-0.5)
    flat_grad = grad_rows.reshape(-1, model_width)
    grad_proj = jnp.dot(head_mix.T, flat_grad, preferred_element_type=jnp.float32)
    grad_mix = jnp.dot(flat_grad, w_proj.T, preferred_element_type=jnp.float32).astype(jnp.bfloat16)
    grad_mix = grad_mix.reshape(blocks, length, head_count, HD)
    grad_probs = jnp.einsum(
        "bqhe,bkhe->bhqk", grad_mix, val_part, preferred_element_type=jnp.float32
    )
    grad_val = jnp.einsum(
        "bhqk,bqhe->bkhe", probs_low, grad_mix, preferred_element_type=jnp.float32
    )
    grad_scores = probs * (grad_probs - jnp.sum(probs * grad_probs, axis=-1, keepdims=True))
    grad_low = (grad_scores * score_scale).astype(jnp.bfloat16)
    grad_query = jnp.einsum(
        "bhqk,bkhe->bqhe", grad_low, key_part, preferred_element_type=jnp.float32
    )
    grad_key = jnp.einsum("bhqk,bqhe->bkhe", grad_low, queries, preferred_element_type=jnp.float32)
    grad_packed = (
        jnp.stack((grad_query, grad_key, grad_val), axis=2)
        .astype(jnp.bfloat16)
        .reshape(-1, 3 * model_width)
    )
    grad_qkv = jnp.dot(
        h_rows.reshape(-1, model_width).T, grad_packed, preferred_element_type=jnp.float32
    )
    grad_input = jnp.dot(grad_packed, w_qkv.T, preferred_element_type=jnp.float32).reshape(
        blocks, length, model_width
    )
    return (grad_input, grad_qkv, grad_proj)


def mlp_backward(wide_tok, attn_out, up_tok, ln2_gain, w_fc1, b_fc1, w_fc2):
    model_width = wide_tok.shape[-1]
    lead_shape = wide_tok.shape[:-1]
    resid_mid = (wide_tok + attn_out).astype(jnp.bfloat16)
    normed, inv_std = row_stats(resid_mid.astype(jnp.float32))
    hidden_in = (normed * ln2_gain).astype(jnp.bfloat16).reshape(-1, model_width)
    preact = jnp.dot(hidden_in, w_fc1, preferred_element_type=jnp.float32) + b_fc1
    gelu_value, gelu_slope = gelu_pair(preact)
    hidden = gelu_value.astype(jnp.bfloat16)
    flat_up = up_tok.reshape(-1, model_width)
    grad_fc2 = jnp.dot(hidden.T, flat_up, preferred_element_type=jnp.float32)
    grad_pre = (jnp.dot(flat_up, w_fc2.T, preferred_element_type=jnp.float32) * gelu_slope).astype(
        jnp.bfloat16
    )
    grad_bias = jnp.sum(grad_pre.astype(jnp.float32), axis=0)
    grad_fc1 = jnp.dot(hidden_in.T, grad_pre, preferred_element_type=jnp.float32)
    grad_norm = jnp.dot(grad_pre, w_fc1.T, preferred_element_type=jnp.float32).reshape(
        lead_shape + (model_width,)
    )
    grad_mid, grad_gain2 = norm_back(grad_norm, normed, inv_std, ln2_gain)
    grad_res = up_tok.astype(jnp.float32) + grad_mid
    return (grad_res, (grad_gain2, grad_fc1, grad_bias, grad_fc2))


def body(tokens, upstream, window_labels, ln1_gain, w_qkv, w_proj, ln2_gain, w_fc1, b_fc1, w_fc2):
    tile_x, tile_y, tile_z, model_width = tokens.shape
    last_x = lax.axis_index("gx") == lax.axis_size("gx") - 1
    last_y = lax.axis_index("gy") == lax.axis_size("gy") - 1
    wrap_x = (last_x & (jnp.arange(tile_x) >= tile_x - tile_x // 2)).astype(jnp.int32)
    wrap_y = (last_y & (jnp.arange(tile_y) >= tile_y - tile_y // 2)).astype(jnp.int32)
    wrap_z = (jnp.arange(tile_z) >= tile_z - WZ // 2).astype(jnp.int32)
    code_tile = (
        window_labels * 8
        + wrap_x[:, None, None] * 4
        + wrap_y[None, :, None] * 2
        + wrap_z[None, None, :]
    )
    region_codes = to_windows(code_tile, WZ)
    wide_tok = tokens.astype(jnp.float32)
    normed_first, inv_first = row_stats(wide_tok)
    h_first = (normed_first * ln1_gain).astype(jnp.bfloat16)
    h_rows = to_windows(roll_ahead(h_first, 0), WZ)
    attn_rows, saved = attend_forward(h_rows, region_codes, w_qkv, w_proj)
    attn_tile = unroll_wide(from_windows(attn_rows, tile_x, tile_y, WZ))
    grad_res, mlp_grads = mlp_backward(wide_tok, attn_tile, upstream, ln2_gain, w_fc1, b_fc1, w_fc2)
    grad_attn = grad_res.astype(jnp.bfloat16)
    grad_rows = to_windows(roll_ahead(grad_attn, 0), WZ)
    input_rows, grad_qkv, grad_proj = attend_backward(grad_rows, saved, h_rows, w_qkv, w_proj)
    grad_first = unroll_wide(from_windows(input_rows, tile_x, tile_y, WZ))
    grad_tok, grad_gain1 = norm_back(grad_first, normed_first, inv_first, ln1_gain)
    result = (grad_res + grad_tok).astype(jnp.bfloat16)
    grad_gain2, grad_fc1, grad_bias, grad_fc2 = mlp_grads
    local_grads = (grad_gain1, grad_qkv, grad_proj, grad_gain2, grad_fc1, grad_bias, grad_fc2)
    param_total = 0
    for grad_term in local_grads:
        param_total = param_total + math.prod(grad_term.shape)
    summed = lax.psum(
        (
            local_grads[0],
            local_grads[1],
            local_grads[2],
            local_grads[3],
            local_grads[4],
            local_grads[5],
            local_grads[6],
        ),
        ("gx", "gy"),
    )
    square_sum = jnp.zeros((), jnp.float32)
    for grad_term in summed:
        square_sum = square_sum + jnp.sum(grad_term * grad_term)
    factor = math.sqrt(param_total) * lax.rsqrt(square_sum)
    scaled = tuple((grad_term * factor for grad_term in summed))
    return (
        result,
        scaled[0],
        scaled[1].astype(jnp.bfloat16),
        scaled[2].astype(jnp.bfloat16),
        scaled[3],
        scaled[4].astype(jnp.bfloat16),
        scaled[5],
        scaled[6].astype(jnp.bfloat16),
    )


def solution(mesh):
    return jax.shard_map(
        body,
        mesh=mesh,
        in_specs=(
            P("gx", "gy", None, None),
            P("gx", "gy", None, None),
            P("gx", "gy", None),
            P(),
            P(),
            P(),
            P(),
            P(),
            P(),
            P(),
        ),
        out_specs=(P("gx", "gy", None, None), P(), P(), P(), P(), P(), P(), P()),
        check_vma=False,
    )
```

profile of v0, /device:TPU:0, one launch (start us, length us, event | category | flops | bytes accessed | tf_op | source)
XLA Modules:
  0.0 288.3 jit_solution(15074106265206905131)
XLA Ops:
  7.2 1.2 convert_reduce_fusion.1
  8.4 1.2 fusion.67
  9.6 1.1 fusion.60
  10.7 6.1 %collective-permute-start = (bf16[3,6,8,384]{3,2,1,0:T(8,128)(2,1)S(1)}, bf16[3,6,8,384]{3,2,1,0:T(8,128)(2,1)S(1)}, u32[]{:S(2)}, u32[]{:S(2)}) collective-permute-start(bf16[3,6,8,384]{3,2,1,0:T(8,128)(2,1)S(1)} %get-tuple-element.33), channel_id=1, source_target_pairs={{0,28},{4,0},{8,4},{12,8},{16,12},{20,16},{24,20},{28,24},{1,29},{... | collective-permute-start | bytes 331784 | tf_op jit(solution)/shard_map/ppermute | solution.py:19
  16.8 0.8 add_add_fusion
  17.7 1.4 collective-permute-done
  19.4 2.2 collective-permute-done.1
  22.8 4.2 %fusion.108 = (f32[12,288]{1,0:T(8,128)S(1)}, f32[12,288,288]{1,2,0:T(8,128)}) fusion(pred[288,288]{0,1:T(8,128)(4,1)S(1)} %broadcast_compare_fusion, bf16[1,288,3,12,32]{1,4,3,2,0:T(8,128)(2,1)S(1)} %bitcast.100), kind=kOutput, calls=%fused_computation.164 | convolution fusion | flops 67682592 | bytes 4695552 | tf_op jit(solution)/shard_map/sub | solution.py:112
  27.0 3.1 %fusion.36 = bf16[12,32,288]{2,1,0:T(8,128)(2,1)S(1)} fusion(bf16[1,288,3,12,32]{1,4,3,2,0:T(8,128)(2,1)S(1)} %bitcast.101, f32[12,288,288]{1,2,0:T(8,128)} %get-tuple-element.35, f32[12,288]{1,0:T(8,128)S(1)} %get-tuple-element.34), kind=kOutput, calls=%fused_computation.43 | convolution fusion | flops 65802240 | bytes 4521984 | tf_op jit(solution)/shard_map/bhqk,bkhe->bqhe/dot_general | solution.py:115
  30.1 1.1 copy.31
  31.2 0.8 dot_general.62
  32.9 7.8 %collective-permute-done.2 = bf16[3,6,8,384]{3,2,1,0:T(8,128)(2,1)S(1)} collective-permute-done((bf16[3,6,8,384]{3,2,1,0:T(8,128)(2,1)S(1)}, bf16[3,6,8,384]{3,2,1,0:T(8,128)(2,1)S(1)}, u32[]{:S(2)}, u32[]{:S(2)}) %collective-permute-start.2) | collective-permute-done | bytes 110624 | tf_op jit(solution)/shard_map/ppermute | solution.py:19
  40.8 0.8 collective-permute-start.3
  41.6 3.6 %collective-permute-done.3 = bf16[6,3,8,384]{3,2,1,0:T(8,128)(2,1)S(1)} collective-permute-done((bf16[6,3,8,384]{3,2,1,0:T(8,128)(2,1)S(1)}, bf16[6,3,8,384]{3,2,1,0:T(8,128)(2,1)S(1)}, u32[]{:S(2)}, u32[]{:S(2)}) %collective-permute-start.3) | collective-permute-done | bytes 110624 | tf_op jit(solution)/shard_map/ppermute | solution.py:19
  45.9 0.6 convolution_add_fusion
  46.7 2.0 convert_reduce_fusion
  48.8 0.9 copy-done.15
  49.7 0.7 multiply_reduce_fusion.5
  50.4 0.8 fusion.73
  51.6 2.1 collective-permute-start.4
  53.8 4.1 %fusion.39 = f32[1536,384]{1,0:T(8,128)} fusion(bf16[288,384]{1,0:T(8,128)(2,1)S(1)} %bitcast.110, f32[288,1536]{1,0:T(8,128)} %copy-done.7), kind=kOutput, calls=%fused_computation.45 | convolution fusion | flops 343719936 | bytes 4349952 | tf_op jit(solution)/shard_map/dot_general | solution.py:170
  58.1 2.2 fusion.111
  60.9 0.9 copy.32
  61.8 4.2 %fusion.33 = bf16[1,288,1,12,32]{1,4,3,2,0:T(8,128)(2,1)} fusion(bf16[288,12,32]{0,2,1:T(8,128)(2,1)} %bitcast.105, f32[12,288,288]{1,2,0:T(8,128)} %get-tuple-element.35, f32[12,288]{1,0:T(8,128)} %copy-done.27), kind=kOutput, calls=%fused_computation.42 | convolution fusion | flops 65691648 | bytes 4437504 | tf_op jit(solution)/shard_map/bhqk,bqhe->bkhe/dot_general | solution.py:137
  66.0 3.2 %fusion.80 = f32[12,288,288]{1,2,0:T(8,128)} fusion(bf16[288,12,32]{0,2,1:T(8,128)(2,1)S(1)} %bitcast.106, bf16[1,288,3,12,32]{1,4,3,2,0:T(8,128)(2,1)S(1)} %bitcast.102), kind=kOutput, calls=%fused_computation.104 | convolution fusion | flops 63700992 | bytes 4571136 | tf_op jit(solution)/shard_map/bqhe,bkhe->bhqk/dot_general | solution.py:134
  69.3 9.4 %fusion.30 = bf16[1,288,1,12,32]{1,4,3,2,0:T(8,128)(2,1)} fusion(f32[12,288,288]{1,2,0:T(8,128)} %fusion.80, bf16[1,288,3,12,32]{1,4,3,2,0:T(8,128)(2,1)S(1)} %bitcast.103, f32[12,288,288]{1,2,0:T(8,128)} %get-tuple-element.35, f32[12,288]{1,0:T(8,128)} %copy-done.27), kind=kOutput, calls=%fused_computation.41 | convolution fusion | flops 70672032 | bytes 21798912 | tf_op jit(solution)/shard_map/bhqk,bqhe->bkhe/dot_general | solution.py:145
  78.7 9.4 %fusion.27 = bf16[1,288,1,12,32]{1,4,3,2,0:T(8,128)(2,1)} fusion(f32[12,288,288]{1,2,0:T(8,128)} %fusion.80, bf16[1,288,3,12,32]{1,4,3,2,0:T(8,128)(2,1)S(1)} %bitcast.104, f32[12,288,288]{1,2,0:T(8,128)} %get-tuple-element.35, f32[12,288]{1,0:T(8,128)} %copy-done.27), kind=kOutput, calls=%fused_computation.40 | convolution fusion | flops 70672032 | bytes 21798912 | tf_op jit(solution)/shard_map/bhqk,bkhe->bqhe/dot_general | solution.py:142
  88.1 1.4 maximum_convert_fusion
  89.4 1.9 fusion.109
  91.4 1.1 fusion.110
  92.5 4.4 %copy.36 = bf16[1,288,3,12,32]{4,3,2,1,0:T(8,128)(2,1)} copy(bf16[1,288,3,12,32]{1,4,3,2,0:T(8,128)(2,1)S(1)} %maximum_convert_fusion) | data formatting | bytes 1327104 | tf_op jit(solution)/shard_map/convert_element_type | solution.py:148
  96.9 5.2 %convert_element_type.139 = bf16[6,6,8,1152]{3,2,1,0:T(8,128)(2,1)} reshape(bf16[1,288,3,12,32]{4,3,2,1,0:T(8,128)(2,1)} %copy.36) | data formatting | bytes 1327104 | tf_op jit(solution)/shard_map/convert_element_type | solution.py:148
  102.1 1.6 fusion.40
  104.0 10.6 %collective-permute-done.6 = bf16[3,6,8,384]{3,2,1,0:T(8,128)(2,1)S(1)} collective-permute-done((bf16[3,6,8,384]{3,2,1,0:T(8,128)(2,1)S(1)}, bf16[3,6,8,384]{3,2,1,0:T(8,128)(2,1)S(1)}, u32[]{:S(2)}, u32[]{:S(2)}) %collective-permute-start.6) | collective-permute-done | bytes 110624 | tf_op jit(solution)/shard_map/ppermute | solution.py:19
  114.6 1.1 collective-permute-start.7
  115.8 4.9 %collective-permute-done.7 = bf16[6,3,8,384]{3,2,1,0:T(8,128)(2,1)S(1)} collective-permute-done((bf16[6,3,8,384]{3,2,1,0:T(8,128)(2,1)S(1)}, bf16[6,3,8,384]{3,2,1,0:T(8,128)(2,1)S(1)}, u32[]{:S(2)}, u32[]{:S(2)}) %collective-permute-start.7) | collective-permute-done | bytes 110624 | tf_op jit(solution)/shard_map/ppermute | solution.py:19
  121.0 38.2 %all-reduce = (f32[384]{0:T(512)S(1)}, f32[384]{0:T(512)S(1)}, f32[1536]{0:T(1024)S(1)}) all-reduce(f32[384]{0:T(512)S(1)} %get-tuple-element.10, f32[384]{0:T(512)} %get-tuple-element.8, f32[1536]{0:T(1024)} %get-tuple-element.38), channel_id=1, replica_groups=mesh['gx'=8,'gy'=4] {'gx','gy'}, use_global_device_ids=true, to_apply=%region_12.13 | all-reduce | flops 2304 | bytes 18432 | tf_op jit(solution)/shard_map/psum | solution.py:216
  160.4 0.7 multiply_reduce_fusion.7
  161.1 1.1 fusion.65
  162.2 98.9 %all-reduce.4.cloned.1.call-done = (f32[384,1152]{1,0:T(8,128)}, f32[384,384]{1,0:T(8,128)}, f32[384,1536]{1,0:T(8,128)}, f32[1536,384]{1,0:T(8,128)}) async-done(((f32[384,1152]{1,0:T(8,128)}, f32[384,384]{1,0:T(8,128)}, f32[384,1536]{1,0:T(8,128)}, f32[1536,384]{1,0:T(8,128)}), (f32[384,1152]{1,0:T(8,128)}, f32[384,384]{1,0:T(8,128)}, f32[384,1536]{1,0:T(8,128)}, ...) | async-done | bytes 7077904 | tf_op jit(solution)/shard_map/psum | solution.py:216
  261.1 2.7 multiply_reduce_fusion.3
  263.8 1.8 multiply_reduce_fusion.4
  265.6 1.2 multiply_reduce_fusion.2
  266.8 1.3 multiply_reduce_fusion.1
  273.4 2.6 multiply_convert_fusion.3
  276.0 1.8 multiply_convert_fusion.6
  278.4 1.2 multiply_convert_fusion.2
  280.2 1.2 multiply_convert_fusion.1
  (112 shorter events, 8.2 us)
Async XLA Ops:
  7.2 38.7 %copy-start = (bf16[384,1536]{1,0:T(8,128)(2,1)S(1)}, bf16[384,1536]{1,0:T(8,128)(2,1)}, u32[]{:S(2)}) copy-start(bf16[384,1536]{1,0:T(8,128)(2,1)} %param.17) | copy-start | bytes 3538948
  7.2 14.6 %copy-start.5 = (bf16[384,1152]{1,0:T(8,128)(2,1)S(1)}, bf16[384,1152]{1,0:T(8,128)(2,1)}, u32[]{:S(2)}) copy-start(bf16[384,1152]{1,0:T(8,128)(2,1)} %param.14) | copy-start | bytes 2654212
  7.2 253.9 %all-reduce.4.cloned.1.call-start = ((), (), s32[]{:S(2)}) async-start(), calls=%async_computation | async-start | bytes 14155776 | tf_op jit(solution)/shard_map/psum | solution.py:216
  10.7 8.4 %collective-permute-start = (bf16[3,6,8,384]{3,2,1,0:T(8,128)(2,1)S(1)}, bf16[3,6,8,384]{3,2,1,0:T(8,128)(2,1)S(1)}, u32[]{:S(2)}, u32[]{:S(2)}) collective-permute-start(bf16[3,6,8,384]{3,2,1,0:T(8,128)(2,1)S(1)} %get-tuple-element.33), channel_id=1, source_target_pairs={{0,28},{4,0},{8,4},{12,8},{16,12},{20,16},{24,20},{28,24},{1,29},{... | collective-permute-start | bytes 331784 | tf_op jit(solution)/shard_map/ppermute | solution.py:19
  19.2 2.5 collective-permute-start.1
  22.8 4.2 %copy-start.8 = (bf16[288,1152]{0,1:T(8,128)(2,1)}, bf16[288,1152]{0,1:T(8,128)(2,1)S(1)}, u32[]{:S(2)}) copy-start(bf16[288,1152]{0,1:T(8,128)(2,1)S(1)} %copy.29) | copy-start | bytes 1990660
  27.0 3.1 %copy-start.27 = (f32[12,288]{1,0:T(8,128)}, f32[12,288]{1,0:T(8,128)S(1)}, u32[]{:S(2)}) copy-start(f32[12,288]{1,0:T(8,128)S(1)} %get-tuple-element.34) | copy-start | bytes 41476
  30.1 2.4 copy-start.13
  30.1 1.9 copy-start.11
  32.0 13.3 %copy-start.4 = (bf16[6,6,8,384]{3,2,1,0:T(8,128)(2,1)S(1)}, bf16[6,6,8,384]{3,2,1,0:T(8,128)(2,1)}, u32[]{:S(2)}) copy-start(bf16[6,6,8,384]{3,2,1,0:T(8,128)(2,1)} %param.10) | copy-start | bytes 663556
  32.4 13.4 %copy-start.19 = (f32[384]{0:T(512)S(1)}, f32[384]{0:T(512)}, u32[]{:S(2)}) copy-start(f32[384]{0:T(512)} %param.16) | copy-start | bytes 4612
  32.5 13.5 %copy-start.21 = (f32[1536]{0:T(1024)S(1)}, f32[1536]{0:T(1024)}, u32[]{:S(2)}) copy-start(f32[1536]{0:T(1024)} %param.18) | copy-start | bytes 18436
  32.5 8.2 %collective-permute-start.2 = (bf16[3,6,8,384]{3,2,1,0:T(8,128)(2,1)S(1)}, bf16[3,6,8,384]{3,2,1,0:T(8,128)(2,1)S(1)}, u32[]{:S(2)}, u32[]{:S(2)}) collective-permute-start(bf16[3,6,8,384]{3,2,1,0:T(8,128)(2,1)S(1)} %fusion.85), channel_id=1, source_target_pairs={{0,4},{4,8},{8,12},{12,16},{16,20},{20,24},{24,28},{28,0},{1,5},{5... | collective-permute-start | bytes 331784 | tf_op jit(solution)/shard_map/ppermute | solution.py:19
  40.8 4.5 %collective-permute-start.3 = (bf16[6,3,8,384]{3,2,1,0:T(8,128)(2,1)S(1)}, bf16[6,3,8,384]{3,2,1,0:T(8,128)(2,1)S(1)}, u32[]{:S(2)}, u32[]{:S(2)}) collective-permute-start(bf16[6,3,8,384]{3,2,1,0:T(8,128)(2,1)S(1)} %slice.203), channel_id=1, source_target_pairs={{0,1},{1,2},{2,3},{3,0},{4,5},{5,6},{6,7},{7,4},{8,9},{9,10},{10,1... | collective-permute-start | bytes 331784 | tf_op jit(solution)/shard_map/ppermute | solution.py:19
  45.3 1.2 copy-start.17
  45.3 1.4 copy-start.26
  46.5 2.2 copy-start.7
  48.8 0.9 copy-start.15
  51.6 6.5 %copy-start.16 = (bf16[288,1536]{1,0:T(8,128)(2,1)S(1)}, bf16[288,1536]{1,0:T(8,128)(2,1)}, u32[]{:S(2)}) copy-start(bf16[288,1536]{1,0:T(8,128)(2,1)} %copy-done.15) | copy-start | bytes 2654212
  51.6 6.2 %collective-permute-start.4 = (bf16[3,6,8,384]{3,2,1,0:T(8,128)(2,1)S(1)}, bf16[3,6,8,384]{3,2,1,0:T(8,128)(2,1)S(1)}, u32[]{:S(2)}, u32[]{:S(2)}) collective-permute-start(bf16[3,6,8,384]{3,2,1,0:T(8,128)(2,1)S(1)} %get-tuple-element.29), channel_id=1, source_target_pairs={{0,28},{4,0},{8,4},{12,8},{16,12},{20,16},{24,20},{28,24},{1,29},{... | collective-permute-start | bytes 331784 | tf_op jit(solution)/shard_map/ppermute | solution.py:19
  57.8 2.8 copy-start.12
  57.8 2.6 collective-permute-start.5
  61.8 4.2 %copy-start.9 = (bf16[288,1152]{0,1:T(8,128)(2,1)S(1)}, bf16[288,1152]{0,1:T(8,128)(2,1)}, u32[]{:S(2)}) copy-start(bf16[288,1152]{0,1:T(8,128)(2,1)} %copy-done.8) | copy-start | bytes 1990660
  61.8 4.2 %copy-start.10 = (bf16[288,384]{0,1:T(8,128)(2,1)S(1)}, bf16[288,384]{0,1:T(8,128)(2,1)}, u32[]{:S(2)}) copy-start(bf16[288,384]{0,1:T(8,128)(2,1)} %copy.32) | copy-start | bytes 663556
  88.1 3.3 %copy-start.14 = (bf16[12,32,288]{2,1,0:T(8,128)(2,1)S(1)}, bf16[12,32,288]{2,1,0:T(8,128)(2,1)}, u32[]{:S(2)}) copy-start(bf16[12,32,288]{2,1,0:T(8,128)(2,1)} %copy-done.13) | copy-start | bytes 663556
  96.9 5.2 %copy-start.6 = (bf16[384,1152]{1,0:T(8,128)(2,1)S(1)}, bf16[384,1152]{1,0:T(8,128)(2,1)}, u32[]{:S(2)}) copy-start(bf16[384,1152]{1,0:T(8,128)(2,1)} %param.14) | copy-start | bytes 2654212
  103.7 16.9 %copy-start.20 = (f32[384]{0:T(512)S(1)}, f32[384]{0:T(512)}, u32[]{:S(2)}) copy-start(f32[384]{0:T(512)} %param.13) | copy-start | bytes 4612
  103.7 57.4 %copy-start.18 = (bf16[6,6,8,384]{3,2,1,0:T(8,128)(2,1)S(1)}, bf16[6,6,8,384]{3,2,1,0:T(8,128)(2,1)}, u32[]{:S(2)}) copy-start(bf16[6,6,8,384]{3,2,1,0:T(8,128)(2,1)} %param.11) | copy-start | bytes 663556
  103.9 10.6 %collective-permute-start.6 = (bf16[3,6,8,384]{3,2,1,0:T(8,128)(2,1)S(1)}, bf16[3,6,8,384]{3,2,1,0:T(8,128)(2,1)S(1)}, u32[]{:S(2)}, u32[]{:S(2)}) collective-permute-start(bf16[3,6,8,384]{3,2,1,0:T(8,128)(2,1)S(1)} %fusion.83), channel_id=1, source_target_pairs={{0,4},{4,8},{8,12},{12,16},{16,20},{20,24},{24,28},{28,0},{1,5},{5... | collective-permute-start | bytes 331784 | tf_op jit(solution)/shard_map/ppermute | solution.py:19
  114.6 6.0 %collective-permute-start.7 = (bf16[6,3,8,384]{3,2,1,0:T(8,128)(2,1)S(1)}, bf16[6,3,8,384]{3,2,1,0:T(8,128)(2,1)S(1)}, u32[]{:S(2)}, u32[]{:S(2)}) collective-permute-start(bf16[6,3,8,384]{3,2,1,0:T(8,128)(2,1)S(1)} %slice.202), channel_id=1, source_target_pairs={{0,1},{1,2},{2,3},{3,0},{4,5},{5,6},{6,7},{7,4},{8,9},{9,10},{10,1... | collective-permute-start | bytes 331784 | tf_op jit(solution)/shard_map/ppermute | solution.py:19
  159.2 1.9 copy-start.22
  159.2 1.9 copy-start.24
  261.1 4.5 %copy-start.2 = (f32[384,1536]{1,0:T(8,128)S(1)}, f32[384,1536]{1,0:T(8,128)}, u32[]{:S(2)}) copy-start(f32[384,1536]{1,0:T(8,128)} %get-tuple-element.18) | copy-start | bytes 7077892
  261.1 5.7 %copy-start.1 = (f32[1536,384]{1,0:T(8,128)S(1)}, f32[1536,384]{1,0:T(8,128)}, u32[]{:S(2)}) copy-start(f32[1536,384]{1,0:T(8,128)} %get-tuple-element.19) | copy-start | bytes 7077892
  265.6 7.2 %copy-start.25 = (f32[384]{0:T(512)S(1)}, f32[384]{0:T(512)}, u32[]{:S(2)}) copy-start(f32[384]{0:T(512)} %copy-done.24) | copy-start | bytes 4612
  268.1 9.7 %copy-start.23 = (f32[384]{0:T(512)S(1)}, f32[384]{0:T(512)}, u32[]{:S(2)}) copy-start(f32[384]{0:T(512)} %copy-done.22) | copy-start | bytes 4612
  272.8 5.6 %copy-start.3 = (f32[384,1536]{1,0:T(8,128)S(1)}, f32[384,1536]{1,0:T(8,128)}, u32[]{:S(2)}) copy-start(f32[384,1536]{1,0:T(8,128)} %get-tuple-element.18) | copy-start | bytes 7077892
Sparse Core Ops, SparseCore 0:
  92.6 168.4 all-reduce.3
where the time goes:
time: 289 us; the launch traced here: 288 us
  waiting for transfers between devices  130 us (45%)
  matrix products  49 us (17%)
  blocking collectives  38.2 us (13%)
  other arithmetic  27 us (9%)
  between operations  19.3 us (7%)
  local copies, waits for them, and re-layouts  14.4 us (5%)
  starting transfers between devices  11 us (4%)
    psum x1, waiting for transfers between devices, body(): lax.psum((local_grads[0], local_grads[1], local_grads[2], local_grads[3],...  98.9 us
    psum x1, blocking collectives, body(): lax.psum((local_grads[0], local_grads[1], local_grads[2], local_grads[3],...  38.2 us
    ppermute x8, waiting for transfers between devices, shifted(): lax.ppermute(shard, axis, [(i, (i + by) % size) for i in range(size)])  30.6 us
    ppermute x8, starting transfers between devices, shifted(): lax.ppermute(shard, axis, [(i, (i + by) % size) for i in range(size)])  10.9 us
    convert_element_type x2, local copies, waits for them, and re-layouts, attend_backward(): grad_packed = jnp.stack((grad_query, grad_key, grad_val), axis=2).astype(...  9.59 us
    dot_general x1, matrix products, attend_backward(): jnp.einsum('bhqk,bqhe->bkhe', grad_low, queries, preferred_element_type=j...  9.44 us
    dot_general x1, matrix products, attend_backward(): jnp.einsum('bhqk,bkhe->bqhe', grad_low, key_part, preferred_element_type=...  9.35 us
    reduce_sum x7, other arithmetic, body(): square_sum = square_sum + jnp.sum(grad_term * grad_term)  8.87 us
  transfers between devices with their start and end apart: 9, of which 8 were waited for; matrix products, arithmetic and copies ran while one was open for 8% of the time, Pallas kernels for 0%

commit v1 on v0

v1 whole, which is shorter than its diff:
```python
import functools
import math

import jax
import jax.numpy as jnp
from jax import lax
from jax.experimental import pallas as pl
from jax.experimental.pallas import tpu as pltpu
from jax.sharding import PartitionSpec as P

HD = 32
WZ = 8
EPS = 1e-05
CUBIC = 0.044715
ROOT_TWO_PI = math.sqrt(2.0 / math.pi)
LOG2_E = 1.0 / math.log(2.0)
LANES = 128
PIECES = 32
BLOCKS = 4
EXTRA = 8
KERNEL_VMEM = 40 << 20
F32 = jnp.float32
BF16 = jnp.bfloat16


def dot(a, b):
    return jnp.dot(a, b, preferred_element_type=F32)


def dot_last(a, b):
    return lax.dot_general(a, b, (((1,), (1,)), ((), ())), preferred_element_type=F32)


def dot_first(a, b):
    return lax.dot_general(a, b, (((0,), (0,)), ((), ())), preferred_element_type=F32)


def row_stats(values):
    row_mean = jnp.mean(values, axis=-1, keepdims=True)
    center = values - row_mean
    variance = jnp.mean(center * center, axis=-1, keepdims=True)
    inv_std = lax.rsqrt(variance + EPS)
    return (center * inv_std, inv_std)


def norm_back(incoming, normed, inv_std, gain_vec):
    terms = incoming * normed
    scaled = incoming * gain_vec
    first_mean = jnp.mean(scaled, axis=-1, keepdims=True)
    second_mean = jnp.mean(terms * gain_vec, axis=-1, keepdims=True)
    back = inv_std * (scaled - first_mean - normed * second_mean)
    return (back, jnp.sum(terms, axis=0, keepdims=True))


def load_rows(part_refs):
    rows = [ref[...].astype(F32).reshape(-1, ref.shape[-1]) for ref in part_refs]
    return jnp.concatenate(rows, axis=0)


def head_columns(qkv, head, width):
    group, sub = divmod(head, LANES // HD)
    lo = group * LANES
    mine = lax.broadcasted_iota(jnp.int32, (1, LANES), 1) // HD == sub
    q, k, v = (qkv[:, i * width + lo : i * width + lo + LANES] for i in range(3))
    return (lo, sub, mine, q, k, v)


def put_block(stage, block, value, me):
    pieces = stage.shape[0] // BLOCKS
    rows = value.shape[0] // pieces
    for i in range(pieces):
        slot = (block * pieces + i) ^ me
        stage[slot, 0:rows] = value[i * rows : (i + 1) * rows]


def hand_out(stage, keep, send):
    half = stage.shape[0] // 2
    keep[...] = stage[:half]
    send[...] = stage[half:]


def forward_kernel(
    me, tok_a, tok_b, tok_c, tok_d, up_a, up_b, up_c, up_d, code_col, code_row,
    gain1, w_qkv, w_proj, gain2, w_fc1, b_fc1, w_fc2,
    keep_a, send_a, keep_b, send_b, small, grad_mid, normed1, inv1, qkv, probs, mix,
    allowed, stage_a, stage_b,
):
    width = w_proj.shape[0]
    heads = width // HD
    me_a, me_b = me[0], me[1]
    x = load_rows((tok_a, tok_b, tok_c, tok_d))
    normed, inv = row_stats(x)
    normed1[...] = normed
    inv1[...] = inv
    h1 = (normed * gain1[...]).astype(BF16)
    qkv[...] = dot(h1, w_qkv[...]).astype(BF16)
    allowed[...] = (code_col[...] == code_row[...]).astype(F32)

    for head in range(heads):
        lo, sub, mine, q, k, v = head_columns(qkv, head, width)
        scores = dot_last(jnp.where(mine, q, jnp.zeros_like(q)), k)
        scores = jnp.where(allowed[...] > 0.0, scores, -1e30)
        highest = jnp.max(scores, axis=-1, keepdims=True)
        weight = jnp.exp2((scores - highest) * (HD ** (-0.5) * LOG2_E))
        total = jnp.sum(weight, axis=-1, keepdims=True)
        prob = (weight * (1.0 / total)).astype(BF16)
        probs[head] = prob
        part = dot(prob, v)
        mix[:, lo : lo + LANES] = part if sub == 0 else jnp.where(mine, part, mix[:, lo : lo + LANES])

    mix_low = mix[...].astype(BF16)
    mid = (x + dot(mix_low, w_proj[...])).astype(BF16).astype(F32)
    normed2, inv2 = row_stats(mid)
    h2 = (normed2 * gain2[...]).astype(BF16)
    up = load_rows((up_a, up_b, up_c, up_d))
    up_low = up.astype(BF16)

    t2 = None
    for j in range(BLOCKS):
        cols = slice(j * width, (j + 1) * width)
        pre = dot(h2, w_fc1[:, cols]) + b_fc1[:, cols]
        square = pre * pre
        tanh_value = jnp.tanh(ROOT_TWO_PI * pre * (1.0 + CUBIC * square))
        half = 0.5 * (1.0 + tanh_value)
        hidden = (pre * half).astype(BF16)
        slope = half + 0.5 * pre * (1.0 - tanh_value * tanh_value) * (
            ROOT_TWO_PI * (1.0 + 3.0 * CUBIC * square)
        )
        put_block(stage_a, j, dot_first(hidden, up_low).astype(BF16), me_a)
        gp = (dot_last(up_low, w_fc2[cols, :]) * slope).astype(BF16)
        small[1 + j : 2 + j, :] = jnp.sum(gp.astype(F32), axis=0, keepdims=True)
        put_block(stage_b, j, dot_first(h2, gp).astype(BF16), me_b)
        part = dot_last(gp, w_fc1[:, cols])
        t2 = part if t2 is None else t2 + part
    back2, s_ln2 = norm_back(t2, normed2, inv2, gain2[...])
    small[0:1, :] = s_ln2
    grad_mid[...] = up + back2
    hand_out(stage_a, keep_a, send_a)
    hand_out(stage_b, keep_b, send_b)


def backward_kernel(
    me, small, grad_mid, normed1, inv1, qkv, probs, mix, gain1, w_qkv, w_proj,
    out_a, out_b, out_c, out_d, keep_t, send_t,
    dmix, dqkv, stage_t,
):
    width = w_proj.shape[0]
    heads = width // HD
    score_scale = HD ** (-0.5)
    me_t = me[0]
    grad_attn = grad_mid[...].astype(BF16)
    dmix[...] = dot_last(grad_attn, w_proj[...]).astype(BF16)
    pieces, rows, _ = stage_t.shape
    stage_t[:, rows - EXTRA :] = jnp.zeros((pieces, EXTRA, width), BF16)
    for i in range(BLOCKS + 1):
        slot = (i + 1) ^ me_t
        stage_t[slot, rows - EXTRA : rows - EXTRA + 1] = small[i : i + 1, :].astype(BF16)
    put_block(stage_t, 3, dot_first(mix[...].astype(BF16), grad_attn).astype(BF16), me_t)

    for head in range(heads):
        lo, sub, mine, q, k, v = head_columns(qkv, head, width)
        do = dmix[:, lo : lo + LANES]
        do_mine = jnp.where(mine, do, jnp.zeros_like(do))
        delta = jnp.sum(do_mine.astype(F32) * mix[:, lo : lo + LANES], axis=-1, keepdims=True)
        prob = probs[head]
        ds = (prob.astype(F32) * (dot_last(do_mine, v) - delta)).astype(BF16)
        parts = (dot(ds, k) * score_scale, dot_first(ds, q) * score_scale, dot_first(prob, do))
        for i, part in enumerate(parts):
            at = i * width + lo
            dqkv[:, at : at + LANES] = (
                part if sub == 0 else jnp.where(mine, part, dqkv[:, at : at + LANES])
            )

    dqkv_low = dqkv[...].astype(BF16)
    normed = normed1[...]
    h1 = (normed * gain1[...]).astype(BF16)
    t1 = None
    for j in range(3):
        cols = slice(j * width, (j + 1) * width)
        put_block(stage_t, j, dot_first(h1, dqkv_low[:, cols]).astype(BF16), me_t)
        part = dot_last(dqkv_low[:, cols], w_qkv[:, cols])
        t1 = part if t1 is None else t1 + part
    back1, s_ln1 = norm_back(t1, normed, inv1[...], gain1[...])
    stage_t[me_t, rows - EXTRA : rows - EXTRA + 1] = s_ln1.astype(BF16)
    hand_out(stage_t, keep_t, send_t)
    result = grad_mid[...] + back1
    quarter = result.shape[0] // 4
    for i, ref in enumerate((out_a, out_b, out_c, out_d)):
        ref[...] = result[i * quarter : (i + 1) * quarter].reshape(ref.shape).astype(BF16)


def finish_kernel(*refs):
    (me, stats), refs = refs[:2], refs[2:]
    parts, (g_qkv, g_proj, g_fc1, g_fc2, g_small, both) = refs[:-6], refs[-6:]
    each = len(parts) // 3
    width = g_proj.shape[0]
    pieces = PIECES // BLOCKS
    total = jnp.sum(stats[...], keepdims=True)
    factor = jnp.sqrt(float(param_count(width, g_fc1.shape[1]))) * lax.rsqrt(total)
    g_small[...] = jnp.zeros_like(g_small)
    for kind in range(3):
        for i, ref in enumerate(parts[kind * each : (kind + 1) * each]):
            for j in range(ref.shape[0]):
                piece = (i * ref.shape[0] + j) ^ me[kind]
                value = ref[j].astype(F32) * factor
                rows = width // pieces
                block, row = piece // pieces, pl.multiple_of(piece % pieces * rows, rows)
                low = value[:rows].astype(BF16)
                if kind == 0:
                    g_fc2[pl.ds(pl.multiple_of(piece * rows, rows), rows), :] = low
                else:
                    into = g_fc1 if kind == 1 else both
                    into[pl.ds(row, rows), pl.ds(pl.multiple_of(block * width, width), width)] = low
                if kind == 2:
                    g_small[piece] = value[rows:]
    g_qkv[...] = both[:, : 3 * width]
    g_proj[...] = both[:, 3 * width :]


def param_count(width, ff):
    return 4 * width * width + 2 * width * ff + 2 * width + ff


VMEM = pl.BlockSpec(memory_space=pltpu.VMEM)
SMEM = pl.BlockSpec(memory_space=pltpu.SMEM)


def shape(dims, dtype):
    return jax.ShapeDtypeStruct(dims, dtype)


def call(kernel, outs, scratch, flops, *args):
    moved = sum(a.size * a.dtype.itemsize for a in args) + sum(
        math.prod(o.shape) * o.dtype.itemsize for o in outs
    )
    return pl.pallas_call(
        kernel,
        out_shape=outs,
        in_specs=[SMEM] + [VMEM] * (len(args) - 1),
        out_specs=(VMEM,) * len(outs),
        scratch_shapes=scratch,
        cost_estimate=pl.CostEstimate(flops=flops, bytes_accessed=moved, transcendentals=0),
        compiler_params=pltpu.CompilerParams(vmem_limit_bytes=KERNEL_VMEM),
    )(*args)


def neighbour(shard, step_x, step_y):
    size_x, size_y = lax.axis_size("gx"), lax.axis_size("gy")
    pairs = [
        (x * size_y + y, (x + step_x) % size_x * size_y + (y + step_y) % size_y)
        for x in range(size_x)
        for y in range(size_y)
    ]
    return lax.ppermute(shard, ("gx", "gy"), pairs)


def quarters(tile):
    half_x, half_y = tile.shape[0] // 2, tile.shape[1] // 2
    return (
        tile[half_x:, half_y:],
        neighbour(tile[half_x:, :half_y], 0, -1),
        neighbour(tile[:half_x, half_y:], -1, 0),
        neighbour(tile[:half_x, :half_y], -1, -1),
    )


def window_codes(labels):
    tile_x, tile_y, tile_z = labels.shape
    half_x, half_y = tile_x // 2, tile_y // 2
    last_x = (lax.axis_index("gx") == lax.axis_size("gx") - 1).astype(jnp.int32)
    last_y = (lax.axis_index("gy") == lax.axis_size("gy") - 1).astype(jnp.int32)
    upper_x = (jnp.arange(tile_x) >= half_x).astype(jnp.int32)
    upper_y = (jnp.arange(tile_y) >= half_y).astype(jnp.int32)
    upper_z = (jnp.arange(tile_z) >= tile_z - WZ // 2).astype(jnp.int32)
    codes = (
        labels * 8
        + (4 * last_x) * upper_x[:, None, None]
        + (2 * last_y) * upper_y[None, :, None]
        + upper_z[None, None, :]
    )
    codes = jnp.roll(codes, WZ // 2, axis=2)
    parts = (
        codes[:half_x, :half_y], codes[:half_x, half_y:],
        codes[half_x:, :half_y], codes[half_x:, half_y:],
    )
    return jnp.concatenate([part.reshape(-1) for part in parts])


def swap(shard, flip_x, flip_y):
    size_x, size_y = lax.axis_size("gx"), lax.axis_size("gy")
    pairs = [
        (x * size_y + y, (x ^ flip_x) * size_y + (y ^ flip_y))
        for x in range(size_x)
        for y in range(size_y)
    ]
    return lax.ppermute(shard, ("gx", "gy"), pairs)


def add(first, *others):
    total = first.astype(F32)
    for other in others:
        total = total + other.astype(F32)
    return total


CORE, SIDE = (0, 1), (0, 2)
NEAR, FAR = (1, 0), ((2, 0), (4, 0), (6, 0))
ORDERS = ((CORE, SIDE, NEAR), (CORE, NEAR, SIDE), (CORE, SIDE, NEAR))


def place(order):
    index_x, index_y = lax.axis_index("gx"), lax.axis_index("gy")
    number = jnp.int32(0)
    for flip_x, flip_y in order:
        bit = (index_x & flip_x) if flip_x else (index_y & flip_y)
        number = 2 * number + (bit != 0).astype(jnp.int32)
    return 4 * number + ((index_x // 2) & 3)


def scatter_sum(keep, send, order):
    for step, flips in enumerate(order):
        got = swap(send, *flips)
        if step == len(order) - 1:
            break
        half = keep.shape[0] // 2
        keep, send = (
            add(keep[:half], got[:half]).astype(BF16),
            add(keep[half:], got[half:]).astype(BF16),
        )
    last = [add(keep[i], got[i]) for i in range(keep.shape[0])]
    own = add(last[0], *(swap(last[i + 1].astype(BF16), *flips) for i, flips in enumerate(FAR)))
    for axis, spare in (("gx", 8), ("gy", 4)):
        while spare < lax.axis_size(axis):
            flips = (spare, 0) if axis == "gx" else (0, spare)
            own = add(own.astype(BF16), swap(own.astype(BF16), *flips))
            spare *= 2
    return own


def gather(own, order):
    parts = [jnp.stack([own] + [swap(own, *flips) for flips in FAR])]
    for flips in reversed(order):
        parts = parts + [swap(part, *flips) for part in parts]
    return parts


def body(tokens, upstream, window_labels, ln1_gain, w_qkv, w_proj, ln2_gain, w_fc1, b_fc1, w_fc2):
    width, ff = w_fc1.shape
    heads = width // HD
    tok_parts = quarters(tokens)
    up_parts = quarters(upstream)
    codes = window_codes(window_labels)
    rows = codes.shape[0]
    me = jnp.stack([place(order) for order in ORDERS])
    piece = BLOCKS * width // PIECES
    half = shape((PIECES // 2, piece, width), BF16)
    half_t = shape((PIECES // 2, piece + EXTRA, width), BF16)
    gain1 = ln1_gain[None, :]
    outs = call(
        forward_kernel,
        (half, half, half, half)
        + (shape((1 + BLOCKS, width), F32), shape((rows, width), F32), shape((rows, width), F32), shape((rows, 1), F32))
        + (shape((rows, 3 * width), BF16), shape((heads, rows, rows), BF16), shape((rows, width), F32)),
        [
            pltpu.VMEM((rows, rows), F32),
            pltpu.VMEM((PIECES, piece, width), BF16),
            pltpu.VMEM((PIECES, piece, width), BF16),
        ],
        2 * rows * width * (4 * width + 5 * ff) + 4 * heads * rows * rows * LANES,
        me, *tok_parts, *up_parts, codes[:, None], codes[None, :],
        gain1, w_qkv, w_proj, ln2_gain[None, :], w_fc1, b_fc1[None, :], w_fc2,
    )
    keep_a, send_a, keep_b, send_b = outs[:4]
    sum_a = scatter_sum(keep_a, send_a, ORDERS[0])
    sum_b = scatter_sum(keep_b, send_b, ORDERS[1])
    done = call(
        backward_kernel,
        (shape(tok_parts[0].shape, BF16),) * 4 + (half_t, half_t),
        [
            pltpu.VMEM((rows, width), BF16),
            pltpu.VMEM((rows, 3 * width), F32),
            pltpu.VMEM((PIECES, piece + EXTRA, width), BF16),
        ],
        2 * rows * width * 8 * width + 8 * heads * rows * rows * LANES,
        me[2:], *outs[4:], gain1, w_qkv, w_proj,
    )
    sum_t = scatter_sum(done[4], done[5], ORDERS[2])
    square = jnp.sum(sum_a * sum_a) + jnp.sum(sum_b * sum_b) + jnp.sum(sum_t * sum_t)
    high = square.astype(BF16)
    lower = square - high.astype(F32)
    middle = lower.astype(BF16)
    at = lax.broadcasted_iota(jnp.int32, sum_t.shape, 0) - piece
    own_t = jnp.where(at == 1, high, jnp.where(at == 2, middle, sum_t.astype(BF16)))
    parts_a = gather(sum_a.astype(BF16), ORDERS[0])
    parts_b = gather(sum_b.astype(BF16), ORDERS[1])
    parts_t = gather(own_t, ORDERS[2])
    stats = jnp.concatenate([part[:, piece + 1 : piece + 3, 0] for part in parts_t]).astype(F32)
    g_qkv, g_proj, g_fc1, g_fc2, g_small = call(
        finish_kernel,
        (
            shape((width, 3 * width), BF16), shape((width, width), BF16),
            shape((width, ff), BF16), shape((ff, width), BF16), shape((PIECES, EXTRA, width), F32),
        ),
        [pltpu.VMEM((width, 4 * width), BF16)],
        4 * width * width,
        me, stats, *parts_a, *parts_b, *parts_t,
    )
    back = (done[0], neighbour(done[1], 0, 1), neighbour(done[2], 1, 0), neighbour(done[3], 1, 1))
    result = jnp.concatenate(
        (
            jnp.concatenate((back[3], back[2]), axis=1),
            jnp.concatenate((back[1], back[0]), axis=1),
        ),
        axis=0,
    )
    return (
        result, g_small[0, 0], g_qkv, g_proj, g_small[1, 0], g_fc1,
        g_small[2 : 2 + BLOCKS, 0].reshape(ff), g_fc2,
    )


def solution(mesh):
    return jax.shard_map(
        body,
        mesh=mesh,
        in_specs=(
            P("gx", "gy", None, None),
            P("gx", "gy", None, None),
            P("gx", "gy", None),
            P(), P(), P(), P(), P(), P(), P(),
        ),
        out_specs=(P("gx", "gy", None, None), P(), P(), P(), P(), P(), P(), P()),
        check_vma=False,
    )
```

time: 289 us -> 138 us (0.48)
  waiting for transfers between devices: 130 us -> 40.2 us
  matrix products: 49 us -> 0 us
  starting transfers between devices: 11 us -> 54.3 us
  blocking collectives: 38.2 us -> 0 us
  Pallas kernels: 0 us -> 21.9 us
  other arithmetic: 27 us -> 5.49 us
  between operations: 19.3 us -> 2.97 us
    psum x1 -> x0, waiting for transfers between devices: 98.9 us -> none  [body(): lax.psum((local_grads[0], local_grads[1], local_grads[2], local_grads[3],...]
    dot_general x16 -> x0, matrix products: 44.8 us -> none  [the longest x1 9.44 us: attend_backward(): jnp.einsum('bhqk,bqhe->bkhe', grad_low, queries, preferred_element_type=j...]
    ppermute x8 -> x57, starting transfers between devices: 10.9 us -> 54.3 us  [the longest x48 43.6 us: swap(): return lax.ppermute(shard, ('gx', 'gy'), pairs)]
    psum x1 -> x0, blocking collectives: 38.2 us -> none  [body(): lax.psum((local_grads[0], local_grads[1], local_grads[2], local_grads[3],...]
    pallas_call x0 -> x3, Pallas kernels: none -> 21.9 us  [call(): pl.pallas_call(kernel, out_shape=outs, in_specs=[SMEM] + [VMEM] * (len(ar...]
    reduce_sum x13 -> x1, other arithmetic: 12.7 us -> 0.63 us  [body(): jnp.sum(sum_t * sum_t)]
    convert_element_type x5 -> x1, local copies, waits for them, and re-layouts: 12 us -> 0.1 us  [body(): jnp.concatenate([part[:, piece + 1:piece + 3, 0] for part in parts_t])]
    ppermute x8 -> x57, waiting for transfers between devices: 30.6 us -> 40.2 us  [the longest x48 33.8 us: swap(): return lax.ppermute(shard, ('gx', 'gy'), pairs)]
  transfers between devices with their start and end apart: 9 -> 57, of which waited for: 8 -> 14; matrix products, arithmetic and copies ran while one was open for 8% -> 6% of each run, Pallas kernels for 0% -> 5%
where the time goes in v1:
time: 138 us; the launch traced here: 137 us
  starting transfers between devices  54.3 us (39%)
  waiting for transfers between devices  40.2 us (29%)
  Pallas kernels  21.9 us (16%)
  local copies, waits for them, and re-layouts  12.6 us (9%)
  other arithmetic  5.49 us (4%)
  between operations  2.97 us (2%)
    ppermute x48, starting transfers between devices, swap(): return lax.ppermute(shard, ('gx', 'gy'), pairs)  43.6 us
    ppermute x48, waiting for transfers between devices, swap(): return lax.ppermute(shard, ('gx', 'gy'), pairs)  33.8 us
    pallas_call x3, Pallas kernels, call(): pl.pallas_call(kernel, out_shape=outs, in_specs=[SMEM] + [VMEM] * (len(ar...  21.9 us
    ppermute x9, starting transfers between devices, neighbour(): return lax.ppermute(shard, ('gx', 'gy'), pairs)  10.7 us
    unnamed x30, local copies, waits for them, and re-layouts  7.72 us
    ppermute x9, waiting for transfers between devices, neighbour(): return lax.ppermute(shard, ('gx', 'gy'), pairs)  6.34 us
  transfers between devices with their start and end apart: 57, of which 14 were waited for; matrix products, arithmetic and copies ran while one was open for 6% of the time, Pallas kernels for 5%

profile of v1, /device:TPU:0, one launch (start us, length us, event | category | flops | bytes accessed | tf_op | source)
XLA Modules:
  0.0 137.5 jit_solution(10197937876742134786)
XLA Ops:
  0.7 1.0 fusion.23
  1.7 2.4 %collective-permute-start = (bf16[3,3,8,384]{3,2,1,0:T(8,128)(2,1)S(1)}, bf16[3,3,8,384]{3,2,1,0:T(8,128)(2,1)S(1)}, u32[]{:S(2)}, u32[]{:S(2)}) collective-permute-start(bf16[3,3,8,384]{3,2,1,0:T(8,128)(2,1)S(1)} %get-tuple-element.84), channel_id=1, source_target_pairs={{0,3},{1,0},{2,1},{3,2},{4,7},{5,4},{6,5},{7,6},{8,11},{9,8},{10,9... | collective-permute-start | bytes 165896 | tf_op jit(solution)/shard_map/ppermute | solution.py:254
  4.1 4.6 %collective-permute-start.1 = (bf16[3,3,8,384]{3,2,1,0:T(8,128)(2,1)S(1)}, bf16[3,3,8,384]{3,2,1,0:T(8,128)(2,1)S(1)}, u32[]{:S(2)}, u32[]{:S(2)}) collective-permute-start(bf16[3,3,8,384]{3,2,1,0:T(8,128)(2,1)S(1)} %get-tuple-element.86), channel_id=1, source_target_pairs={{0,28},{1,29},{2,30},{3,31},{4,0},{5,1},{6,2},{7,3},{8,4},{9,5},{1... | collective-permute-start | bytes 165896 | tf_op jit(solution)/shard_map/ppermute | solution.py:254
  9.0 0.9 fusion.22
  10.5 1.4 %collective-permute-start.4 = (bf16[3,3,8,384]{3,2,1,0:T(8,128)(2,1)S(1)}, bf16[3,3,8,384]{3,2,1,0:T(8,128)(2,1)S(1)}, u32[]{:S(2)}, u32[]{:S(2)}) collective-permute-start(bf16[3,3,8,384]{3,2,1,0:T(8,128)(2,1)S(1)} %get-tuple-element.82), channel_id=1, source_target_pairs={{0,28},{1,29},{2,30},{3,31},{4,0},{5,1},{6,2},{7,3},{8,4},{9,5},{1... | collective-permute-start | bytes 165896 | tf_op jit(solution)/shard_map/ppermute | solution.py:254
  15.5 1.4 %collective-permute-done.5.up_d = bf16[3,3,8,384]{3,2,1,0:T(8,128)(2,1)S(1)} collective-permute-done((bf16[3,3,8,384]{3,2,1,0:T(8,128)(2,1)S(1)}, bf16[3,3,8,384]{3,2,1,0:T(8,128)(2,1)S(1)}, u32[]{:S(2)}, u32[]{:S(2)}) %collective-permute-start.5) | collective-permute-done | bytes 55328 | tf_op jit(solution)/shard_map/ppermute | solution.py:254
  17.0 1.3 copy-done.1
  18.2 1.2 copy-done.2
  19.4 1.0 copy-done.4
  22.8 11.8 %shard_map.161 = (bf16[16,48,384]{2,1,0:T(8,128)(2,1)S(1)}, bf16[16,48,384]{2,1,0:T(8,128)(2,1)S(1)}, bf16[16,48,384]{2,1,0:T(8,128)(2,1)S(1)}, bf16[16,48,384]{...) custom-call(s32[3]{0:T(128)S(1)} %pad_add_fusion.2.me.refs_0_, ...), custom_call_target="tpu_custom_call" | custom-call | flops 2548039680 | bytes 10342284 | tf_op jit(solution)/shard_map/pallas_call | solution.py:236
  35.4 6.4 %shard_map.162 = (bf16[3,3,8,384]{3,2,1,0:T(8,128)(2,1)S(1)}, bf16[3,3,8,384]{3,2,1,0:T(8,128)(2,1)S(1)}, bf16[3,3,8,384]{3,2,1,0:T(8,128)(2,1)S(1)}, bf16[3,3,8...) custom-call(s32[1]{0:T(128)} %bitcast.me, ...), custom_call_target="tpu_custom_call" | custom-call | flops 1698693120 | bytes 6768772 | tf_op jit(solution)/shard_map/pallas_call | solution.py:236
  42.5 1.8 %collective-permute-start.10 = (bf16[8,48,384]{2,1,0:T(8,128)(2,1)S(1)}, bf16[8,48,384]{2,1,0:T(8,128)(2,1)S(1)}, u32[]{:S(2)}, u32[]{:S(2)}) collective-permute-start(bf16[8,48,384]{2,1,0:T(8,128)(2,1)S(1)} %get-tuple-element.59), channel_id=1, source_target_pairs={{0,2},{1,3},{2,0},{3,1},{4,6},{5,7},{6,4},{7,5},{8,10},{9,11},{10,... | collective-permute-start | bytes 884744 | tf_op jit(solution)/shard_map/ppermute | solution.py:296
  44.5 1.6 %collective-permute-start.16 = (bf16[8,48,384]{2,1,0:T(8,128)(2,1)S(1)}, bf16[8,48,384]{2,1,0:T(8,128)(2,1)S(1)}, u32[]{:S(2)}, u32[]{:S(2)}) collective-permute-start(bf16[8,48,384]{2,1,0:T(8,128)(2,1)S(1)} %get-tuple-element.57), channel_id=1, source_target_pairs={{0,4},{1,5},{2,6},{3,7},{4,0},{5,1},{6,2},{7,3},{8,12},{9,13},{10,... | collective-permute-start | bytes 884744 | tf_op jit(solution)/shard_map/ppermute | solution.py:296
  46.2 1.0 collective-permute-start.22
  47.2 4.9 %collective-permute-done.10 = bf16[8,48,384]{2,1,0:T(8,128)(2,1)S(1)} collective-permute-done((bf16[8,48,384]{2,1,0:T(8,128)(2,1)S(1)}, bf16[8,48,384]{2,1,0:T(8,128)(2,1)S(1)}, u32[]{:S(2)}, u32[]{:S(2)}) %collective-permute-start.10) | collective-permute-done | bytes 294944 | tf_op jit(solution)/shard_map/ppermute | solution.py:296
  52.1 2.5 %collective-permute-start.11 = (bf16[4,48,384]{2,1,0:T(8,128)(2,1)S(1)}, bf16[4,48,384]{2,1,0:T(8,128)(2,1)S(1)}, u32[]{:S(2)}, u32[]{:S(2)}) collective-permute-start(bf16[4,48,384]{2,1,0:T(8,128)(2,1)S(1)} %get-tuple-element.65), channel_id=1, source_target_pairs={{0,4},{1,5},{2,6},{3,7},{4,0},{5,1},{6,2},{7,3},{8,12},{9,13},{10,... | collective-permute-start | bytes 442376 | tf_op jit(solution)/shard_map/ppermute | solution.py:296
  54.8 1.2 collective-permute-start.17
  56.0 2.9 %collective-permute-done.11 = bf16[4,48,384]{2,1,0:T(8,128)(2,1)S(1)} collective-permute-done((bf16[4,48,384]{2,1,0:T(8,128)(2,1)S(1)}, bf16[4,48,384]{2,1,0:T(8,128)(2,1)S(1)}, u32[]{:S(2)}, u32[]{:S(2)}) %collective-permute-start.11) | collective-permute-done | bytes 147488 | tf_op jit(solution)/shard_map/ppermute | solution.py:296
  58.9 2.0 %collective-permute-start.14 = (bf16[48,384]{1,0:T(8,128)(2,1)S(1)}, bf16[48,384]{1,0:T(8,128)(2,1)S(1)}, u32[]{:S(2)}, u32[]{:S(2)}) collective-permute-start(bf16[48,384]{1,0:T(8,128)(2,1)S(1)} %get-tuple-element.77), channel_id=1, source_target_pairs={{0,24},{1,25},{2,26},{3,27},{4,28},{5,29},{6,30},{7,31},{8,16},{9,... | collective-permute-start | bytes 110600 | tf_op jit(solution)/shard_map/ppermute | solution.py:296
  60.8 1.1 collective-permute-start.13
  62.6 1.6 %collective-permute-start.12 = (bf16[48,384]{1,0:T(8,128)(2,1)S(1)}, bf16[48,384]{1,0:T(8,128)(2,1)S(1)}, u32[]{:S(2)}, u32[]{:S(2)}) collective-permute-start(bf16[48,384]{1,0:T(8,128)(2,1)S(1)} %get-tuple-element.76), channel_id=1, source_target_pairs={{0,8},{1,9},{2,10},{3,11},{4,12},{5,13},{6,14},{7,15},{8,0},{9,1},... | collective-permute-start | bytes 110600 | tf_op jit(solution)/shard_map/ppermute | solution.py:296
  64.2 1.1 collective-permute-start.20
  66.4 2.5 %collective-permute-start.18 = (bf16[48,384]{1,0:T(8,128)(2,1)S(1)}, bf16[48,384]{1,0:T(8,128)(2,1)S(1)}, u32[]{:S(2)}, u32[]{:S(2)}) collective-permute-start(bf16[48,384]{1,0:T(8,128)(2,1)S(1)} %get-tuple-element.73), channel_id=1, source_target_pairs={{0,8},{1,9},{2,10},{3,11},{4,12},{5,13},{6,14},{7,15},{8,0},{9,1},... | collective-permute-start | bytes 110600 | tf_op jit(solution)/shard_map/ppermute | solution.py:296
  70.2 4.3 %collective-permute-done.23 = bf16[4,56,384]{2,1,0:T(8,128)(2,1)S(1)} collective-permute-done((bf16[4,56,384]{2,1,0:T(8,128)(2,1)S(1)}, bf16[4,56,384]{2,1,0:T(8,128)(2,1)S(1)}, u32[]{:S(2)}, u32[]{:S(2)}) %collective-permute-start.23) | collective-permute-done | bytes 172064 | tf_op jit(solution)/shard_map/ppermute | solution.py:296
  74.5 1.0 collective-permute-start.39
  75.5 2.9 %collective-permute-start.26 = (bf16[56,384]{1,0:T(8,128)(2,1)S(1)}, bf16[56,384]{1,0:T(8,128)(2,1)S(1)}, u32[]{:S(2)}, u32[]{:S(2)}) collective-permute-start(bf16[56,384]{1,0:T(8,128)(2,1)S(1)} %get-tuple-element.71), channel_id=1, source_target_pairs={{0,24},{1,25},{2,26},{3,27},{4,28},{5,29},{6,30},{7,31},{8,16},{9,... | collective-permute-start | bytes 129032 | tf_op jit(solution)/shard_map/ppermute | solution.py:296
  78.4 1.6 %collective-permute-start.24 = (bf16[56,384]{1,0:T(8,128)(2,1)S(1)}, bf16[56,384]{1,0:T(8,128)(2,1)S(1)}, u32[]{:S(2)}, u32[]{:S(2)}) collective-permute-start(bf16[56,384]{1,0:T(8,128)(2,1)S(1)} %get-tuple-element.70), channel_id=1, source_target_pairs={{0,8},{1,9},{2,10},{3,11},{4,12},{5,13},{6,14},{7,15},{8,0},{9,1},... | collective-permute-start | bytes 129032 | tf_op jit(solution)/shard_map/ppermute | solution.py:296
  81.9 1.4 %collective-permute-start.38 = (bf16[48,384]{1,0:T(8,128)(2,1)S(1)}, bf16[48,384]{1,0:T(8,128)(2,1)S(1)}, u32[]{:S(2)}, u32[]{:S(2)}) collective-permute-start(bf16[48,384]{1,0:T(8,128)(2,1)S(1)} %get-tuple-element.68), channel_id=1, source_target_pairs={{0,16},{1,17},{2,18},{3,19},{4,20},{5,21},{6,22},{7,23},{8,24},{9,... | collective-permute-start | bytes 110600 | tf_op jit(solution)/shard_map/ppermute | solution.py:296
  84.1 1.3 collective-permute-start.37
  85.4 1.0 collective-permute-start.49
  87.8 2.9 %collective-permute-start.29 = (bf16[56,384]{1,0:T(8,128)(2,1)S(1)}, bf16[56,384]{1,0:T(8,128)(2,1)S(1)}, u32[]{:S(2)}, u32[]{:S(2)}) collective-permute-start(bf16[56,384]{1,0:T(8,128)(2,1)S(1)} %select_select_fusion), channel_id=1, source_target_pairs={{0,24},{1,25},{2,26},{3,27},{4,28},{5,29},{6,30},{7,31},{8,16},{9,... | collective-permute-start | bytes 129032 | tf_op jit(solution)/shard_map/ppermute | solution.py:296
  90.7 1.6 %collective-permute-start.27 = (bf16[56,384]{1,0:T(8,128)(2,1)S(1)}, bf16[56,384]{1,0:T(8,128)(2,1)S(1)}, u32[]{:S(2)}, u32[]{:S(2)}) collective-permute-start(bf16[56,384]{1,0:T(8,128)(2,1)S(1)} %select_select_fusion), channel_id=1, source_target_pairs={{0,8},{1,9},{2,10},{3,11},{4,12},{5,13},{6,14},{7,15},{8,0},{9,1},... | collective-permute-start | bytes 129032 | tf_op jit(solution)/shard_map/ppermute | solution.py:296
  92.3 1.8 %collective-permute-done.29 = bf16[56,384]{1,0:T(8,128)(2,1)S(1)} collective-permute-done((bf16[56,384]{1,0:T(8,128)(2,1)S(1)}, bf16[56,384]{1,0:T(8,128)(2,1)S(1)}, u32[]{:S(2)}, u32[]{:S(2)}) %collective-permute-start.29) | collective-permute-done | bytes 43040 | tf_op jit(solution)/shard_map/ppermute | solution.py:296
  94.1 1.6 %collective-permute-done.28 = bf16[56,384]{1,0:T(8,128)(2,1)S(1)} collective-permute-done((bf16[56,384]{1,0:T(8,128)(2,1)S(1)}, bf16[56,384]{1,0:T(8,128)(2,1)S(1)}, u32[]{:S(2)}, u32[]{:S(2)}) %collective-permute-start.28) | collective-permute-done | bytes 43040 | tf_op jit(solution)/shard_map/ppermute | solution.py:296
  95.6 1.6 %collective-permute-start.47 = (bf16[48,384]{1,0:T(8,128)(2,1)S(1)}, bf16[48,384]{1,0:T(8,128)(2,1)S(1)}, u32[]{:S(2)}, u32[]{:S(2)}) collective-permute-start(bf16[48,384]{1,0:T(8,128)(2,1)S(1)} %get-tuple-element.66), channel_id=1, source_target_pairs={{0,8},{1,9},{2,10},{3,11},{4,12},{5,13},{6,14},{7,15},{8,0},{9,1},... | collective-permute-start | bytes 110600 | tf_op jit(solution)/shard_map/ppermute | solution.py:296
  98.0 1.3 collective-permute-start.7
  99.3 1.2 collective-permute-start.41
  100.5 1.4 %collective-permute-start.30 = (bf16[4,56,384]{2,1,0:T(8,128)(2,1)S(1)}, bf16[4,56,384]{2,1,0:T(8,128)(2,1)S(1)}, u32[]{:S(2)}, u32[]{:S(2)}) collective-permute-start(bf16[4,56,384]{2,1,0:T(8,128)(2,1)S(1)} %pad_maximum_fusion.refs_18_), channel_id=1, source_target_pairs={{0,4},{1,5},{2,6},{3,7},{4,0},{5,1},{6,2},{7,3},{8,12},{9,13},{10,... | collective-permute-start | bytes 516104 | tf_op jit(solution)/shard_map/ppermute | solution.py:296
  102.0 3.0 %collective-permute-done.7 = bf16[3,3,8,384]{3,2,1,0:T(8,128)(2,1)S(1)} collective-permute-done((bf16[3,3,8,384]{3,2,1,0:T(8,128)(2,1)S(1)}, bf16[3,3,8,384]{3,2,1,0:T(8,128)(2,1)S(1)}, u32[]{:S(2)}, u32[]{:S(2)}) %collective-permute-start.7) | collective-permute-done | bytes 55328 | tf_op jit(solution)/shard_map/ppermute | solution.py:254
  105.0 1.9 %collective-permute-done.6 = bf16[3,3,8,384]{3,2,1,0:T(8,128)(2,1)S(1)} collective-permute-done((bf16[3,3,8,384]{3,2,1,0:T(8,128)(2,1)S(1)}, bf16[3,3,8,384]{3,2,1,0:T(8,128)(2,1)S(1)}, u32[]{:S(2)}, u32[]{:S(2)}) %collective-permute-start.6) | collective-permute-done | bytes 55328 | tf_op jit(solution)/shard_map/ppermute | solution.py:254
  106.9 0.9 collective-permute-start.50
  107.8 1.2 collective-permute-start.31
  110.1 3.6 %collective-permute-done.50.refs_11_ = bf16[4,48,384]{2,1,0:T(8,128)(2,1)S(1)} collective-permute-done((bf16[4,48,384]{2,1,0:T(8,128)(2,1)S(1)}, bf16[4,48,384]{2,1,0:T(8,128)(2,1)S(1)}, u32[]{:S(2)}, u32[]{:S(2)}) %collective-permute-start.50) | collective-permute-done | bytes 147488 | tf_op jit(solution)/shard_map/ppermute | solution.py:296
  113.7 0.9 collective-permute-start.42
  115.1 6.7 %collective-permute-done.42.refs_5_ = bf16[4,48,384]{2,1,0:T(8,128)(2,1)S(1)} collective-permute-done((bf16[4,48,384]{2,1,0:T(8,128)(2,1)S(1)}, bf16[4,48,384]{2,1,0:T(8,128)(2,1)S(1)}, u32[]{:S(2)}, u32[]{:S(2)}) %collective-permute-start.42) | collective-permute-done | bytes 147488 | tf_op jit(solution)/shard_map/ppermute | solution.py:296
  122.4 6.2 %collective-permute-done.52.refs_13_ = bf16[4,48,384]{2,1,0:T(8,128)(2,1)S(1)} collective-permute-done((bf16[4,48,384]{2,1,0:T(8,128)(2,1)S(1)}, bf16[4,48,384]{2,1,0:T(8,128)(2,1)S(1)}, u32[]{:S(2)}, u32[]{:S(2)}) %collective-permute-start.52) | collective-permute-done | bytes 147488 | tf_op jit(solution)/shard_map/ppermute | solution.py:296
  129.7 1.5 %maximum_maximum_fusion = bf16[6,6,8,384]{3,2,1,0:T(8,128)(2,1)} fusion(bf16[3,3,8,384]{3,2,1,0:T(8,128)(2,1)S(1)} %get-tuple-element.40, bf16[3,3,8,384]{3,2,1,0:T(8,128)(2,1)} %collective-permute-done.8, bf16[3,3,8,384]{3,2,1,0:T(8,128)(2,1)S(1)} %collective-permute-done.7, bf16[3,3,8,384]{3,2,1,0:T(8,128)(2,1)S(1)} %collective-permute-done.6), kind=kLoop, calls=%fused_computation.12 | loop fusion | flops 331776 | bytes 442368 | tf_op jit(solution)/shard_map/concatenate | solution.py:409
  132.5 3.8 %shard_map.163 = (bf16[384,1152]{1,0:T(8,128)(2,1)}, bf16[384,384]{1,0:T(8,128)(2,1)}, bf16[384,1536]{1,0:T(8,128)(2,1)}, bf16[1536,384]{1,0:T(8,128)(2,1)}, f32[32,8,384]{2,1,0:T(8,128)S(1)}) custom-call(s32[3]{0:T(128)S(1)} %pad_add_fusion.2.me.refs_0_, f32[32,2]{1,0:T(8,128)S(1)} %copy.70.refs_1_, bf16[4,48,384]{2,1,0:T(8,128)(2,1)S(1)} %pad_maximum_fusion.1.refs_2_, ...), custom_call_target="tpu_custom_call" | custom-call | flops 589824 | bytes 7667980 | tf_op jit(solution)/shard_map/pallas_call | solution.py:236
  (156 shorter events, 20.7 us)
Async XLA Ops:
  1.7 11.6 %collective-permute-start = (bf16[3,3,8,384]{3,2,1,0:T(8,128)(2,1)S(1)}, bf16[3,3,8,384]{3,2,1,0:T(8,128)(2,1)S(1)}, u32[]{:S(2)}, u32[]{:S(2)}) collective-permute-start(bf16[3,3,8,384]{3,2,1,0:T(8,128)(2,1)S(1)} %get-tuple-element.84), channel_id=1, source_target_pairs={{0,3},{1,0},{2,1},{3,2},{4,7},{5,4},{6,5},{7,6},{8,11},{9,8},{10,9... | collective-permute-start | bytes 165896 | tf_op jit(solution)/shard_map/ppermute | solution.py:254
  4.1 9.5 %collective-permute-start.1 = (bf16[3,3,8,384]{3,2,1,0:T(8,128)(2,1)S(1)}, bf16[3,3,8,384]{3,2,1,0:T(8,128)(2,1)S(1)}, u32[]{:S(2)}, u32[]{:S(2)}) collective-permute-start(bf16[3,3,8,384]{3,2,1,0:T(8,128)(2,1)S(1)} %get-tuple-element.86), channel_id=1, source_target_pairs={{0,28},{1,29},{2,30},{3,31},{4,0},{5,1},{6,2},{7,3},{8,4},{9,5},{1... | collective-permute-start | bytes 165896 | tf_op jit(solution)/shard_map/ppermute | solution.py:254
  8.7 5.0 %collective-permute-start.2 = (bf16[3,3,8,384]{3,2,1,0:T(8,128)(2,1)S(1)}, bf16[3,3,8,384]{3,2,1,0:T(8,128)(2,1)S(1)}, u32[]{:S(2)}, u32[]{:S(2)}) collective-permute-start(bf16[3,3,8,384]{3,2,1,0:T(8,128)(2,1)S(1)} %get-tuple-element.83), channel_id=1, source_target_pairs={{0,31},{1,28},{2,29},{3,30},{4,3},{5,0},{6,1},{7,2},{8,7},{9,4},{1... | collective-permute-start | bytes 165896 | tf_op jit(solution)/shard_map/ppermute | solution.py:254
  34.6 7.7 %collective-permute-start.9 = (bf16[16,48,384]{2,1,0:T(8,128)(2,1)S(1)}, bf16[16,48,384]{2,1,0:T(8,128)(2,1)S(1)}, u32[]{:S(2)}, u32[]{:S(2)}) collective-permute-start(bf16[16,48,384]{2,1,0:T(8,128)(2,1)S(1)} %get-tuple-element.42), channel_id=1, source_target_pairs={{0,1},{1,0},{2,3},{3,2},{4,5},{5,4},{6,7},{7,6},{8,9},{9,8},{10,11... | collective-permute-start | bytes 1769480 | tf_op jit(solution)/shard_map/ppermute | solution.py:296
  35.3 9.0 %collective-permute-start.15 = (bf16[16,48,384]{2,1,0:T(8,128)(2,1)S(1)}, bf16[16,48,384]{2,1,0:T(8,128)(2,1)S(1)}, u32[]{:S(2)}, u32[]{:S(2)}) collective-permute-start(bf16[16,48,384]{2,1,0:T(8,128)(2,1)S(1)} %get-tuple-element.44), channel_id=1, source_target_pairs={{0,1},{1,0},{2,3},{3,2},{4,5},{5,4},{6,7},{7,6},{8,9},{9,8},{10,11... | collective-permute-start | bytes 1769480 | tf_op jit(solution)/shard_map/ppermute | solution.py:296
  42.2 55.8 %collective-permute-start.8 = (bf16[3,3,8,384]{3,2,1,0:T(8,128)(2,1)S(1)}, bf16[3,3,8,384]{3,2,1,0:T(8,128)(2,1)}, u32[]{:S(2)}, u32[]{:S(2)}) collective-permute-start(bf16[3,3,8,384]{3,2,1,0:T(8,128)(2,1)S(1)} %get-tuple-element.39), channel_id=1, source_target_pairs={{0,1},{1,2},{2,3},{3,0},{4,5},{5,6},{6,7},{7,4},{8,9},{9,10},{10,1... | collective-permute-start | bytes 165896 | tf_op jit(solution)/shard_map/ppermute | solution.py:254
  42.5 9.6 %collective-permute-start.10 = (bf16[8,48,384]{2,1,0:T(8,128)(2,1)S(1)}, bf16[8,48,384]{2,1,0:T(8,128)(2,1)S(1)}, u32[]{:S(2)}, u32[]{:S(2)}) collective-permute-start(bf16[8,48,384]{2,1,0:T(8,128)(2,1)S(1)} %get-tuple-element.59), channel_id=1, source_target_pairs={{0,2},{1,3},{2,0},{3,1},{4,6},{5,7},{6,4},{7,5},{8,10},{9,11},{10,... | collective-permute-start | bytes 884744 | tf_op jit(solution)/shard_map/ppermute | solution.py:296
  44.5 10.2 %collective-permute-start.16 = (bf16[8,48,384]{2,1,0:T(8,128)(2,1)S(1)}, bf16[8,48,384]{2,1,0:T(8,128)(2,1)S(1)}, u32[]{:S(2)}, u32[]{:S(2)}) collective-permute-start(bf16[8,48,384]{2,1,0:T(8,128)(2,1)S(1)} %get-tuple-element.57), channel_id=1, source_target_pairs={{0,4},{1,5},{2,6},{3,7},{4,0},{5,1},{6,2},{7,3},{8,12},{9,13},{10,... | collective-permute-start | bytes 884744 | tf_op jit(solution)/shard_map/ppermute | solution.py:296
  46.2 18.0 %collective-permute-start.22 = (bf16[8,56,384]{2,1,0:T(8,128)(2,1)S(1)}, bf16[8,56,384]{2,1,0:T(8,128)(2,1)S(1)}, u32[]{:S(2)}, u32[]{:S(2)}) collective-permute-start(bf16[8,56,384]{2,1,0:T(8,128)(2,1)S(1)} %get-tuple-element.55), channel_id=1, source_target_pairs={{0,2},{1,3},{2,0},{3,1},{4,6},{5,7},{6,4},{7,5},{8,10},{9,11},{10,... | collective-permute-start | bytes 1032200 | tf_op jit(solution)/shard_map/ppermute | solution.py:296
  52.1 6.7 %collective-permute-start.11 = (bf16[4,48,384]{2,1,0:T(8,128)(2,1)S(1)}, bf16[4,48,384]{2,1,0:T(8,128)(2,1)S(1)}, u32[]{:S(2)}, u32[]{:S(2)}) collective-permute-start(bf16[4,48,384]{2,1,0:T(8,128)(2,1)S(1)} %get-tuple-element.65), channel_id=1, source_target_pairs={{0,4},{1,5},{2,6},{3,7},{4,0},{5,1},{6,2},{7,3},{8,12},{9,13},{10,... | collective-permute-start | bytes 442376 | tf_op jit(solution)/shard_map/ppermute | solution.py:296
  54.8 7.8 %collective-permute-start.17 = (bf16[4,48,384]{2,1,0:T(8,128)(2,1)S(1)}, bf16[4,48,384]{2,1,0:T(8,128)(2,1)S(1)}, u32[]{:S(2)}, u32[]{:S(2)}) collective-permute-start(bf16[4,48,384]{2,1,0:T(8,128)(2,1)S(1)} %get-tuple-element.63), channel_id=1, source_target_pairs={{0,2},{1,3},{2,0},{3,1},{4,6},{5,7},{6,4},{7,5},{8,10},{9,11},{10,... | collective-permute-start | bytes 442376 | tf_op jit(solution)/shard_map/ppermute | solution.py:296
  58.9 6.6 %collective-permute-start.14 = (bf16[48,384]{1,0:T(8,128)(2,1)S(1)}, bf16[48,384]{1,0:T(8,128)(2,1)S(1)}, u32[]{:S(2)}, u32[]{:S(2)}) collective-permute-start(bf16[48,384]{1,0:T(8,128)(2,1)S(1)} %get-tuple-element.77), channel_id=1, source_target_pairs={{0,24},{1,25},{2,26},{3,27},{4,28},{5,29},{6,30},{7,31},{8,16},{9,... | collective-permute-start | bytes 110600 | tf_op jit(solution)/shard_map/ppermute | solution.py:296
  60.8 5.5 %collective-permute-start.13 = (bf16[48,384]{1,0:T(8,128)(2,1)S(1)}, bf16[48,384]{1,0:T(8,128)(2,1)S(1)}, u32[]{:S(2)}, u32[]{:S(2)}) collective-permute-start(bf16[48,384]{1,0:T(8,128)(2,1)S(1)} %get-tuple-element.78), channel_id=1, source_target_pairs={{0,16},{1,17},{2,18},{3,19},{4,20},{5,21},{6,22},{7,23},{8,24},{9,... | collective-permute-start | bytes 110600 | tf_op jit(solution)/shard_map/ppermute | solution.py:296
  62.6 6.2 %collective-permute-start.12 = (bf16[48,384]{1,0:T(8,128)(2,1)S(1)}, bf16[48,384]{1,0:T(8,128)(2,1)S(1)}, u32[]{:S(2)}, u32[]{:S(2)}) collective-permute-start(bf16[48,384]{1,0:T(8,128)(2,1)S(1)} %get-tuple-element.76), channel_id=1, source_target_pairs={{0,8},{1,9},{2,10},{3,11},{4,12},{5,13},{6,14},{7,15},{8,0},{9,1},... | collective-permute-start | bytes 110600 | tf_op jit(solution)/shard_map/ppermute | solution.py:296
  64.2 11.3 %collective-permute-start.20 = (bf16[48,384]{1,0:T(8,128)(2,1)S(1)}, bf16[48,384]{1,0:T(8,128)(2,1)S(1)}, u32[]{:S(2)}, u32[]{:S(2)}) collective-permute-start(bf16[48,384]{1,0:T(8,128)(2,1)S(1)} %get-tuple-element.74), channel_id=1, source_target_pairs={{0,24},{1,25},{2,26},{3,27},{4,28},{5,29},{6,30},{7,31},{8,16},{9,... | collective-permute-start | bytes 110600 | tf_op jit(solution)/shard_map/ppermute | solution.py:296
  65.4 13.0 %collective-permute-start.19 = (bf16[48,384]{1,0:T(8,128)(2,1)S(1)}, bf16[48,384]{1,0:T(8,128)(2,1)S(1)}, u32[]{:S(2)}, u32[]{:S(2)}) collective-permute-start(bf16[48,384]{1,0:T(8,128)(2,1)S(1)} %get-tuple-element.75), channel_id=1, source_target_pairs={{0,16},{1,17},{2,18},{3,19},{4,20},{5,21},{6,22},{7,23},{8,24},{9,... | collective-permute-start | bytes 110600 | tf_op jit(solution)/shard_map/ppermute | solution.py:296
  66.4 12.1 %collective-permute-start.18 = (bf16[48,384]{1,0:T(8,128)(2,1)S(1)}, bf16[48,384]{1,0:T(8,128)(2,1)S(1)}, u32[]{:S(2)}, u32[]{:S(2)}) collective-permute-start(bf16[48,384]{1,0:T(8,128)(2,1)S(1)} %get-tuple-element.73), channel_id=1, source_target_pairs={{0,8},{1,9},{2,10},{3,11},{4,12},{5,13},{6,14},{7,15},{8,0},{9,1},... | collective-permute-start | bytes 110600 | tf_op jit(solution)/shard_map/ppermute | solution.py:296
  68.8 5.7 %collective-permute-start.23 = (bf16[4,56,384]{2,1,0:T(8,128)(2,1)S(1)}, bf16[4,56,384]{2,1,0:T(8,128)(2,1)S(1)}, u32[]{:S(2)}, u32[]{:S(2)}) collective-permute-start(bf16[4,56,384]{2,1,0:T(8,128)(2,1)S(1)} %get-tuple-element.61), channel_id=1, source_target_pairs={{0,4},{1,5},{2,6},{3,7},{4,0},{5,1},{6,2},{7,3},{8,12},{9,13},{10,... | collective-permute-start | bytes 516104 | tf_op jit(solution)/shard_map/ppermute | solution.py:296
  74.5 13.3 %collective-permute-start.39 = (bf16[48,384]{1,0:T(8,128)(2,1)S(1)}, bf16[48,384]{1,0:T(8,128)(2,1)S(1)}, u32[]{:S(2)}, u32[]{:S(2)}) collective-permute-start(bf16[48,384]{1,0:T(8,128)(2,1)S(1)} %get-tuple-element.68), channel_id=1, source_target_pairs={{0,24},{1,25},{2,26},{3,27},{4,28},{5,29},{6,30},{7,31},{8,16},{9,... | collective-permute-start | bytes 110600 | tf_op jit(solution)/shard_map/ppermute | solution.py:296
  75.5 6.4 %collective-permute-start.26 = (bf16[56,384]{1,0:T(8,128)(2,1)S(1)}, bf16[56,384]{1,0:T(8,128)(2,1)S(1)}, u32[]{:S(2)}, u32[]{:S(2)}) collective-permute-start(bf16[56,384]{1,0:T(8,128)(2,1)S(1)} %get-tuple-element.71), channel_id=1, source_target_pairs={{0,24},{1,25},{2,26},{3,27},{4,28},{5,29},{6,30},{7,31},{8,16},{9,... | collective-permute-start | bytes 129032 | tf_op jit(solution)/shard_map/ppermute | solution.py:296
  78.4 5.7 %collective-permute-start.25 = (bf16[56,384]{1,0:T(8,128)(2,1)S(1)}, bf16[56,384]{1,0:T(8,128)(2,1)S(1)}, u32[]{:S(2)}, u32[]{:S(2)}) collective-permute-start(bf16[56,384]{1,0:T(8,128)(2,1)S(1)} %get-tuple-element.72), channel_id=1, source_target_pairs={{0,16},{1,17},{2,18},{3,19},{4,20},{5,21},{6,22},{7,23},{8,24},{9,... | collective-permute-start | bytes 129032 | tf_op jit(solution)/shard_map/ppermute | solution.py:296
  78.4 7.0 %collective-permute-start.24 = (bf16[56,384]{1,0:T(8,128)(2,1)S(1)}, bf16[56,384]{1,0:T(8,128)(2,1)S(1)}, u32[]{:S(2)}, u32[]{:S(2)}) collective-permute-start(bf16[56,384]{1,0:T(8,128)(2,1)S(1)} %get-tuple-element.70), channel_id=1, source_target_pairs={{0,8},{1,9},{2,10},{3,11},{4,12},{5,13},{6,14},{7,15},{8,0},{9,1},... | collective-permute-start | bytes 129032 | tf_op jit(solution)/shard_map/ppermute | solution.py:296
  81.9 8.8 %collective-permute-start.38 = (bf16[48,384]{1,0:T(8,128)(2,1)S(1)}, bf16[48,384]{1,0:T(8,128)(2,1)S(1)}, u32[]{:S(2)}, u32[]{:S(2)}) collective-permute-start(bf16[48,384]{1,0:T(8,128)(2,1)S(1)} %get-tuple-element.68), channel_id=1, source_target_pairs={{0,16},{1,17},{2,18},{3,19},{4,20},{5,21},{6,22},{7,23},{8,24},{9,... | collective-permute-start | bytes 110600 | tf_op jit(solution)/shard_map/ppermute | solution.py:296
  84.1 6.6 %collective-permute-start.37 = (bf16[48,384]{1,0:T(8,128)(2,1)S(1)}, bf16[48,384]{1,0:T(8,128)(2,1)S(1)}, u32[]{:S(2)}, u32[]{:S(2)}) collective-permute-start(bf16[48,384]{1,0:T(8,128)(2,1)S(1)} %get-tuple-element.68), channel_id=1, source_target_pairs={{0,8},{1,9},{2,10},{3,11},{4,12},{5,13},{6,14},{7,15},{8,0},{9,1},... | collective-permute-start | bytes 110600 | tf_op jit(solution)/shard_map/ppermute | solution.py:296
  85.4 13.9 %collective-permute-start.49 = (bf16[48,384]{1,0:T(8,128)(2,1)S(1)}, bf16[48,384]{1,0:T(8,128)(2,1)S(1)}, u32[]{:S(2)}, u32[]{:S(2)}) collective-permute-start(bf16[48,384]{1,0:T(8,128)(2,1)S(1)} %get-tuple-element.66), channel_id=1, source_target_pairs={{0,24},{1,25},{2,26},{3,27},{4,28},{5,29},{6,30},{7,31},{8,16},{9,... | collective-permute-start | bytes 110600 | tf_op jit(solution)/shard_map/ppermute | solution.py:296
  87.8 6.3 %collective-permute-start.29 = (bf16[56,384]{1,0:T(8,128)(2,1)S(1)}, bf16[56,384]{1,0:T(8,128)(2,1)S(1)}, u32[]{:S(2)}, u32[]{:S(2)}) collective-permute-start(bf16[56,384]{1,0:T(8,128)(2,1)S(1)} %select_select_fusion), channel_id=1, source_target_pairs={{0,24},{1,25},{2,26},{3,27},{4,28},{5,29},{6,30},{7,31},{8,16},{9,... | collective-permute-start | bytes 129032 | tf_op jit(solution)/shard_map/ppermute | solution.py:296
  90.7 4.9 %collective-permute-start.28 = (bf16[56,384]{1,0:T(8,128)(2,1)S(1)}, bf16[56,384]{1,0:T(8,128)(2,1)S(1)}, u32[]{:S(2)}, u32[]{:S(2)}) collective-permute-start(bf16[56,384]{1,0:T(8,128)(2,1)S(1)} %select_select_fusion), channel_id=1, source_target_pairs={{0,16},{1,17},{2,18},{3,19},{4,20},{5,21},{6,22},{7,23},{8,24},{9,... | collective-permute-start | bytes 129032 | tf_op jit(solution)/shard_map/ppermute | solution.py:296
  90.7 6.5 %collective-permute-start.27 = (bf16[56,384]{1,0:T(8,128)(2,1)S(1)}, bf16[56,384]{1,0:T(8,128)(2,1)S(1)}, u32[]{:S(2)}, u32[]{:S(2)}) collective-permute-start(bf16[56,384]{1,0:T(8,128)(2,1)S(1)} %select_select_fusion), channel_id=1, source_target_pairs={{0,8},{1,9},{2,10},{3,11},{4,12},{5,13},{6,14},{7,15},{8,0},{9,1},... | collective-permute-start | bytes 129032 | tf_op jit(solution)/shard_map/ppermute | solution.py:296
  94.1 5.3 %collective-permute-start.48 = (bf16[48,384]{1,0:T(8,128)(2,1)S(1)}, bf16[48,384]{1,0:T(8,128)(2,1)S(1)}, u32[]{:S(2)}, u32[]{:S(2)}) collective-permute-start(bf16[48,384]{1,0:T(8,128)(2,1)S(1)} %get-tuple-element.66), channel_id=1, source_target_pairs={{0,16},{1,17},{2,18},{3,19},{4,20},{5,21},{6,22},{7,23},{8,24},{9,... | collective-permute-start | bytes 110600 | tf_op jit(solution)/shard_map/ppermute | solution.py:296
  95.6 4.9 %collective-permute-start.47 = (bf16[48,384]{1,0:T(8,128)(2,1)S(1)}, bf16[48,384]{1,0:T(8,128)(2,1)S(1)}, u32[]{:S(2)}, u32[]{:S(2)}) collective-permute-start(bf16[48,384]{1,0:T(8,128)(2,1)S(1)} %get-tuple-element.66), channel_id=1, source_target_pairs={{0,8},{1,9},{2,10},{3,11},{4,12},{5,13},{6,14},{7,15},{8,0},{9,1},... | collective-permute-start | bytes 110600 | tf_op jit(solution)/shard_map/ppermute | solution.py:296
  97.2 10.6 %collective-permute-start.40 = (bf16[4,48,384]{2,1,0:T(8,128)(2,1)S(1)}, bf16[4,48,384]{2,1,0:T(8,128)(2,1)S(1)}, u32[]{:S(2)}, u32[]{:S(2)}) collective-permute-start(bf16[4,48,384]{2,1,0:T(8,128)(2,1)S(1)} %pad_maximum_fusion.1.refs_2_), channel_id=1, source_target_pairs={{0,4},{1,5},{2,6},{3,7},{4,0},{5,1},{6,2},{7,3},{8,12},{9,13},{10,... | collective-permute-start | bytes 442376 | tf_op jit(solution)/shard_map/ppermute | solution.py:296
  98.0 7.0 %collective-permute-start.7 = (bf16[3,3,8,384]{3,2,1,0:T(8,128)(2,1)S(1)}, bf16[3,3,8,384]{3,2,1,0:T(8,128)(2,1)S(1)}, u32[]{:S(2)}, u32[]{:S(2)}) collective-permute-start(bf16[3,3,8,384]{3,2,1,0:T(8,128)(2,1)S(1)} %get-tuple-element.38), channel_id=1, source_target_pairs={{0,4},{1,5},{2,6},{3,7},{4,8},{5,9},{6,10},{7,11},{8,12},{9,13},{1... | collective-permute-start | bytes 165896 | tf_op jit(solution)/shard_map/ppermute | solution.py:254
  99.3 7.6 %collective-permute-start.6 = (bf16[3,3,8,384]{3,2,1,0:T(8,128)(2,1)S(1)}, bf16[3,3,8,384]{3,2,1,0:T(8,128)(2,1)S(1)}, u32[]{:S(2)}, u32[]{:S(2)}) collective-permute-start(bf16[3,3,8,384]{3,2,1,0:T(8,128)(2,1)S(1)} %get-tuple-element.37), channel_id=1, source_target_pairs={{0,5},{1,6},{2,7},{3,4},{4,9},{5,10},{6,11},{7,8},{8,13},{9,14},{1... | collective-permute-start | bytes 165896 | tf_op jit(solution)/shard_map/ppermute | solution.py:254
  99.3 8.5 %collective-permute-start.41 = (bf16[4,48,384]{2,1,0:T(8,128)(2,1)S(1)}, bf16[4,48,384]{2,1,0:T(8,128)(2,1)S(1)}, u32[]{:S(2)}, u32[]{:S(2)}) collective-permute-start(bf16[4,48,384]{2,1,0:T(8,128)(2,1)S(1)} %pad_maximum_fusion.1.refs_2_), channel_id=1, source_target_pairs={{0,2},{1,3},{2,0},{3,1},{4,6},{5,7},{6,4},{7,5},{8,10},{9,11},{10,... | collective-permute-start | bytes 442376 | tf_op jit(solution)/shard_map/ppermute | solution.py:296
  100.5 9.0 %collective-permute-start.30 = (bf16[4,56,384]{2,1,0:T(8,128)(2,1)S(1)}, bf16[4,56,384]{2,1,0:T(8,128)(2,1)S(1)}, u32[]{:S(2)}, u32[]{:S(2)}) collective-permute-start(bf16[4,56,384]{2,1,0:T(8,128)(2,1)S(1)} %pad_maximum_fusion.refs_18_), channel_id=1, source_target_pairs={{0,4},{1,5},{2,6},{3,7},{4,0},{5,1},{6,2},{7,3},{8,12},{9,13},{10,... | collective-permute-start | bytes 516104 | tf_op jit(solution)/shard_map/ppermute | solution.py:296
  105.0 5.1 %collective-permute-start.43 = (bf16[4,48,384]{2,1,0:T(8,128)(2,1)S(1)}, bf16[4,48,384]{2,1,0:T(8,128)(2,1)S(1)}, u32[]{:S(2)}, u32[]{:S(2)}) collective-permute-start(bf16[4,48,384]{2,1,0:T(8,128)(2,1)S(1)} %pad_maximum_fusion.1.refs_2_), channel_id=1, source_target_pairs={{0,1},{1,0},{2,3},{3,2},{4,5},{5,4},{6,7},{7,6},{8,9},{9,8},{10,11... | collective-permute-start | bytes 442376 | tf_op jit(solution)/shard_map/ppermute | solution.py:296
  106.9 6.8 %collective-permute-start.50 = (bf16[4,48,384]{2,1,0:T(8,128)(2,1)S(1)}, bf16[4,48,384]{2,1,0:T(8,128)(2,1)S(1)}, u32[]{:S(2)}, u32[]{:S(2)}) collective-permute-start(bf16[4,48,384]{2,1,0:T(8,128)(2,1)S(1)} %pad_maximum_fusion.2.refs_10_), channel_id=1, source_target_pairs={{0,2},{1,3},{2,0},{3,1},{4,6},{5,7},{6,4},{7,5},{8,10},{9,11},{10,... | collective-permute-start | bytes 442376 | tf_op jit(solution)/shard_map/ppermute | solution.py:296
  107.8 6.8 %collective-permute-start.51 = (bf16[4,48,384]{2,1,0:T(8,128)(2,1)S(1)}, bf16[4,48,384]{2,1,0:T(8,128)(2,1)S(1)}, u32[]{:S(2)}, u32[]{:S(2)}) collective-permute-start(bf16[4,48,384]{2,1,0:T(8,128)(2,1)S(1)} %pad_maximum_fusion.2.refs_10_), channel_id=1, source_target_pairs={{0,4},{1,5},{2,6},{3,7},{4,0},{5,1},{6,2},{7,3},{8,12},{9,13},{10,... | collective-permute-start | bytes 442376 | tf_op jit(solution)/shard_map/ppermute | solution.py:296
  107.8 14.0 %collective-permute-start.31 = (bf16[4,56,384]{2,1,0:T(8,128)(2,1)S(1)}, bf16[4,56,384]{2,1,0:T(8,128)(2,1)S(1)}, u32[]{:S(2)}, u32[]{:S(2)}) collective-permute-start(bf16[4,56,384]{2,1,0:T(8,128)(2,1)S(1)} %pad_maximum_fusion.refs_18_), channel_id=1, source_target_pairs={{0,2},{1,3},{2,0},{3,1},{4,6},{5,7},{6,4},{7,5},{8,10},{9,11},{10,... | collective-permute-start | bytes 516104 | tf_op jit(solution)/shard_map/ppermute | solution.py:296
  109.6 12.8 %collective-permute-start.32 = (bf16[4,56,384]{2,1,0:T(8,128)(2,1)S(1)}, bf16[4,56,384]{2,1,0:T(8,128)(2,1)S(1)}, u32[]{:S(2)}, u32[]{:S(2)}) collective-permute-start(bf16[4,56,384]{2,1,0:T(8,128)(2,1)S(1)} %collective-permute-done.30.refs_19_), channel_id=1, source_target_pairs={{0,2},{1,3},{2,0},{3,1},{4,6},{5,7},{6,4},{7,5},{8,10},{9,11},{10,... | collective-permute-start | bytes 516104 | tf_op jit(solution)/shard_map/ppermute | solution.py:296
  110.1 4.5 %collective-permute-start.53 = (bf16[4,48,384]{2,1,0:T(8,128)(2,1)S(1)}, bf16[4,48,384]{2,1,0:T(8,128)(2,1)S(1)}, u32[]{:S(2)}, u32[]{:S(2)}) collective-permute-start(bf16[4,48,384]{2,1,0:T(8,128)(2,1)S(1)} %pad_maximum_fusion.2.refs_10_), channel_id=1, source_target_pairs={{0,1},{1,0},{2,3},{3,2},{4,5},{5,4},{6,7},{7,6},{8,9},{9,8},{10,11... | collective-permute-start | bytes 442376 | tf_op jit(solution)/shard_map/ppermute | solution.py:296
  113.7 8.1 %collective-permute-start.42 = (bf16[4,48,384]{2,1,0:T(8,128)(2,1)S(1)}, bf16[4,48,384]{2,1,0:T(8,128)(2,1)S(1)}, u32[]{:S(2)}, u32[]{:S(2)}) collective-permute-start(bf16[4,48,384]{2,1,0:T(8,128)(2,1)S(1)} %collective-permute-done.40.refs_3_), channel_id=1, source_target_pairs={{0,2},{1,3},{2,0},{3,1},{4,6},{5,7},{6,4},{7,5},{8,10},{9,11},{10,... | collective-permute-start | bytes 442376 | tf_op jit(solution)/shard_map/ppermute | solution.py:296
  114.6 7.8 %collective-permute-start.44 = (bf16[4,48,384]{2,1,0:T(8,128)(2,1)S(1)}, bf16[4,48,384]{2,1,0:T(8,128)(2,1)S(1)}, u32[]{:S(2)}, u32[]{:S(2)}) collective-permute-start(bf16[4,48,384]{2,1,0:T(8,128)(2,1)S(1)} %collective-permute-done.40.refs_3_), channel_id=1, source_target_pairs={{0,1},{1,0},{2,3},{3,2},{4,5},{5,4},{6,7},{7,6},{8,9},{9,8},{10,11... | collective-permute-start | bytes 442376 | tf_op jit(solution)/shard_map/ppermute | solution.py:296
  114.6 14.0 %collective-permute-start.33 = (bf16[4,56,384]{2,1,0:T(8,128)(2,1)S(1)}, bf16[4,56,384]{2,1,0:T(8,128)(2,1)S(1)}, u32[]{:S(2)}, u32[]{:S(2)}) collective-permute-start(bf16[4,56,384]{2,1,0:T(8,128)(2,1)S(1)} %pad_maximum_fusion.refs_18_), channel_id=1, source_target_pairs={{0,1},{1,0},{2,3},{3,2},{4,5},{5,4},{6,7},{7,6},{8,9},{9,8},{10,11... | collective-permute-start | bytes 516104 | tf_op jit(solution)/shard_map/ppermute | solution.py:296
  121.8 7.3 %collective-permute-start.34 = (bf16[4,56,384]{2,1,0:T(8,128)(2,1)S(1)}, bf16[4,56,384]{2,1,0:T(8,128)(2,1)S(1)}, u32[]{:S(2)}, u32[]{:S(2)}) collective-permute-start(bf16[4,56,384]{2,1,0:T(8,128)(2,1)S(1)} %collective-permute-done.30.refs_19_), channel_id=1, source_target_pairs={{0,1},{1,0},{2,3},{3,2},{4,5},{5,4},{6,7},{7,6},{8,9},{9,8},{10,11... | collective-permute-start | bytes 516104 | tf_op jit(solution)/shard_map/ppermute | solution.py:296
  121.8 7.4 %collective-permute-start.35 = (bf16[4,56,384]{2,1,0:T(8,128)(2,1)S(1)}, bf16[4,56,384]{2,1,0:T(8,128)(2,1)S(1)}, u32[]{:S(2)}, u32[]{:S(2)}) collective-permute-start(bf16[4,56,384]{2,1,0:T(8,128)(2,1)S(1)} %collective-permute-done.31.refs_20_), channel_id=1, source_target_pairs={{0,1},{1,0},{2,3},{3,2},{4,5},{5,4},{6,7},{7,6},{8,9},{9,8},{10,11... | collective-permute-start | bytes 516104 | tf_op jit(solution)/shard_map/ppermute | solution.py:296
  122.3 7.3 %collective-permute-start.36 = (bf16[4,56,384]{2,1,0:T(8,128)(2,1)S(1)}, bf16[4,56,384]{2,1,0:T(8,128)(2,1)S(1)}, u32[]{:S(2)}, u32[]{:S(2)}) collective-permute-start(bf16[4,56,384]{2,1,0:T(8,128)(2,1)S(1)} %collective-permute-done.32.refs_21_), channel_id=1, source_target_pairs={{0,1},{1,0},{2,3},{3,2},{4,5},{5,4},{6,7},{7,6},{8,9},{9,8},{10,11... | collective-permute-start | bytes 516104 | tf_op jit(solution)/shard_map/ppermute | solution.py:296
  122.4 6.2 %collective-permute-start.52 = (bf16[4,48,384]{2,1,0:T(8,128)(2,1)S(1)}, bf16[4,48,384]{2,1,0:T(8,128)(2,1)S(1)}, u32[]{:S(2)}, u32[]{:S(2)}) collective-permute-start(bf16[4,48,384]{2,1,0:T(8,128)(2,1)S(1)} %collective-permute-done.50.refs_11_), channel_id=1, source_target_pairs={{0,4},{1,5},{2,6},{3,7},{4,0},{5,1},{6,2},{7,3},{8,12},{9,13},{10,... | collective-permute-start | bytes 442376 | tf_op jit(solution)/shard_map/ppermute | solution.py:296
  (24 other events, 121.6 us)

commit v2 on v1

v2 whole, which is shorter than its diff:
```python
import functools
import math

import jax
import jax.numpy as jnp
from jax import lax
from jax.experimental import pallas as pl
from jax.experimental.pallas import tpu as pltpu
from jax.sharding import PartitionSpec as P

HD = 32
WZ = 8
EPS = 1e-05
CUBIC = 0.044715
ROOT_TWO_PI = math.sqrt(2.0 / math.pi)
LOG2_E = 1.0 / math.log(2.0)
LANES = 128
PIECES = 16
BLOCKS = 4
EXTRA = 8
EARLY = 2
KERNEL_VMEM = 40 << 20
F32 = jnp.float32
BF16 = jnp.bfloat16


def dot(a, b):
    return jnp.dot(a, b, preferred_element_type=F32)


def dot_last(a, b):
    return lax.dot_general(a, b, (((1,), (1,)), ((), ())), preferred_element_type=F32)


def dot_first(a, b):
    return lax.dot_general(a, b, (((0,), (0,)), ((), ())), preferred_element_type=F32)


def row_stats(values):
    row_mean = jnp.mean(values, axis=-1, keepdims=True)
    center = values - row_mean
    variance = jnp.mean(center * center, axis=-1, keepdims=True)
    inv_std = lax.rsqrt(variance + EPS)
    return (center * inv_std, inv_std)


def norm_back(incoming, normed, inv_std, gain_vec):
    terms = incoming * normed
    scaled = incoming * gain_vec
    first_mean = jnp.mean(scaled, axis=-1, keepdims=True)
    second_mean = jnp.mean(terms * gain_vec, axis=-1, keepdims=True)
    back = inv_std * (scaled - first_mean - normed * second_mean)
    return (back, jnp.sum(terms, axis=0, keepdims=True))


def head_columns(qkv, head, width):
    group, sub = divmod(head, LANES // HD)
    lo = group * LANES
    mine = lax.broadcasted_iota(jnp.int32, (1, LANES), 1) // HD == sub
    q, k, v = (qkv[:, i * width + lo : i * width + lo + LANES] for i in range(3))
    return (lo, sub, mine, q, k, v)


def low_slot(piece, me, order):
    half = PIECES // 2
    return (piece % half) ^ me[1 + 2 * order + piece // half]


def put_block(stage, block, value, me, order, top=0):
    pieces = PIECES // BLOCKS
    rows = value.shape[0] // pieces
    for i in range(pieces):
        piece = block * pieces + i
        core = piece // (PIECES // 2)
        slot = (core ^ me[0]) * (PIECES // 2) + low_slot(piece, me, order)
        stage[slot, top : top + rows] = value[i * rows : (i + 1) * rows]


def hand_out(stage, keep, send):
    half = stage.shape[0] // 2
    keep[...] = stage[:half]
    send[...] = stage[half:]


def load_window(own, parts, index):
    half_x, half_y = own.shape[0] // 2, own.shape[1] // 2
    rows = [own[half_x:, half_y:]] + [part[index] for part in parts]
    return jnp.concatenate([r.astype(F32).reshape(-1, r.shape[-1]) for r in rows], axis=0)


def forward_kernel(
    me, tok, up_own, part_b, part_c, part_d, code_col, code_row,
    gain1, gain2, b_fc1, w_qkv, w_proj_far, w_fc1_far, w_fc2_far,
    keep, send, small, grad_mid, normed1, inv1, qkv, probs, mix,
    allowed, stage, w_proj, w_fc1, w_fc2, sems,
):
    far = (w_proj_far, w_fc2_far, w_fc1_far)
    near = (w_proj, w_fc2, w_fc1)
    fetch = [pltpu.make_async_copy(a, b, sems.at[i]) for i, (a, b) in enumerate(zip(far, near))]
    for copy in fetch:
        copy.start()
    width = w_proj.shape[0]
    heads = width // HD
    piece = stage.shape[1] // 2
    parts = (part_b, part_c, part_d)
    x = load_window(tok, parts, 0)
    normed, inv = row_stats(x)
    normed1[...] = normed
    inv1[...] = inv
    h1 = (normed * gain1[...]).astype(BF16)
    qkv[...] = dot(h1, w_qkv[...]).astype(BF16)
    allowed[...] = (code_col[...] == code_row[...]).astype(F32)

    for head in range(heads):
        lo, sub, mine, q, k, v = head_columns(qkv, head, width)
        scores = dot_last(jnp.where(mine, q, jnp.zeros_like(q)), k)
        scores = jnp.where(allowed[...] > 0.0, scores, -1e30)
        highest = jnp.max(scores, axis=-1, keepdims=True)
        weight = jnp.exp2((scores - highest) * (HD ** (-0.5) * LOG2_E))
        total = jnp.sum(weight, axis=-1, keepdims=True)
        prob = (weight * (1.0 / total)).astype(BF16)
        probs[head] = prob
        part = dot(prob, v)
        mix[:, lo : lo + LANES] = part if sub == 0 else jnp.where(mine, part, mix[:, lo : lo + LANES])

    for copy in fetch:
        copy.wait()
    mix_low = mix[...].astype(BF16)
    mid = (x + dot(mix_low, w_proj[...])).astype(BF16).astype(F32)
    normed2, inv2 = row_stats(mid)
    h2 = (normed2 * gain2[...]).astype(BF16)
    up = load_window(up_own, parts, 1)
    up_low = up.astype(BF16)

    t2 = None
    for j in range(BLOCKS):
        cols = slice(j * width, (j + 1) * width)
        pre = dot(h2, w_fc1[:, cols]) + b_fc1[:, cols]
        square = pre * pre
        tanh_value = jnp.tanh(ROOT_TWO_PI * pre * (1.0 + CUBIC * square))
        half = 0.5 * (1.0 + tanh_value)
        hidden = (pre * half).astype(BF16)
        slope = half + 0.5 * pre * (1.0 - tanh_value * tanh_value) * (
            ROOT_TWO_PI * (1.0 + 3.0 * CUBIC * square)
        )
        put_block(stage, j, dot_first(hidden, up_low).astype(BF16), me, 0)
        gp = (dot_last(up_low, w_fc2[cols, :]) * slope).astype(BF16)
        small[1 + j : 2 + j, :] = jnp.sum(gp.astype(F32), axis=0, keepdims=True)
        put_block(stage, j, dot_first(h2, gp).astype(BF16), me, 0, piece)
        part = dot_last(gp, w_fc1[:, cols])
        t2 = part if t2 is None else t2 + part
    back2, s_ln2 = norm_back(t2, normed2, inv2, gain2[...])
    small[0:1, :] = s_ln2
    grad_mid[...] = up + back2
    hand_out(stage, keep, send)


def heads_back(groups, qkv, probs, mix, dmix, dqkv):
    width = mix.shape[1]
    score_scale = HD ** (-0.5)
    per_group = LANES // HD
    for group in groups:
        sums = None
        for head in range(group * per_group, (group + 1) * per_group):
            lo, sub, mine, q, k, v = head_columns(qkv, head, width)
            do = dmix[:, lo : lo + LANES]
            do_mine = jnp.where(mine, do, jnp.zeros_like(do))
            delta = jnp.sum(do_mine.astype(F32) * mix[:, lo : lo + LANES], axis=-1, keepdims=True)
            prob = probs[head]
            ds = (prob.astype(F32) * (dot_last(do_mine, v) - delta)).astype(BF16)
            parts = (dot(ds, k) * score_scale, dot_first(ds, q) * score_scale, dot_first(prob, do))
            sums = parts if sums is None else [jnp.where(mine, a, b) for a, b in zip(parts, sums)]
        for i, part in enumerate(sums):
            dqkv[:, i * width + lo : i * width + lo + LANES] = part.astype(BF16)


def first_back_kernel(me, grad_mid, qkv, probs, mix, w_proj, dmix, dqkv):
    dmix[...] = dot_last(grad_mid[...].astype(BF16), w_proj[...]).astype(BF16)
    heads_back(range(EARLY), qkv, probs, mix, dmix, dqkv)


def second_back_kernel(
    me, small, grad_mid, normed1, inv1, qkv, probs, mix, dmix, dqkv_early, gain1, w_qkv,
    out_a, out_b, out_c, out_d, keep_t, send_t,
    dqkv, stage_t,
):
    width = mix.shape[1]
    pieces, rows, _ = stage_t.shape
    stage_t[:, rows - EXTRA :] = jnp.zeros((pieces, EXTRA, width), BF16)
    extra = [me[0] * (PIECES // 2) + low_slot(i, me, 1) for i in range(BLOCKS + 2)]
    for i in range(BLOCKS + 1):
        stage_t[extra[i + 1], rows - EXTRA : rows - EXTRA + 1] = small[i : i + 1, :].astype(BF16)
    grad_attn = grad_mid[...].astype(BF16)
    put_block(stage_t, 3, dot_first(mix[...].astype(BF16), grad_attn).astype(BF16), me, 1)
    heads_back(range(EARLY, width // LANES), qkv, probs, mix, dmix, dqkv)
    normed = normed1[...]
    h1 = (normed * gain1[...]).astype(BF16)
    t1 = None
    early = EARLY * LANES
    for j in range(3):
        lo = j * width
        own = jnp.concatenate(
            [dqkv_early[:, lo : lo + early], dqkv[:, lo + early : lo + width]], axis=1
        )
        put_block(stage_t, j, dot_first(h1, own).astype(BF16), me, 1)
        part = dot_last(own, w_qkv[:, lo : lo + width])
        t1 = part if t1 is None else t1 + part
    back1, s_ln1 = norm_back(t1, normed, inv1[...], gain1[...])
    stage_t[extra[0], rows - EXTRA : rows - EXTRA + 1] = s_ln1.astype(BF16)
    hand_out(stage_t, keep_t, send_t)
    result = grad_mid[...] + back1
    quarter = result.shape[0] // 4
    for i, ref in enumerate((out_a, out_b, out_c, out_d)):
        ref[...] = result[i * quarter : (i + 1) * quarter].reshape(ref.shape).astype(BF16)


def finish_kernel(*refs):
    me, back_a, back_b, back_c, back_d = refs[:5]
    parts = refs[5:-14]
    out, g_ln1, g_qkv, g_proj, g_ln2, g_fc1, g_bfc1, g_fc2 = refs[-14:-6]
    out_near, fc1, fc2, both, smalls, sems = refs[-6:]
    half = PIECES // 2
    width, ff = fc1.shape
    rows = width * BLOCKS // PIECES
    half_x, half_y = out_near.shape[0] // 2, out_near.shape[1] // 2
    copies = []

    def leave(source, target):
        copies.append(pltpu.make_async_copy(source, target, sems.at[len(copies)]))
        copies[-1].start()

    out_near[half_x:, half_y:] = back_a[...]
    out_near[half_x:, :half_y] = back_b[...]
    out_near[:half_x, half_y:] = back_c[...]
    out_near[:half_x, :half_y] = back_d[...]
    leave(out_near, out)
    total = jnp.zeros((8, width), F32)
    for ref in parts:
        for j in range(ref.shape[0]):
            value = ref[j].astype(F32)
            total = total + jnp.sum((value * value).reshape(-1, 8, width), axis=0)
    total = jnp.sum(jnp.sum(total, axis=0, keepdims=True), axis=1, keepdims=True)
    factor = math.sqrt(param_count(width, ff)) * lax.rsqrt(total)
    per_block = PIECES // BLOCKS
    slots_t = [arrivals(ORDERS[1], core) for core in range(2)]

    def spot(core, order, slot):
        piece = core * half + (slot ^ jnp.where(core == 0, me[1 + 2 * order], me[2 + 2 * order]))
        top = pl.multiple_of(piece % per_block * rows, rows)
        left = pl.multiple_of(piece // per_block * width, width)
        return piece, pl.ds(top, rows), pl.ds(left, width)

    for kind in range(2):
        for i, ref in enumerate(parts):
            core = me[0] ^ (i // 2)
            for j in range(ref.shape[0]):
                slot = i % 2 * ref.shape[0] + j
                if kind == 0:
                    value = ref[j, : 2 * rows].astype(F32) * factor
                    piece, down, across = spot(core, 0, slot)
                    fc2[pl.ds(pl.multiple_of(piece * rows, rows), rows), :] = value[:rows].astype(BF16)
                    fc1[down, across] = value[rows:].astype(BF16)
                else:
                    value = ref[j, 2 * rows :].astype(F32) * factor
                    slot_t = jnp.where(core == 0, slots_t[0][slot], slots_t[1][slot])
                    piece, down, across = spot(core, 1, slot_t)
                    both[down, across] = value[:rows].astype(BF16)
                    smalls[piece] = value[rows:]
        if kind == 0:
            leave(fc2, g_fc2)
            leave(fc1, g_fc1)
        else:
            leave(both.at[:, : 3 * width], g_qkv)
            leave(both.at[:, 3 * width :], g_proj)
    g_ln1[...] = smalls[0, 0]
    g_ln2[...] = smalls[1, 0]
    for j in range(BLOCKS):
        g_bfc1[j * width : (j + 1) * width] = smalls[2 + j, 0]
    for copy in copies:
        copy.wait()


def param_count(width, ff):
    return 4 * width * width + 2 * width * ff + 2 * width + ff


VMEM = pl.BlockSpec(memory_space=pltpu.VMEM)
SMEM = pl.BlockSpec(memory_space=pltpu.SMEM)
HBM = pl.BlockSpec(memory_space=pltpu.HBM)


def shape(dims, dtype):
    return jax.ShapeDtypeStruct(dims, dtype)


def like(*arrays):
    return [pltpu.VMEM(a.shape, a.dtype) for a in arrays]


def call(kernel, outs, scratch, flops, me, near, far=(), out_specs=None):
    far = tuple(pltpu.with_memory_space_constraint(a, pltpu.HBM) for a in far)
    args = (me, *near, *far)
    moved = sum(a.size * a.dtype.itemsize for a in args) + sum(
        math.prod(o.shape) * o.dtype.itemsize for o in outs
    )
    return pl.pallas_call(
        kernel,
        out_shape=outs,
        in_specs=[SMEM] + [VMEM] * len(near) + [HBM] * len(far),
        out_specs=out_specs or (VMEM,) * len(outs),
        scratch_shapes=scratch,
        cost_estimate=pl.CostEstimate(flops=flops, bytes_accessed=moved, transcendentals=0),
        compiler_params=pltpu.CompilerParams(vmem_limit_bytes=KERNEL_VMEM),
    )(*args)


def neighbour(shard, step_x, step_y):
    size_x, size_y = lax.axis_size("gx"), lax.axis_size("gy")
    pairs = [
        (x * size_y + y, (x + step_x) % size_x * size_y + (y + step_y) % size_y)
        for x in range(size_x)
        for y in range(size_y)
    ]
    return lax.ppermute(shard, ("gx", "gy"), pairs)


def arriving(tile):
    half_x, half_y = tile.shape[1] // 2, tile.shape[2] // 2
    return (
        neighbour(tile[:, half_x:, :half_y], 0, -1),
        neighbour(tile[:, :half_x, half_y:], -1, 0),
        neighbour(tile[:, :half_x, :half_y], -1, -1),
    )


def window_codes(labels):
    tile_x, tile_y, tile_z = labels.shape
    half_x, half_y = tile_x // 2, tile_y // 2
    last_x = (lax.axis_index("gx") == lax.axis_size("gx") - 1).astype(jnp.int32)
    last_y = (lax.axis_index("gy") == lax.axis_size("gy") - 1).astype(jnp.int32)
    upper_x = (jnp.arange(tile_x) >= half_x).astype(jnp.int32)
    upper_y = (jnp.arange(tile_y) >= half_y).astype(jnp.int32)
    upper_z = (jnp.arange(tile_z) >= tile_z - WZ // 2).astype(jnp.int32)
    codes = (
        labels * 8
        + (4 * last_x) * upper_x[:, None, None]
        + (2 * last_y) * upper_y[None, :, None]
        + upper_z[None, None, :]
    )
    codes = jnp.roll(codes, WZ // 2, axis=2)
    parts = (
        codes[:half_x, :half_y], codes[:half_x, half_y:],
        codes[half_x:, :half_y], codes[half_x:, half_y:],
    )
    return jnp.concatenate([part.reshape(-1) for part in parts])


def swap(shard, flips):
    size_x, size_y = lax.axis_size("gx"), lax.axis_size("gy")
    pairs = [
        (x * size_y + y, (x ^ flips[y % 2][0]) * size_y + (y ^ flips[y % 2][1]))
        for x in range(size_x)
        for y in range(size_y)
    ]
    return lax.ppermute(shard, ("gx", "gy"), pairs)


def add(first, *others):
    total = first.astype(F32)
    for other in others:
        total = total + other.astype(F32)
    return total


SIDE, NEAR, LAYER = (0, 2), (1, 0), (2, 0)
CORE = ((0, 1), (0, 1))
SPARE = 4
ORDERS = (
    ((SIDE, LAYER), (NEAR, SIDE), (LAYER, NEAR)),
    ((NEAR, NEAR), (LAYER, LAYER), (SIDE, SIDE)),
)


def arrivals(order, core):
    slots = [0]
    for flips in reversed(ORDERS[0]):
        bit = 2 - [step[core] for step in order].index(flips[core])
        slots = slots + [slot | 1 << bit for slot in slots]
    return slots


def place():
    index_x, index_y = lax.axis_index("gx"), lax.axis_index("gy")
    numbers = [index_y % 2]
    for order in ORDERS:
        for core in range(2):
            number = jnp.int32(0)
            for flips in order:
                flip_x, flip_y = flips[core]
                bit = (index_x & flip_x) if flip_x else (index_y & flip_y)
                number = 2 * number + (bit != 0).astype(jnp.int32)
            numbers.append(number)
    return jnp.stack(numbers)


def fold(keep, got):
    half = keep.shape[0] // 2
    return (
        add(keep[:half], got[:half]).astype(BF16),
        add(keep[half:], got[half:]).astype(BF16),
    )


def after(values, first):
    return lax.optimization_barrier((*values, first))[: len(values)]


def spares():
    for axis in (0, 1):
        spare = SPARE
        while spare < lax.axis_size(("gx", "gy")[axis]):
            yield ((spare, 0) if axis == 0 else (0, spare),) * 2
            spare *= 2


def reduce_all(keep, send, got, keep_t, send_t, away):
    order, order_t = ORDERS
    got_t, = after([swap(send_t, CORE)], send)
    keep_t, send_t = fold(keep_t, got_t)
    for step in range(3):
        got_t = swap(send_t, order_t[step])
        got, = after([got], send_t)
        if step < 2:
            keep, send = fold(keep, got)
            got = swap(send, order[step + 1])
            got_t, = after([got_t], send)
            keep_t, send_t = fold(keep_t, got_t)
        else:
            low = add(keep[0], got[0]).astype(BF16)
            got_t, = after([got_t], low)
            low_t = add(keep_t[0], got_t[0]).astype(BF16)
    for flips in spares():
        got, got_t = swap(low, flips), swap(low_t, flips)
        low = add(low, after([got], low_t)[0]).astype(BF16)
        low_t = add(low_t, after([got_t], low)[0]).astype(BF16)
    own = jnp.concatenate([low, low_t])[None]
    two = jnp.concatenate([own, swap(own, order[2])])
    four = jnp.concatenate([two, swap(two, order[1])])
    side = swap(four, order[0])
    away = after(away, four)
    back = [neighbour(away[0], 0, 1), neighbour(away[1], 1, 0), neighbour(away[2], 1, 1)]
    side, *back = after([side, *back], four)
    return back, [four, side, swap(four, CORE), swap(side, CORE)]


def body(tokens, upstream, window_labels, ln1_gain, w_qkv, w_proj, ln2_gain, w_fc1, b_fc1, w_fc2):
    width, ff = w_fc1.shape
    heads = width // HD
    parts = arriving(jnp.stack([tokens, upstream]))
    codes = window_codes(window_labels)
    rows = codes.shape[0]
    me = place()
    piece = BLOCKS * width // PIECES
    half = shape((PIECES // 2, 2 * piece, width), BF16)
    half_t = shape((PIECES // 2, piece + EXTRA, width), BF16)
    gain1 = ln1_gain[None, :]
    keep, send, *saved = call(
        forward_kernel,
        (half, half)
        + (shape((1 + BLOCKS, width), F32), shape((rows, width), F32), shape((rows, width), F32), shape((rows, 1), F32))
        + (shape((rows, 3 * width), BF16), shape((heads, rows, rows), BF16), shape((rows, width), F32)),
        [pltpu.VMEM((rows, rows), F32), pltpu.VMEM((PIECES, 2 * piece, width), BF16)]
        + like(w_proj, w_fc1, w_fc2)
        + [pltpu.SemaphoreType.DMA((3,))],
        2 * rows * width * (4 * width + 5 * ff) + 4 * heads * rows * rows * LANES,
        me,
        (tokens, upstream, *parts, codes[:, None], codes[None, :], gain1, ln2_gain[None, :], b_fc1[None, :], w_qkv),
        (w_proj, w_fc1, w_fc2),
    )
    quarter = shape(parts[0].shape[1:], BF16)
    small, grad_mid, normed1, inv1, qkv, probs, mix = saved
    got = swap(send, CORE)
    dmix, dqkv = call(
        first_back_kernel,
        (shape((rows, width), BF16), shape((rows, 3 * width), BF16)),
        [],
        2 * rows * width * width + 8 * EARLY * (LANES // HD) * rows * rows * LANES,
        me,
        (grad_mid, qkv, probs, mix, w_proj),
    )
    got, = after([got], dmix)
    keep, send = fold(keep, got)
    got = swap(send, ORDERS[0][0])
    dmix, = after([dmix], send)
    *done, keep_t, send_t = call(
        second_back_kernel,
        (quarter,) * 4 + (half_t, half_t),
        [pltpu.VMEM((rows, 3 * width), BF16), pltpu.VMEM((PIECES, piece + EXTRA, width), BF16)],
        2 * rows * width * 7 * width + 8 * (heads - EARLY * (LANES // HD)) * rows * rows * LANES,
        me,
        (small, grad_mid, normed1, inv1, qkv, probs, mix, dmix, dqkv, gain1, w_qkv),
    )
    back, slots = reduce_all(keep, send, got, keep_t, send_t, done[1:])
    result, g_ln1, g_qkv, g_proj, g_ln2, g_fc1, g_bfc1, g_fc2 = call(
        finish_kernel,
        (
            shape(tokens.shape, BF16), shape((width,), F32), shape((width, 3 * width), BF16),
            shape((width, width), BF16), shape((width,), F32), shape((width, ff), BF16),
            shape((ff,), F32), shape((ff, width), BF16),
        ),
        like(tokens, w_fc1, w_fc2)
        + [
            pltpu.VMEM((width, 4 * width), BF16),
            pltpu.VMEM((PIECES, EXTRA, width), F32),
            pltpu.SemaphoreType.DMA((5,)),
        ],
        4 * width * width,
        me,
        (done[0], *back, *slots),
        out_specs=(HBM, VMEM, HBM, HBM, VMEM, HBM, VMEM, HBM),
    )
    return (result, g_ln1, g_qkv, g_proj, g_ln2, g_fc1, g_bfc1, g_fc2)


def solution(mesh):
    return jax.shard_map(
        body,
        mesh=mesh,
        in_specs=(
            P("gx", "gy", None, None),
            P("gx", "gy", None, None),
            P("gx", "gy", None),
            P(), P(), P(), P(), P(), P(), P(),
        ),
        out_specs=(P("gx", "gy", None, None), P(), P(), P(), P(), P(), P(), P()),
        check_vma=False,
    )
```

time: 138 us -> 107 us (0.78)
  starting transfers between devices: 54.3 us -> 18.6 us
  waiting for transfers between devices: 40.2 us -> 57.4 us
  local copies, waits for them, and re-layouts: 12.6 us -> 1.59 us
  Pallas kernels: 21.9 us -> 24.7 us
  other arithmetic: 5.49 us -> 3.24 us
  between operations: 2.97 us -> 1.08 us
    ppermute x48 -> x15, starting transfers between devices: 43.6 us -> 8.65 us  [swap(): return lax.ppermute(shard, ('gx', 'gy'), pairs)]
    ppermute x9 -> x6, waiting for transfers between devices: 6.34 us -> 15.3 us  [neighbour(): return lax.ppermute(shard, ('gx', 'gy'), pairs)]
    ppermute x48 -> x15, waiting for transfers between devices: 33.8 us -> 42.1 us  [swap(): return lax.ppermute(shard, ('gx', 'gy'), pairs)]
    unnamed x30 -> x14, local copies, waits for them, and re-layouts: 7.72 us -> 0.96 us
    slice x20 -> x0, local copies, waits for them, and re-layouts: 3.54 us -> none  [the longest x2 1.94 us: quarters(): tile[:half_x, :half_y]]
    pallas_call x3 -> x4, Pallas kernels: 21.9 us -> 24.7 us  [call(): pl.pallas_call(kernel, out_shape=outs, in_specs=[SMEM] + [VMEM] * len(nea...]
    ppermute x9 -> x6, starting transfers between devices: 10.7 us -> 9.91 us  [neighbour(): return lax.ppermute(shard, ('gx', 'gy'), pairs)]
  transfers between devices with their start and end apart: 57 -> 21, of which waited for: 14 -> 16; matrix products, arithmetic and copies ran while one was open for 6% -> 2% of each run, Pallas kernels for 5% -> 4%
where the time goes in v2:
time: 107 us
  waiting for transfers between devices  57.4 us (54%)
  Pallas kernels  24.7 us (23%)
  starting transfers between devices  18.6 us (17%)
  other arithmetic  3.24 us (3%)
  local copies, waits for them, and re-layouts  1.59 us (1%)
  between operations  1.08 us (1%)
    ppermute x15, waiting for transfers between devices, swap(): return lax.ppermute(shard, ('gx', 'gy'), pairs)  42.1 us
    pallas_call x4, Pallas kernels, call(): pl.pallas_call(kernel, out_shape=outs, in_specs=[SMEM] + [VMEM] * len(nea...  24.7 us
    ppermute x6, waiting for transfers between devices, neighbour(): return lax.ppermute(shard, ('gx', 'gy'), pairs)  15.3 us
    ppermute x6, starting transfers between devices, neighbour(): return lax.ppermute(shard, ('gx', 'gy'), pairs)  9.91 us
    ppermute x15, starting transfers between devices, swap(): return lax.ppermute(shard, ('gx', 'gy'), pairs)  8.65 us
  transfers between devices with their start and end apart: 21, of which 16 were waited for; matrix products, arithmetic and copies ran while one was open for 2% of the time, Pallas kernels for 4%

profile of v2, /device:TPU:0, one launch (start us, length us, event | category | flops | bytes accessed | tf_op | source)
XLA Modules:
  0.0 106.5 jit_solution(17967843542576469585)
XLA Ops:
  0.7 1.1 %pad_maximum_fusion.2 = (bf16[2,3,3,8,384]{4,3,2,1,0:T(8,128)(2,1)S(1)}, bf16[2,3,3,8,384]{4,3,2,1,0:T(8,128)(2,1)S(1)}, bf16[2,3,3,8,384]{4,3,2,1,0:T(8,128)(2,1)S(1)}) fusion(bf16[1,6,6,8,384]{4,3,2,1,0:T(8,128)(2,1)} %bitcast.13, bf16[1,6,6,8,384]{4,3,2,1,0:T(8,128)(2,1)} %bitcast.12), kind=kLoop, calls=%fused_computation.20 | loop fusion | flops 165888 | bytes 774144 | tf_op jit(solution)/shard_map/stack | solution.py:459
  1.8 2.4 %collective-permute-start = (bf16[2,3,3,8,384]{4,3,2,1,0:T(8,128)(2,1)S(1)}, bf16[2,3,3,8,384]{4,3,2,1,0:T(8,128)(2,1)S(1)}, u32[]{:S(2)}, u32[]{:S(2)}) collective-permute-start(bf16[2,3,3,8,384]{4,3,2,1,0:T(8,128)(2,1)S(1)} %get-tuple-element.88), channel_id=1, source_target_pairs={{0,3},{1,0},{2,1},{3,2},{4,7},{5,4},{6,5},{7,6},{8,11},{9,8},{10,9... | collective-permute-start | bytes 331784 | tf_op jit(solution)/shard_map/ppermute | solution.py:324
  4.2 4.6 %collective-permute-start.1 = (bf16[2,3,3,8,384]{4,3,2,1,0:T(8,128)(2,1)S(1)}, bf16[2,3,3,8,384]{4,3,2,1,0:T(8,128)(2,1)S(1)}, u32[]{:S(2)}, u32[]{:S(2)}) collective-permute-start(bf16[2,3,3,8,384]{4,3,2,1,0:T(8,128)(2,1)S(1)} %get-tuple-element.87), channel_id=1, source_target_pairs={{0,28},{1,29},{2,30},{3,31},{4,0},{5,1},{6,2},{7,3},{8,4},{9,5},{1... | collective-permute-start | bytes 331784 | tf_op jit(solution)/shard_map/ppermute | solution.py:324
  8.8 0.3 collective-permute-start.2
  9.1 0.8 add_add_fusion
  10.1 0.1 reshape.53
  10.2 0.1 reshape.54
  10.3 0.1 reshape.55
  10.4 0.1 reshape.56
  10.5 0.1 broadcast_in_dim.27.code_col
  10.8 0.1 stack.29.me.refs_0_
  10.8 1.3 %collective-permute-done.1.part_c = bf16[2,3,3,8,384]{4,3,2,1,0:T(8,128)(2,1)S(1)} collective-permute-done((bf16[2,3,3,8,384]{4,3,2,1,0:T(8,128)(2,1)S(1)}, bf16[2,3,3,8,384]{4,3,2,1,0:T(8,128)(2,1)S(1)}, u32[]{:S(2)}, u32[]{:S(2)}) %collective-permute-start.1) | collective-permute-done | bytes 110624 | tf_op jit(solution)/shard_map/ppermute | solution.py:324
  12.2 2.0 %collective-permute-done.2.part_d = bf16[2,3,3,8,384]{4,3,2,1,0:T(8,128)(2,1)S(1)} collective-permute-done((bf16[2,3,3,8,384]{4,3,2,1,0:T(8,128)(2,1)S(1)}, bf16[2,3,3,8,384]{4,3,2,1,0:T(8,128)(2,1)S(1)}, u32[]{:S(2)}, u32[]{:S(2)}) %collective-permute-start.2) | collective-permute-done | bytes 110624 | tf_op jit(solution)/shard_map/ppermute | solution.py:324
  14.2 0.9 copy-done.3
  15.1 13.2 %shard_map.161 = (bf16[8,192,384]{2,1,0:T(8,128)(2,1)S(1)}, bf16[8,192,384]{2,1,0:T(8,128)(2,1)S(1)}, f32[5,384]{1,0:T(8,128)S(1)}, f32[288,384]{1,0:T(8,128)S(1...) custom-call(s32[5]{0:T(128)S(1)} %stack.29.me.refs_0_, ...), custom_call_target="tpu_custom_call" | custom-call | flops 2548039680 | bytes 10674068 | tf_op jit(solution)/shard_map/pallas_call | solution.py:306
  28.4 4.0 %shard_map.162 = (bf16[288,384]{1,0:T(8,128)(2,1)S(1)}, bf16[288,1152]{1,0:T(8,128)(2,1)S(1)}) custom-call(s32[5]{0:T(128)S(1)} %stack.29.me.refs_0_, f32[288,384]{1,0:T(8,128)S(1)} %get-tuple-element.44.grad_mid, bf16[288,1152]{1,0:T(8,128)(2,1)S(1)} %get-tuple-element.47.qkv, bf16[12,288,288]{2,1,0:T(8,128)(2,1)S(1)} %get-tuple-element.48.probs, ...), custom_call_target="tpu_custom_call" | custom-call | flops 764411904 | bytes 4718612 | tf_op jit(solution)/shard_map/pallas_call | solution.py:306
  32.4 0.3 add_convert_fusion
  32.7 3.7 %shard_map.163 = (bf16[3,3,8,384]{3,2,1,0:T(8,128)(2,1)S(1)}, bf16[3,3,8,384]{3,2,1,0:T(8,128)(2,1)S(1)}, bf16[3,3,8,384]{3,2,1,0:T(8,128)(2,1)S(1)}, bf16[3,3,8...) custom-call(s32[5]{0:T(128)S(1)} %stack.29.me.refs_0_, ...), custom_call_target="tpu_custom_call" | custom-call | flops 934281216 | bytes 7260308 | tf_op jit(solution)/shard_map/pallas_call | solution.py:306
  36.5 0.6 collective-permute-start.5
  37.0 0.6 collective-permute-start.4
  37.6 1.1 %collective-permute-done.5 = bf16[8,104,384]{2,1,0:T(8,128)(2,1)S(1)} collective-permute-done((bf16[8,104,384]{2,1,0:T(8,128)(2,1)S(1)}, bf16[8,104,384]{2,1,0:T(8,128)(2,1)S(1)}, u32[]{:S(2)}, u32[]{:S(2)}) %collective-permute-start.5) | collective-permute-done | bytes 639008 | tf_op jit(solution)/shard_map/ppermute | solution.py:365
  38.7 0.2 add_convert_fusion.3
  38.9 0.1 collective-permute-start.7
  39.0 7.9 %collective-permute-done.4 = bf16[4,192,384]{2,1,0:T(8,128)(2,1)S(1)} collective-permute-done((bf16[4,192,384]{2,1,0:T(8,128)(2,1)S(1)}, bf16[4,192,384]{2,1,0:T(8,128)(2,1)S(1)}, u32[]{:S(2)}, u32[]{:S(2)}) %collective-permute-start.4) | collective-permute-done | bytes 589856 | tf_op jit(solution)/shard_map/ppermute | solution.py:365
  46.9 0.2 add_convert_fusion.5
  47.1 1.6 %collective-permute-done.7 = bf16[4,104,384]{2,1,0:T(8,128)(2,1)S(1)} collective-permute-done((bf16[4,104,384]{2,1,0:T(8,128)(2,1)S(1)}, bf16[4,104,384]{2,1,0:T(8,128)(2,1)S(1)}, u32[]{:S(2)}, u32[]{:S(2)}) %collective-permute-start.7) | collective-permute-done | bytes 319520 | tf_op jit(solution)/shard_map/ppermute | solution.py:365
  48.9 4.9 %collective-permute-done.6 = bf16[2,192,384]{2,1,0:T(8,128)(2,1)S(1)} collective-permute-done((bf16[2,192,384]{2,1,0:T(8,128)(2,1)S(1)}, bf16[2,192,384]{2,1,0:T(8,128)(2,1)S(1)}, u32[]{:S(2)}, u32[]{:S(2)}) %collective-permute-start.6) | collective-permute-done | bytes 294944 | tf_op jit(solution)/shard_map/ppermute | solution.py:365
  54.0 0.5 collective-permute-done.9
  54.5 0.6 collective-permute-start.11
  55.1 3.9 %collective-permute-done.8 = bf16[1,192,384]{2,1,0:T(8,128)(2,1)S(1)} collective-permute-done((bf16[1,192,384]{2,1,0:T(8,128)(2,1)S(1)}, bf16[1,192,384]{2,1,0:T(8,128)(2,1)S(1)}, u32[]{:S(2)}, u32[]{:S(2)}) %collective-permute-start.8) | collective-permute-done | bytes 147488 | tf_op jit(solution)/shard_map/ppermute | solution.py:365
  59.1 1.7 %collective-permute-start.10 = (bf16[192,384]{1,0:T(8,128)(2,1)S(1)}, bf16[192,384]{1,0:T(8,128)(2,1)S(1)}, u32[]{:S(2)}, u32[]{:S(2)}) collective-permute-start(bf16[192,384]{1,0:T(8,128)(2,1)S(1)} %fusion), channel_id=1, source_target_pairs={{0,16},{1,17},{2,18},{3,19},{4,20},{5,21},{6,22},{7,23},{8,24},{9,... | collective-permute-start | bytes 442376 | tf_op jit(solution)/shard_map/ppermute | solution.py:365
  60.9 1.4 %collective-permute-start.12 = (bf16[104,384]{1,0:T(8,128)(2,1)S(1)}, bf16[104,384]{1,0:T(8,128)(2,1)S(1)}, u32[]{:S(2)}, u32[]{:S(2)}) collective-permute-start(bf16[104,384]{1,0:T(8,128)(2,1)S(1)} %fusion.1), channel_id=1, source_target_pairs={{0,16},{1,17},{2,18},{3,19},{4,20},{5,21},{6,22},{7,23},{8,24},{9,... | collective-permute-start | bytes 239624 | tf_op jit(solution)/shard_map/ppermute | solution.py:365
  62.2 6.6 %collective-permute-done.10 = bf16[192,384]{1,0:T(8,128)(2,1)S(1)} collective-permute-done((bf16[192,384]{1,0:T(8,128)(2,1)S(1)}, bf16[192,384]{1,0:T(8,128)(2,1)S(1)}, u32[]{:S(2)}, u32[]{:S(2)}) %collective-permute-start.10) | collective-permute-done | bytes 147488 | tf_op jit(solution)/shard_map/ppermute | solution.py:365
  68.9 0.8 collective-permute-done.12
  69.7 0.7 collective-permute-start.13
  70.4 5.4 %collective-permute-done.13 = bf16[1,296,384]{2,1,0:T(8,128)(2,1)S(1)} collective-permute-done((bf16[1,296,384]{2,1,0:T(8,128)(2,1)S(1)}, bf16[1,296,384]{2,1,0:T(8,128)(2,1)S(1)}, u32[]{:S(2)}, u32[]{:S(2)}) %collective-permute-start.13) | collective-permute-done | bytes 227360 | tf_op jit(solution)/shard_map/ppermute | solution.py:365
  75.9 1.7 %collective-permute-start.14 = (bf16[2,296,384]{2,1,0:T(8,128)(2,1)S(1)}, bf16[2,296,384]{2,1,0:T(8,128)(2,1)S(1)}, u32[]{:S(2)}, u32[]{:S(2)}) collective-permute-start(bf16[2,296,384]{2,1,0:T(8,128)(2,1)S(1)} %pad_maximum_fusion.1), channel_id=1, source_target_pairs={{0,4},{1,3},{2,6},{3,1},{4,0},{5,7},{6,2},{7,5},{8,12},{9,11},{10,... | collective-permute-start | bytes 1363976 | tf_op jit(solution)/shard_map/ppermute | solution.py:365
  77.5 6.8 %collective-permute-done.14 = bf16[2,296,384]{2,1,0:T(8,128)(2,1)S(1)} collective-permute-done((bf16[2,296,384]{2,1,0:T(8,128)(2,1)S(1)}, bf16[2,296,384]{2,1,0:T(8,128)(2,1)S(1)}, u32[]{:S(2)}, u32[]{:S(2)}) %collective-permute-start.14) | collective-permute-done | bytes 454688 | tf_op jit(solution)/shard_map/ppermute | solution.py:365
  84.4 0.1 pad_maximum_fusion.refs_5_
  84.5 1.0 collective-permute-start.15
  85.5 1.7 %collective-permute-start.17 = (bf16[3,3,8,384]{3,2,1,0:T(8,128)(2,1)S(1)}, bf16[3,3,8,384]{3,2,1,0:T(8,128)(2,1)S(1)}, u32[]{:S(2)}, u32[]{:S(2)}) collective-permute-start(bf16[3,3,8,384]{3,2,1,0:T(8,128)(2,1)S(1)} %get-tuple-element.72), channel_id=1, source_target_pairs={{0,4},{1,5},{2,6},{3,7},{4,8},{5,9},{6,10},{7,11},{8,12},{9,13},{1... | collective-permute-start | bytes 165896 | tf_op jit(solution)/shard_map/ppermute | solution.py:324
  87.2 0.8 collective-permute-start.18
  88.1 0.1 collective-permute-start.19
  88.2 1.4 %collective-permute-done.16.refs_2_ = bf16[3,3,8,384]{3,2,1,0:T(8,128)(2,1)S(1)} collective-permute-done((bf16[3,3,8,384]{3,2,1,0:T(8,128)(2,1)S(1)}, bf16[3,3,8,384]{3,2,1,0:T(8,128)(2,1)S(1)}, u32[]{:S(2)}, u32[]{:S(2)}) %collective-permute-start.16) | collective-permute-done | bytes 55328 | tf_op jit(solution)/shard_map/ppermute | solution.py:324
  89.5 3.4 %collective-permute-done.17.refs_3_ = bf16[3,3,8,384]{3,2,1,0:T(8,128)(2,1)S(1)} collective-permute-done((bf16[3,3,8,384]{3,2,1,0:T(8,128)(2,1)S(1)}, bf16[3,3,8,384]{3,2,1,0:T(8,128)(2,1)S(1)}, u32[]{:S(2)}, u32[]{:S(2)}) %collective-permute-start.17) | collective-permute-done | bytes 55328 | tf_op jit(solution)/shard_map/ppermute | solution.py:324
  93.0 7.2 %collective-permute-done.18.refs_4_ = bf16[3,3,8,384]{3,2,1,0:T(8,128)(2,1)S(1)} collective-permute-done((bf16[3,3,8,384]{3,2,1,0:T(8,128)(2,1)S(1)}, bf16[3,3,8,384]{3,2,1,0:T(8,128)(2,1)S(1)}, u32[]{:S(2)}, u32[]{:S(2)}) %collective-permute-start.18) | collective-permute-done | bytes 55328 | tf_op jit(solution)/shard_map/ppermute | solution.py:324
  100.2 2.5 %collective-permute-done.20.refs_8_ = bf16[4,296,384]{2,1,0:T(8,128)(2,1)S(1)} collective-permute-done((bf16[4,296,384]{2,1,0:T(8,128)(2,1)S(1)}, bf16[4,296,384]{2,1,0:T(8,128)(2,1)S(1)}, u32[]{:S(2)}, u32[]{:S(2)}) %collective-permute-start.20) | collective-permute-done | bytes 909344 | tf_op jit(solution)/shard_map/ppermute | solution.py:365
  102.6 3.7 %shard_map.164 = (bf16[6,6,8,384]{3,2,1,0:T(8,128)(2,1)}, f32[384]{0:T(512)}, bf16[384,1152]{1,0:T(8,128)(2,1)}, bf16[384,384]{1,0:T(8,128)(2,1)}, f32[384]{0:T(...) custom-call(s32[5]{0:T(128)S(1)} %stack.29.me.refs_0_, ...), custom_call_target="tpu_custom_call" | custom-call | flops 589824 | bytes 7627796 | tf_op jit(solution)/shard_map/pallas_call | solution.py:306
  (42 shorter events, 1.0 us)
Async XLA Ops:
  0.6 13.5 %copy-start.2 = (bf16[6,6,8,384]{3,2,1,0:T(8,128)(2,1)S(1)}, bf16[6,6,8,384]{3,2,1,0:T(8,128)(2,1)}, u32[]{:S(2)}) copy-start(bf16[6,6,8,384]{3,2,1,0:T(8,128)(2,1)} %tok.1) | copy-start | bytes 663556
  0.6 10.0 %copy-start.5 = (f32[384]{0:T(512)S(1)}, f32[384]{0:T(512)}, u32[]{:S(2)}) copy-start(f32[384]{0:T(512)} %param.13) | copy-start | bytes 4612
  0.7 10.1 %copy-start.4 = (f32[1536]{0:T(1024)S(1)}, f32[1536]{0:T(1024)}, u32[]{:S(2)}) copy-start(f32[1536]{0:T(1024)} %param.18) | copy-start | bytes 18436
  0.7 10.1 %copy-start.6 = (f32[384]{0:T(512)S(1)}, f32[384]{0:T(512)}, u32[]{:S(2)}) copy-start(f32[384]{0:T(512)} %param.16) | copy-start | bytes 4612
  0.7 13.5 %copy-start = (bf16[384,1152]{1,0:T(8,128)(2,1)S(1)}, bf16[384,1152]{1,0:T(8,128)(2,1)}, u32[]{:S(2)}) copy-start(bf16[384,1152]{1,0:T(8,128)(2,1)} %w_qkv.3) | copy-start | bytes 2654212
  1.8 9.1 %collective-permute-start = (bf16[2,3,3,8,384]{4,3,2,1,0:T(8,128)(2,1)S(1)}, bf16[2,3,3,8,384]{4,3,2,1,0:T(8,128)(2,1)S(1)}, u32[]{:S(2)}, u32[]{:S(2)}) collective-permute-start(bf16[2,3,3,8,384]{4,3,2,1,0:T(8,128)(2,1)S(1)} %get-tuple-element.88), channel_id=1, source_target_pairs={{0,3},{1,0},{2,1},{3,2},{4,7},{5,4},{6,5},{7,6},{8,11},{9,8},{10,9... | collective-permute-start | bytes 331784 | tf_op jit(solution)/shard_map/ppermute | solution.py:324
  4.2 7.9 %collective-permute-start.1 = (bf16[2,3,3,8,384]{4,3,2,1,0:T(8,128)(2,1)S(1)}, bf16[2,3,3,8,384]{4,3,2,1,0:T(8,128)(2,1)S(1)}, u32[]{:S(2)}, u32[]{:S(2)}) collective-permute-start(bf16[2,3,3,8,384]{4,3,2,1,0:T(8,128)(2,1)S(1)} %get-tuple-element.87), channel_id=1, source_target_pairs={{0,28},{1,29},{2,30},{3,31},{4,0},{5,1},{6,2},{7,3},{8,4},{9,5},{1... | collective-permute-start | bytes 331784 | tf_op jit(solution)/shard_map/ppermute | solution.py:324
  8.8 5.4 %collective-permute-start.2 = (bf16[2,3,3,8,384]{4,3,2,1,0:T(8,128)(2,1)S(1)}, bf16[2,3,3,8,384]{4,3,2,1,0:T(8,128)(2,1)S(1)}, u32[]{:S(2)}, u32[]{:S(2)}) collective-permute-start(bf16[2,3,3,8,384]{4,3,2,1,0:T(8,128)(2,1)S(1)} %get-tuple-element.86), channel_id=1, source_target_pairs={{0,31},{1,28},{2,29},{3,30},{4,3},{5,0},{6,1},{7,2},{8,7},{9,4},{1... | collective-permute-start | bytes 331784 | tf_op jit(solution)/shard_map/ppermute | solution.py:324
  10.8 17.5 %copy-start.1 = (bf16[384,384]{1,0:T(8,128)(2,1)S(1)}, bf16[384,384]{1,0:T(8,128)(2,1)}, u32[]{:S(2)}) copy-start(bf16[384,384]{1,0:T(8,128)(2,1)} %w_proj.1) | copy-start | bytes 884740
  14.1 0.9 copy-start.3
  28.3 4.1 %collective-permute-start.3 = (bf16[8,192,384]{2,1,0:T(8,128)(2,1)S(1)}, bf16[8,192,384]{2,1,0:T(8,128)(2,1)S(1)}, u32[]{:S(2)}, u32[]{:S(2)}) collective-permute-start(bf16[8,192,384]{2,1,0:T(8,128)(2,1)S(1)} %get-tuple-element.52), channel_id=1, source_target_pairs={{0,1},{1,0},{2,3},{3,2},{4,5},{5,4},{6,7},{7,6},{8,9},{9,8},{10,11... | collective-permute-start | bytes 3538952 | tf_op jit(solution)/shard_map/ppermute | solution.py:365
  36.5 2.3 %collective-permute-start.5 = (bf16[8,104,384]{2,1,0:T(8,128)(2,1)S(1)}, bf16[8,104,384]{2,1,0:T(8,128)(2,1)S(1)}, u32[]{:S(2)}, u32[]{:S(2)}) collective-permute-start(bf16[8,104,384]{2,1,0:T(8,128)(2,1)S(1)} %get-tuple-element.58), channel_id=1, source_target_pairs={{0,1},{1,0},{2,3},{3,2},{4,5},{5,4},{6,7},{7,6},{8,9},{9,8},{10,11... | collective-permute-start | bytes 1916936 | tf_op jit(solution)/shard_map/ppermute | solution.py:365
  37.0 9.9 %collective-permute-start.4 = (bf16[4,192,384]{2,1,0:T(8,128)(2,1)S(1)}, bf16[4,192,384]{2,1,0:T(8,128)(2,1)S(1)}, u32[]{:S(2)}, u32[]{:S(2)}) collective-permute-start(bf16[4,192,384]{2,1,0:T(8,128)(2,1)S(1)} %get-tuple-element.79), channel_id=1, source_target_pairs={{0,2},{1,9},{2,0},{3,11},{4,6},{5,13},{6,4},{7,15},{8,10},{9,1},{1... | collective-permute-start | bytes 1769480 | tf_op jit(solution)/shard_map/ppermute | solution.py:365
  38.9 9.9 %collective-permute-start.7 = (bf16[4,104,384]{2,1,0:T(8,128)(2,1)S(1)}, bf16[4,104,384]{2,1,0:T(8,128)(2,1)S(1)}, u32[]{:S(2)}, u32[]{:S(2)}) collective-permute-start(bf16[4,104,384]{2,1,0:T(8,128)(2,1)S(1)} %get-tuple-element.80), channel_id=1, source_target_pairs={{0,4},{1,5},{2,6},{3,7},{4,0},{5,1},{6,2},{7,3},{8,12},{9,13},{10,... | collective-permute-start | bytes 958472 | tf_op jit(solution)/shard_map/ppermute | solution.py:365
  47.0 6.8 %collective-permute-start.6 = (bf16[2,192,384]{2,1,0:T(8,128)(2,1)S(1)}, bf16[2,192,384]{2,1,0:T(8,128)(2,1)S(1)}, u32[]{:S(2)}, u32[]{:S(2)}) collective-permute-start(bf16[2,192,384]{2,1,0:T(8,128)(2,1)S(1)} %get-tuple-element.83), channel_id=1, source_target_pairs={{0,4},{1,3},{2,6},{3,1},{4,0},{5,7},{6,2},{7,5},{8,12},{9,11},{10,... | collective-permute-start | bytes 884744 | tf_op jit(solution)/shard_map/ppermute | solution.py:365
  48.8 5.6 %collective-permute-start.9 = (bf16[2,104,384]{2,1,0:T(8,128)(2,1)S(1)}, bf16[2,104,384]{2,1,0:T(8,128)(2,1)S(1)}, u32[]{:S(2)}, u32[]{:S(2)}) collective-permute-start(bf16[2,104,384]{2,1,0:T(8,128)(2,1)S(1)} %get-tuple-element.84), channel_id=1, source_target_pairs={{0,8},{1,9},{2,10},{3,11},{4,12},{5,13},{6,14},{7,15},{8,0},{9,1},... | collective-permute-start | bytes 479240 | tf_op jit(solution)/shard_map/ppermute | solution.py:365
  53.9 5.2 %collective-permute-start.8 = (bf16[1,192,384]{2,1,0:T(8,128)(2,1)S(1)}, bf16[1,192,384]{2,1,0:T(8,128)(2,1)S(1)}, u32[]{:S(2)}, u32[]{:S(2)}) collective-permute-start(bf16[1,192,384]{2,1,0:T(8,128)(2,1)S(1)} %add_convert_fusion.10), channel_id=1, source_target_pairs={{0,8},{1,5},{2,10},{3,7},{4,12},{5,1},{6,14},{7,3},{8,0},{9,13},{1... | collective-permute-start | bytes 442376 | tf_op jit(solution)/shard_map/ppermute | solution.py:365
  54.5 6.3 %collective-permute-start.11 = (bf16[1,104,384]{2,1,0:T(8,128)(2,1)S(1)}, bf16[1,104,384]{2,1,0:T(8,128)(2,1)S(1)}, u32[]{:S(2)}, u32[]{:S(2)}) collective-permute-start(bf16[1,104,384]{2,1,0:T(8,128)(2,1)S(1)} %add_convert_fusion.15), channel_id=1, source_target_pairs={{0,2},{1,3},{2,0},{3,1},{4,6},{5,7},{6,4},{7,5},{8,10},{9,11},{10,... | collective-permute-start | bytes 239624 | tf_op jit(solution)/shard_map/ppermute | solution.py:365
  59.1 9.7 %collective-permute-start.10 = (bf16[192,384]{1,0:T(8,128)(2,1)S(1)}, bf16[192,384]{1,0:T(8,128)(2,1)S(1)}, u32[]{:S(2)}, u32[]{:S(2)}) collective-permute-start(bf16[192,384]{1,0:T(8,128)(2,1)S(1)} %fusion), channel_id=1, source_target_pairs={{0,16},{1,17},{2,18},{3,19},{4,20},{5,21},{6,22},{7,23},{8,24},{9,... | collective-permute-start | bytes 442376 | tf_op jit(solution)/shard_map/ppermute | solution.py:365
  60.9 8.8 %collective-permute-start.12 = (bf16[104,384]{1,0:T(8,128)(2,1)S(1)}, bf16[104,384]{1,0:T(8,128)(2,1)S(1)}, u32[]{:S(2)}, u32[]{:S(2)}) collective-permute-start(bf16[104,384]{1,0:T(8,128)(2,1)S(1)} %fusion.1), channel_id=1, source_target_pairs={{0,16},{1,17},{2,18},{3,19},{4,20},{5,21},{6,22},{7,23},{8,24},{9,... | collective-permute-start | bytes 239624 | tf_op jit(solution)/shard_map/ppermute | solution.py:365
  69.7 6.1 %collective-permute-start.13 = (bf16[1,296,384]{2,1,0:T(8,128)(2,1)S(1)}, bf16[1,296,384]{2,1,0:T(8,128)(2,1)S(1)}, u32[]{:S(2)}, u32[]{:S(2)}) collective-permute-start(bf16[1,296,384]{2,1,0:T(8,128)(2,1)S(1)} %maximum_bitcast_fusion), channel_id=1, source_target_pairs={{0,8},{1,5},{2,10},{3,7},{4,12},{5,1},{6,14},{7,3},{8,0},{9,13},{1... | collective-permute-start | bytes 681992 | tf_op jit(solution)/shard_map/ppermute | solution.py:365
  75.9 8.5 %collective-permute-start.14 = (bf16[2,296,384]{2,1,0:T(8,128)(2,1)S(1)}, bf16[2,296,384]{2,1,0:T(8,128)(2,1)S(1)}, u32[]{:S(2)}, u32[]{:S(2)}) collective-permute-start(bf16[2,296,384]{2,1,0:T(8,128)(2,1)S(1)} %pad_maximum_fusion.1), channel_id=1, source_target_pairs={{0,4},{1,3},{2,6},{3,1},{4,0},{5,7},{6,2},{7,5},{8,12},{9,11},{10,... | collective-permute-start | bytes 1363976 | tf_op jit(solution)/shard_map/ppermute | solution.py:365
  84.5 15.7 %collective-permute-start.15 = (bf16[4,296,384]{2,1,0:T(8,128)(2,1)S(1)}, bf16[4,296,384]{2,1,0:T(8,128)(2,1)S(1)}, u32[]{:S(2)}, u32[]{:S(2)}) collective-permute-start(bf16[4,296,384]{2,1,0:T(8,128)(2,1)S(1)} %pad_maximum_fusion.refs_5_), channel_id=1, source_target_pairs={{0,2},{1,9},{2,0},{3,11},{4,6},{5,13},{6,4},{7,15},{8,10},{9,1},{1... | collective-permute-start | bytes 2727944 | tf_op jit(solution)/shard_map/ppermute | solution.py:365
  85.5 4.1 %collective-permute-start.16 = (bf16[3,3,8,384]{3,2,1,0:T(8,128)(2,1)S(1)}, bf16[3,3,8,384]{3,2,1,0:T(8,128)(2,1)S(1)}, u32[]{:S(2)}, u32[]{:S(2)}) collective-permute-start(bf16[3,3,8,384]{3,2,1,0:T(8,128)(2,1)S(1)} %get-tuple-element.71), channel_id=1, source_target_pairs={{0,1},{1,2},{2,3},{3,0},{4,5},{5,6},{6,7},{7,4},{8,9},{9,10},{10,1... | collective-permute-start | bytes 165896 | tf_op jit(solution)/shard_map/ppermute | solution.py:324
  85.5 7.5 %collective-permute-start.17 = (bf16[3,3,8,384]{3,2,1,0:T(8,128)(2,1)S(1)}, bf16[3,3,8,384]{3,2,1,0:T(8,128)(2,1)S(1)}, u32[]{:S(2)}, u32[]{:S(2)}) collective-permute-start(bf16[3,3,8,384]{3,2,1,0:T(8,128)(2,1)S(1)} %get-tuple-element.72), channel_id=1, source_target_pairs={{0,4},{1,5},{2,6},{3,7},{4,8},{5,9},{6,10},{7,11},{8,12},{9,13},{1... | collective-permute-start | bytes 165896 | tf_op jit(solution)/shard_map/ppermute | solution.py:324
  87.2 12.9 %collective-permute-start.18 = (bf16[3,3,8,384]{3,2,1,0:T(8,128)(2,1)S(1)}, bf16[3,3,8,384]{3,2,1,0:T(8,128)(2,1)S(1)}, u32[]{:S(2)}, u32[]{:S(2)}) collective-permute-start(bf16[3,3,8,384]{3,2,1,0:T(8,128)(2,1)S(1)} %get-tuple-element.73), channel_id=1, source_target_pairs={{0,5},{1,6},{2,7},{3,4},{4,9},{5,10},{6,11},{7,8},{8,13},{9,14},{1... | collective-permute-start | bytes 165896 | tf_op jit(solution)/shard_map/ppermute | solution.py:324
  88.1 12.1 %collective-permute-start.19 = (bf16[4,296,384]{2,1,0:T(8,128)(2,1)S(1)}, bf16[4,296,384]{2,1,0:T(8,128)(2,1)S(1)}, u32[]{:S(2)}, u32[]{:S(2)}) collective-permute-start(bf16[4,296,384]{2,1,0:T(8,128)(2,1)S(1)} %pad_maximum_fusion.refs_5_), channel_id=1, source_target_pairs={{0,1},{1,0},{2,3},{3,2},{4,5},{5,4},{6,7},{7,6},{8,9},{9,8},{10,11... | collective-permute-start | bytes 2727944 | tf_op jit(solution)/shard_map/ppermute | solution.py:365
  100.1 2.5 %collective-permute-start.20 = (bf16[4,296,384]{2,1,0:T(8,128)(2,1)S(1)}, bf16[4,296,384]{2,1,0:T(8,128)(2,1)S(1)}, u32[]{:S(2)}, u32[]{:S(2)}) collective-permute-start(bf16[4,296,384]{2,1,0:T(8,128)(2,1)S(1)} %collective-permute-done.15.refs_6_), channel_id=1, source_target_pairs={{0,1},{1,0},{2,3},{3,2},{4,5},{5,4},{6,7},{7,6},{8,9},{9,8},{10,11... | collective-permute-start | bytes 2727944 | tf_op jit(solution)/shard_map/ppermute | solution.py:365

commit v3 on v2

--- a/solution.py
+++ b/solution.py
@@ -66,11 +66,10 @@
     return (piece % half) ^ me[1 + 2 * order + piece // half]
 
 
-def put_block(stage, block, value, me, order, top=0):
-    pieces = PIECES // BLOCKS
+def put_block(stage, value, me, order, top, first=0, pieces=PIECES):
     rows = value.shape[0] // pieces
     for i in range(pieces):
-        piece = block * pieces + i
+        piece = first + i
         core = piece // (PIECES // 2)
         slot = (core ^ me[0]) * (PIECES // 2) + low_slot(piece, me, order)
         stage[slot, top : top + rows] = value[i * rows : (i + 1) * rows]
@@ -88,26 +87,39 @@
     return jnp.concatenate([r.astype(F32).reshape(-1, r.shape[-1]) for r in rows], axis=0)
 
 
+def fetch_kernel(*refs):
+    count = (len(refs) - 2) // 2
+    copies = [
+        pltpu.make_async_copy(refs[1 + i], refs[1 + count + i], refs[-1].at[i]) for i in range(count)
+    ]
+    for copy in copies:
+        copy.start()
+    for copy in copies:
+        copy.wait()
+
+
 def forward_kernel(
     me, tok, up_own, part_b, part_c, part_d, code_col, code_row,
-    gain1, gain2, b_fc1, w_qkv, w_proj_far, w_fc1_far, w_fc2_far,
+    gain1, gain2, b_fc1, w_qkv, w_proj, w_fc1_far, w_fc2_far,
     keep, send, small, grad_mid, normed1, inv1, qkv, probs, mix,
-    allowed, stage, w_proj, w_fc1, w_fc2, sems,
+    allowed, stage, pre_all, up_hidden, hidden_all, grad_pre, w_fc1, w_fc2, sems,
 ):
-    far = (w_proj_far, w_fc2_far, w_fc1_far)
-    near = (w_proj, w_fc2, w_fc1)
-    fetch = [pltpu.make_async_copy(a, b, sems.at[i]) for i, (a, b) in enumerate(zip(far, near))]
+    fetch = [
+        pltpu.make_async_copy(w_fc1_far, w_fc1, sems.at[0]),
+        pltpu.make_async_copy(w_fc2_far, w_fc2, sems.at[1]),
+    ]
     for copy in fetch:
         copy.start()
     width = w_proj.shape[0]
     heads = width // HD
-    piece = stage.shape[1] // 2
+    each = PIECES // BLOCKS
+    piece = each * width * BLOCKS // (PIECES * each)
     parts = (part_b, part_c, part_d)
     x = load_window(tok, parts, 0)
     normed, inv = row_stats(x)
     normed1[...] = normed
     inv1[...] = inv
-    h1 = (normed * gain1[...]).astype(BF16)
+    h1 = (normed * gain1[...][None, :]).astype(BF16)
     qkv[...] = dot(h1, w_qkv[...]).astype(BF16)
     allowed[...] = (code_col[...] == code_row[...]).astype(F32)
 
@@ -128,30 +140,44 @@
     mix_low = mix[...].astype(BF16)
     mid = (x + dot(mix_low, w_proj[...])).astype(BF16).astype(F32)
     normed2, inv2 = row_stats(mid)
-    h2 = (normed2 * gain2[...]).astype(BF16)
+    h2 = (normed2 * gain2[...][None, :]).astype(BF16)
     up = load_window(up_own, parts, 1)
     up_low = up.astype(BF16)
 
-    t2 = None
+    pre_all[...] = dot(h2, w_fc1[...])
+    up_hidden[...] = dot_last(up_low, w_fc2[...])
+    count = pre_all.shape[0]
+    chunk = 32
+    bias = b_fc1[...][None, :]
+    total = None
+    for i in range(count // chunk):
+        at = slice(i * chunk, (i + 1) * chunk)
+        pre = pre_all[at, :] + bias
+        square = pre * pre
+        tanh_value = jnp.tanh(pre * (ROOT_TWO_PI + (ROOT_TWO_PI * CUBIC) * square))
+        half = 0.5 + 0.5 * tanh_value
+        hidden_all[at, :] = (pre * half).astype(BF16)
+        slope = half + pre * (1.0 - tanh_value * tanh_value) * (
+            0.5 * ROOT_TWO_PI + (1.5 * ROOT_TWO_PI * CUBIC) * square
+        )
+        gp = (up_hidden[at, :] * slope).astype(BF16)
+        grad_pre[at, :] = gp
+        part = jnp.sum(gp.astype(F32).reshape(chunk // 8, 8, -1), axis=0)
+        total = part if total is None else total + part
+    total = jnp.sum(total, axis=0, keepdims=True)
     for j in range(BLOCKS):
-        cols = slice(j * width, (j + 1) * width)
-        pre = dot(h2, w_fc1[:, cols]) + b_fc1[:, cols]
-        square = pre * pre
-        tanh_value = jnp.tanh(ROOT_TWO_PI * pre * (1.0 + CUBIC * square))
-        half = 0.5 * (1.0 + tanh_value)
-        hidden = (pre * half).astype(BF16)
-        slope = half + 0.5 * pre * (1.0 - tanh_value * tanh_value) * (
-            ROOT_TWO_PI * (1.0 + 3.0 * CUBIC * square)
-        )
-        put_block(stage, j, dot_first(hidden, up_low).astype(BF16), me, 0)
-        gp = (dot_last(up_low, w_fc2[cols, :]) * slope).astype(BF16)
-        small[1 + j : 2 + j, :] = jnp.sum(gp.astype(F32), axis=0, keepdims=True)
-        put_block(stage, j, dot_first(h2, gp).astype(BF16), me, 0, piece)
-        part = dot_last(gp, w_fc1[:, cols])
-        t2 = part if t2 is None else t2 + part
-    back2, s_ln2 = norm_back(t2, normed2, inv2, gain2[...])
+        small[1 + j : 2 + j, :] = total[:, j * width : (j + 1) * width]
+    put_block(stage, dot_first(hidden_all[...], up_low).astype(BF16), me, 0, 0)
+    t2 = dot_last(grad_pre[...], w_fc1[...])
+    grad = dot_first(h2, grad_pre[...]).astype(BF16)
+    for j in range(BLOCKS):
+        put_block(stage, grad[:, j * width : (j + 1) * width], me, 0, piece, j * each, each)
+    back2, s_ln2 = norm_back(t2, normed2, inv2, gain2[...][None, :])
     small[0:1, :] = s_ln2
-    grad_mid[...] = up + back2
+    grad_res = up + back2
+    grad_mid[...] = grad_res
+    grad_proj = dot_first(mix_low, grad_res.astype(BF16)).astype(BF16)
+    put_block(stage, grad_proj, me, 0, 2 * piece)
     hand_out(stage, keep, send)
 
 
@@ -190,22 +216,18 @@
     extra = [me[0] * (PIECES // 2) + low_slot(i, me, 1) for i in range(BLOCKS + 2)]
     for i in range(BLOCKS + 1):
         stage_t[extra[i + 1], rows - EXTRA : rows - EXTRA + 1] = small[i : i + 1, :].astype(BF16)
-    grad_attn = grad_mid[...].astype(BF16)
-    put_block(stage_t, 3, dot_first(mix[...].astype(BF16), grad_attn).astype(BF16), me, 1)
     heads_back(range(EARLY, width // LANES), qkv, probs, mix, dmix, dqkv)
     normed = normed1[...]
-    h1 = (normed * gain1[...]).astype(BF16)
-    t1 = None
+    h1 = (normed * gain1[...][None, :]).astype(BF16)
     early = EARLY * LANES
     for j in range(3):
         lo = j * width
-        own = jnp.concatenate(
-            [dqkv_early[:, lo : lo + early], dqkv[:, lo + early : lo + width]], axis=1
-        )
-        put_block(stage_t, j, dot_first(h1, own).astype(BF16), me, 1)
-        part = dot_last(own, w_qkv[:, lo : lo + width])
-        t1 = part if t1 is None else t1 + part
-    back1, s_ln1 = norm_back(t1, normed, inv1[...], gain1[...])
+        dqkv[:, lo : lo + early] = dqkv_early[:, lo : lo + early]
+    grad = dot_first(h1, dqkv[...]).astype(BF16)
+    for j in range(3):
+        put_block(stage_t, grad[:, j * width : (j + 1) * width], me, 1, j * width // PIECES)
+    t1 = dot_last(dqkv[...], w_qkv[...])
+    back1, s_ln1 = norm_back(t1, normed, inv1[...], gain1[...][None, :])
     stage_t[extra[0], rows - EXTRA : rows - EXTRA + 1] = s_ln1.astype(BF16)
     hand_out(stage_t, keep_t, send_t)
     result = grad_mid[...] + back1
@@ -216,12 +238,13 @@
 
 def finish_kernel(*refs):
     me, back_a, back_b, back_c, back_d = refs[:5]
-    parts = refs[5:-14]
-    out, g_ln1, g_qkv, g_proj, g_ln2, g_fc1, g_bfc1, g_fc2 = refs[-14:-6]
-    out_near, fc1, fc2, both, smalls, sems = refs[-6:]
+    parts = refs[5:-15]
+    out, g_ln1, g_qkv, g_proj, g_ln2, g_fc1, g_bfc1, g_fc2 = refs[-15:-7]
+    out_near, fc1, fc2, qkv, proj, smalls, sems = refs[-7:]
     half = PIECES // 2
     width, ff = fc1.shape
     rows = width * BLOCKS // PIECES
+    thin = width // PIECES
     half_x, half_y = out_near.shape[0] // 2, out_near.shape[1] // 2
     copies = []
 
@@ -242,8 +265,6 @@
     total = jnp.sum(jnp.sum(total, axis=0, keepdims=True), axis=1, keepdims=True)
     factor = math.sqrt(param_count(width, ff)) * lax.rsqrt(total)
     per_block = PIECES // BLOCKS
-    slots_t = [arrivals(ORDERS[1], core) for core in range(2)]
-
     def spot(core, order, slot):
         piece = core * half + (slot ^ jnp.where(core == 0, me[1 + 2 * order], me[2 + 2 * order]))
         top = pl.multiple_of(piece % per_block * rows, rows)
@@ -251,27 +272,29 @@
         return piece, pl.ds(top, rows), pl.ds(left, width)
 
     for kind in range(2):
-        for i, ref in enumerate(parts):
+        for i, ref in enumerate(parts[4 * kind : 4 * kind + 4]):
             core = me[0] ^ (i // 2)
             for j in range(ref.shape[0]):
                 slot = i % 2 * ref.shape[0] + j
                 if kind == 0:
-                    value = ref[j, : 2 * rows].astype(F32) * factor
+                    value = (ref[j].astype(F32) * factor).astype(BF16)
                     piece, down, across = spot(core, 0, slot)
-                    fc2[pl.ds(pl.multiple_of(piece * rows, rows), rows), :] = value[:rows].astype(BF16)
-                    fc1[down, across] = value[rows:].astype(BF16)
+                    fc2[pl.ds(pl.multiple_of(piece * rows, rows), rows), :] = value[:rows]
+                    fc1[down, across] = value[rows : 2 * rows]
+                    proj[piece] = value[2 * rows :]
                 else:
-                    value = ref[j, 2 * rows :].astype(F32) * factor
-                    slot_t = jnp.where(core == 0, slots_t[0][slot], slots_t[1][slot])
-                    piece, down, across = spot(core, 1, slot_t)
-                    both[down, across] = value[:rows].astype(BF16)
-                    smalls[piece] = value[rows:]
+                    value = ref[j].astype(F32) * factor
+                    piece, down, across = spot(core, 1, slot)
+                    for part in range(3):
+                        at = slice(part * width, (part + 1) * width)
+                        qkv[piece, :, at] = value[part * thin : (part + 1) * thin].astype(BF16)
+                    smalls[piece] = value[3 * thin :]
         if kind == 0:
             leave(fc2, g_fc2)
             leave(fc1, g_fc1)
+            leave(proj, g_proj)
         else:
-            leave(both.at[:, : 3 * width], g_qkv)
-            leave(both.at[:, 3 * width :], g_proj)
+            leave(qkv, g_qkv)
     g_ln1[...] = smalls[0, 0]
     g_ln2[...] = smalls[1, 0]
     for j in range(BLOCKS):
@@ -379,14 +402,6 @@
     ((SIDE, LAYER), (NEAR, SIDE), (LAYER, NEAR)),
     ((NEAR, NEAR), (LAYER, LAYER), (SIDE, SIDE)),
 )
-
-
-def arrivals(order, core):
-    slots = [0]
-    for flips in reversed(ORDERS[0]):
-        bit = 2 - [step[core] for step in order].index(flips[core])
-        slots = slots + [slot | 1 << bit for slot in slots]
-    return slots
 
 
 def place():
@@ -443,14 +458,18 @@
         got, got_t = swap(low, flips), swap(low_t, flips)
         low = add(low, after([got], low_t)[0]).astype(BF16)
         low_t = add(low_t, after([got_t], low)[0]).astype(BF16)
-    own = jnp.concatenate([low, low_t])[None]
-    two = jnp.concatenate([own, swap(own, order[2])])
-    four = jnp.concatenate([two, swap(two, order[1])])
-    side = swap(four, order[0])
-    away = after(away, four)
-    back = [neighbour(away[0], 0, 1), neighbour(away[1], 1, 0), neighbour(away[2], 1, 1)]
-    side, *back = after([side, *back], four)
-    return back, [four, side, swap(four, CORE), swap(side, CORE)]
+    parts, parts_t = low[None], low_t[None]
+    for step in (2, 1, 0):
+        more, more_t = swap(parts, order[step]), swap(parts_t, order_t[step])
+        if step == 0:
+            away = after(away, parts)
+            back = [neighbour(away[0], 0, 1), neighbour(away[1], 1, 0), neighbour(away[2], 1, 1)]
+            more, more_t, *back = lax.optimization_barrier((more, more_t, *back))
+            break
+        more, more_t = lax.optimization_barrier((more, more_t))
+        parts, parts_t = jnp.concatenate([parts, more]), jnp.concatenate([parts_t, more_t])
+    streams = ((parts, more), (parts_t, more_t))
+    return back, [part for pair in streams for part in (*pair, swap(pair[0], CORE), swap(pair[1], CORE))]
 
 
 def body(tokens, upstream, window_labels, ln1_gain, w_qkv, w_proj, ln2_gain, w_fc1, b_fc1, w_fc2):
@@ -461,21 +480,28 @@
     rows = codes.shape[0]
     me = place()
     piece = BLOCKS * width // PIECES
-    half = shape((PIECES // 2, 2 * piece, width), BF16)
-    half_t = shape((PIECES // 2, piece + EXTRA, width), BF16)
-    gain1 = ln1_gain[None, :]
+    thin = width // PIECES
+    rows_f, rows_t = 2 * piece + thin, 3 * thin + EXTRA
+    half = shape((PIECES // 2, rows_f, width), BF16)
+    half_t = shape((PIECES // 2, rows_t, width), BF16)
+    weights = (w_qkv, w_proj)
+    weights = call(
+        fetch_kernel, tuple(shape(w.shape, BF16) for w in weights), [pltpu.SemaphoreType.DMA((2,))], 0, me, (), weights
+    )
+    w_qkv, w_proj = weights
+    parts = after(parts, w_proj)
     keep, send, *saved = call(
         forward_kernel,
         (half, half)
         + (shape((1 + BLOCKS, width), F32), shape((rows, width), F32), shape((rows, width), F32), shape((rows, 1), F32))
         + (shape((rows, 3 * width), BF16), shape((heads, rows, rows), BF16), shape((rows, width), F32)),
-        [pltpu.VMEM((rows, rows), F32), pltpu.VMEM((PIECES, 2 * piece, width), BF16)]
-        + like(w_proj, w_fc1, w_fc2)
-        + [pltpu.SemaphoreType.DMA((3,))],
+        [pltpu.VMEM((rows, rows), F32), pltpu.VMEM((PIECES, rows_f, width), BF16), pltpu.VMEM((rows, ff), F32), pltpu.VMEM((rows, ff), F32), pltpu.VMEM((rows, ff), BF16), pltpu.VMEM((rows, ff), BF16)]
+        + like(w_fc1, w_fc2)
+        + [pltpu.SemaphoreType.DMA((2,))],
         2 * rows * width * (4 * width + 5 * ff) + 4 * heads * rows * rows * LANES,
         me,
-        (tokens, upstream, *parts, codes[:, None], codes[None, :], gain1, ln2_gain[None, :], b_fc1[None, :], w_qkv),
-        (w_proj, w_fc1, w_fc2),
+        (tokens, upstream, *parts, codes[:, None], codes[None, :], ln1_gain, ln2_gain, b_fc1, w_qkv, w_proj),
+        (w_fc1, w_fc2),
     )
     quarter = shape(parts[0].shape[1:], BF16)
     small, grad_mid, normed1, inv1, qkv, probs, mix = saved
@@ -495,22 +521,23 @@
     *done, keep_t, send_t = call(
         second_back_kernel,
         (quarter,) * 4 + (half_t, half_t),
-        [pltpu.VMEM((rows, 3 * width), BF16), pltpu.VMEM((PIECES, piece + EXTRA, width), BF16)],
+        [pltpu.VMEM((rows, 3 * width), BF16), pltpu.VMEM((PIECES, rows_t, width), BF16)],
         2 * rows * width * 7 * width + 8 * (heads - EARLY * (LANES // HD)) * rows * rows * LANES,
         me,
-        (small, grad_mid, normed1, inv1, qkv, probs, mix, dmix, dqkv, gain1, w_qkv),
+        (small, grad_mid, normed1, inv1, qkv, probs, mix, dmix, dqkv, ln1_gain, w_qkv),
     )
     back, slots = reduce_all(keep, send, got, keep_t, send_t, done[1:])
     result, g_ln1, g_qkv, g_proj, g_ln2, g_fc1, g_bfc1, g_fc2 = call(
         finish_kernel,
         (
-            shape(tokens.shape, BF16), shape((width,), F32), shape((width, 3 * width), BF16),
-            shape((width, width), BF16), shape((width,), F32), shape((width, ff), BF16),
+            shape(tokens.shape, BF16), shape((width,), F32), shape((PIECES, thin, 3 * width), BF16),
+            shape((PIECES, thin, width), BF16), shape((width,), F32), shape((width, ff), BF16),
             shape((ff,), F32), shape((ff, width), BF16),
         ),
         like(tokens, w_fc1, w_fc2)
         + [
-            pltpu.VMEM((width, 4 * width), BF16),
+            pltpu.VMEM((PIECES, thin, 3 * width), BF16),
+            pltpu.VMEM((PIECES, thin, width), BF16),
             pltpu.VMEM((PIECES, EXTRA, width), F32),
             pltpu.SemaphoreType.DMA((5,)),
         ],
@@ -519,6 +546,7 @@
         (done[0], *back, *slots),
         out_specs=(HBM, VMEM, HBM, HBM, VMEM, HBM, VMEM, HBM),
     )
+    g_qkv, g_proj = g_qkv.reshape(width, 3 * width), g_proj.reshape(width, width)
     return (result, g_ln1, g_qkv, g_proj, g_ln2, g_fc1, g_bfc1, g_fc2)
 
 

time: 107 us -> 100 us (0.935)
  waiting for transfers between devices: 57.4 us -> 46.2 us
  starting transfers between devices: 18.6 us -> 24.1 us
    ppermute x6, waiting for transfers between devices: 15.3 us -> 7.89 us  [neighbour(): return lax.ppermute(shard, ('gx', 'gy'), pairs)]
    ppermute x15 -> x20, starting transfers between devices: 8.65 us -> 13.5 us  [swap(): return lax.ppermute(shard, ('gx', 'gy'), pairs)]
    ppermute x15 -> x20, waiting for transfers between devices: 42.1 us -> 38.3 us  [swap(): return lax.ppermute(shard, ('gx', 'gy'), pairs)]
    pallas_call x4 -> x5, Pallas kernels: 24.7 us -> 24.7 us  [call(): pl.pallas_call(kernel, out_shape=outs, in_specs=[SMEM] + [VMEM] * len(nea...]
  transfers between devices with their start and end apart: 21 -> 26, of which waited for: 16 -> 16; matrix products, arithmetic and copies ran while one was open for 2% -> 2% of each run, Pallas kernels for 4% -> 6%
where the time goes in v3:
time: 100 us; the launch traced here: 99.9 us
  waiting for transfers between devices  46.2 us (46%)
  Pallas kernels  24.7 us (25%)
  starting transfers between devices  24.1 us (24%)
  other arithmetic  3.19 us (3%)
  between operations  1.08 us (1%)
    ppermute x20, waiting for transfers between devices, swap(): return lax.ppermute(shard, ('gx', 'gy'), pairs)  38.3 us
    pallas_call x5, Pallas kernels, call(): pl.pallas_call(kernel, out_shape=outs, in_specs=[SMEM] + [VMEM] * len(nea...  24.7 us
    ppermute x20, starting transfers between devices, swap(): return lax.ppermute(shard, ('gx', 'gy'), pairs)  13.5 us
    ppermute x6, starting transfers between devices, neighbour(): return lax.ppermute(shard, ('gx', 'gy'), pairs)  10.6 us
    ppermute x6, waiting for transfers between devices, neighbour(): return lax.ppermute(shard, ('gx', 'gy'), pairs)  7.89 us
  transfers between devices with their start and end apart: 26, of which 16 were waited for; matrix products, arithmetic and copies ran while one was open for 2% of the time, Pallas kernels for 6%

profile of v3, /device:TPU:0, one launch (start us, length us, event | category | flops | bytes accessed | tf_op | source)
XLA Modules:
  0.0 99.9 jit_solution(17956125651521522046)
XLA Ops:
  0.7 1.1 %pad_maximum_fusion.4 = (bf16[2,3,3,8,384]{4,3,2,1,0:T(8,128)(2,1)S(1)}, bf16[2,3,3,8,384]{4,3,2,1,0:T(8,128)(2,1)S(1)}, bf16[2,3,3,8,384]{4,3,2,1,0:T(8,128)(2,1)S(1)}) fusion(bf16[1,6,6,8,384]{4,3,2,1,0:T(8,128)(2,1)} %bitcast.16, bf16[1,6,6,8,384]{4,3,2,1,0:T(8,128)(2,1)} %bitcast.15), kind=kLoop, calls=%fused_computation.21 | loop fusion | flops 165888 | bytes 774144 | tf_op jit(solution)/shard_map/stack | solution.py:478
  1.8 2.4 %collective-permute-start = (bf16[2,3,3,8,384]{4,3,2,1,0:T(8,128)(2,1)S(1)}, bf16[2,3,3,8,384]{4,3,2,1,0:T(8,128)(2,1)S(1)}, u32[]{:S(2)}, u32[]{:S(2)}) collective-permute-start(bf16[2,3,3,8,384]{4,3,2,1,0:T(8,128)(2,1)S(1)} %get-tuple-element.124), channel_id=1, source_target_pairs={{0,3},{1,0},{2,1},{3,2},{4,7},{5,4},{6,5},{7,6},{8,11},{9,8},{10,9... | collective-permute-start | bytes 331784 | tf_op jit(solution)/shard_map/ppermute | solution.py:347
  4.2 4.6 %collective-permute-start.1 = (bf16[2,3,3,8,384]{4,3,2,1,0:T(8,128)(2,1)S(1)}, bf16[2,3,3,8,384]{4,3,2,1,0:T(8,128)(2,1)S(1)}, u32[]{:S(2)}, u32[]{:S(2)}) collective-permute-start(bf16[2,3,3,8,384]{4,3,2,1,0:T(8,128)(2,1)S(1)} %get-tuple-element.123), channel_id=1, source_target_pairs={{0,28},{1,29},{2,30},{3,31},{4,0},{5,1},{6,2},{7,3},{8,4},{9,5},{1... | collective-permute-start | bytes 331784 | tf_op jit(solution)/shard_map/ppermute | solution.py:347
  8.8 0.3 collective-permute-start.2
  9.1 0.8 add_add_fusion
  10.2 0.1 reshape.61
  10.3 0.1 reshape.62
  10.5 0.1 broadcast_in_dim.19.code_col
  10.7 1.8 %shard_map.161 = (bf16[384,1152]{1,0:T(8,128)(2,1)S(1)}, bf16[384,384]{1,0:T(8,128)(2,1)S(1)}) custom-call(s32[5]{0:T(128)S(1)} %stack.29.refs_0_.me, bf16[384,1152]{1,0:T(8,128)(2,1)} %refs_1_.1, bf16[384,384]{1,0:T(8,128)(2,1)} %refs_2_.1), custom_call_target="tpu_custom_call" | custom-call | bytes 2359316 | tf_op jit(solution)/shard_map/pallas_call | solution.py:329
  12.6 1.6 %collective-permute-done.2.part_d = bf16[2,3,3,8,384]{4,3,2,1,0:T(8,128)(2,1)S(1)} collective-permute-done((bf16[2,3,3,8,384]{4,3,2,1,0:T(8,128)(2,1)S(1)}, bf16[2,3,3,8,384]{4,3,2,1,0:T(8,128)(2,1)S(1)}, u32[]{:S(2)}, u32[]{:S(2)}) %collective-permute-start.2) | collective-permute-done | bytes 110624 | tf_op jit(solution)/shard_map/ppermute | solution.py:347
  14.1 11.7 %shard_map.162 = (bf16[8,216,384]{2,1,0:T(8,128)(2,1)S(1)}, bf16[8,216,384]{2,1,0:T(8,128)(2,1)S(1)}, f32[5,384]{1,0:T(8,128)S(1)}, f32[288,384]{1,0:T(8,128)S(1...) custom-call(s32[5]{0:T(128)S(1)} %stack.29.refs_0_.me, ...), custom_call_target="tpu_custom_call" | custom-call | flops 2548039680 | bytes 10968980 | tf_op jit(solution)/shard_map/pallas_call | solution.py:329
  25.9 3.9 %shard_map.163 = (bf16[288,384]{1,0:T(8,128)(2,1)S(1)}, bf16[288,1152]{1,0:T(8,128)(2,1)S(1)}) custom-call(s32[5]{0:T(128)S(1)} %stack.29.refs_0_.me, f32[288,384]{1,0:T(8,128)S(1)} %get-tuple-element.67.grad_mid, bf16[288,1152]{1,0:T(8,128)(2,1)S(1)} %get-tuple-element.70.qkv, bf16[12,288,288]{2,1,0:T(8,128)(2,1)S(1)} %get-tuple-element.71.probs, ...), custom_call_target="tpu_custom_call" | custom-call | flops 764411904 | bytes 4718612 | tf_op jit(solution)/shard_map/pallas_call | solution.py:329
  29.8 0.4 add_convert_fusion
  30.2 3.5 %shard_map.164 = (bf16[3,3,8,384]{3,2,1,0:T(8,128)(2,1)S(1)}, bf16[3,3,8,384]{3,2,1,0:T(8,128)(2,1)S(1)}, bf16[3,3,8,384]{3,2,1,0:T(8,128)(2,1)S(1)}, bf16[3,3,8...) custom-call(s32[5]{0:T(128)S(1)} %stack.29.refs_0_.me, ...), custom_call_target="tpu_custom_call" | custom-call | flops 934281216 | bytes 6965396 | tf_op jit(solution)/shard_map/pallas_call | solution.py:329
  33.7 0.6 collective-permute-start.5
  34.3 0.6 collective-permute-start.4
  34.8 0.9 collective-permute-done.5
  35.7 0.1 add_convert_fusion.4
  35.9 0.2 collective-permute-start.7
  36.1 8.8 %collective-permute-done.4 = bf16[4,216,384]{2,1,0:T(8,128)(2,1)S(1)} collective-permute-done((bf16[4,216,384]{2,1,0:T(8,128)(2,1)S(1)}, bf16[4,216,384]{2,1,0:T(8,128)(2,1)S(1)}, u32[]{:S(2)}, u32[]{:S(2)}) %collective-permute-start.4) | collective-permute-done | bytes 663584 | tf_op jit(solution)/shard_map/ppermute | solution.py:388
  44.9 0.2 add_convert_fusion.2
  45.3 1.3 %collective-permute-start.9 = (bf16[2,80,384]{2,1,0:T(8,128)(2,1)S(1)}, bf16[2,80,384]{2,1,0:T(8,128)(2,1)S(1)}, u32[]{:S(2)}, u32[]{:S(2)}) collective-permute-start(bf16[2,80,384]{2,1,0:T(8,128)(2,1)S(1)} %get-tuple-element.121), channel_id=1, source_target_pairs={{0,8},{1,9},{2,10},{3,11},{4,12},{5,13},{6,14},{7,15},{8,0},{9,1},... | collective-permute-start | bytes 368648 | tf_op jit(solution)/shard_map/ppermute | solution.py:388
  46.6 5.7 %collective-permute-done.6 = bf16[2,216,384]{2,1,0:T(8,128)(2,1)S(1)} collective-permute-done((bf16[2,216,384]{2,1,0:T(8,128)(2,1)S(1)}, bf16[2,216,384]{2,1,0:T(8,128)(2,1)S(1)}, u32[]{:S(2)}, u32[]{:S(2)}) %collective-permute-start.6) | collective-permute-done | bytes 331808 | tf_op jit(solution)/shard_map/ppermute | solution.py:388
  52.5 0.6 collective-permute-start.11
  53.1 4.7 %collective-permute-done.8 = bf16[1,216,384]{2,1,0:T(8,128)(2,1)S(1)} collective-permute-done((bf16[1,216,384]{2,1,0:T(8,128)(2,1)S(1)}, bf16[1,216,384]{2,1,0:T(8,128)(2,1)S(1)}, u32[]{:S(2)}, u32[]{:S(2)}) %collective-permute-start.8) | collective-permute-done | bytes 165920 | tf_op jit(solution)/shard_map/ppermute | solution.py:388
  57.8 1.7 %collective-permute-start.10 = (bf16[216,384]{1,0:T(8,128)(2,1)S(1)}, bf16[216,384]{1,0:T(8,128)(2,1)S(1)}, u32[]{:S(2)}, u32[]{:S(2)}) collective-permute-start(bf16[216,384]{1,0:T(8,128)(2,1)S(1)} %fusion), channel_id=1, source_target_pairs={{0,16},{1,17},{2,18},{3,19},{4,20},{5,21},{6,22},{7,23},{8,24},{9,... | collective-permute-start | bytes 497672 | tf_op jit(solution)/shard_map/ppermute | solution.py:388
  59.6 1.3 %collective-permute-start.13 = (bf16[80,384]{1,0:T(8,128)(2,1)S(1)}, bf16[80,384]{1,0:T(8,128)(2,1)S(1)}, u32[]{:S(2)}, u32[]{:S(2)}) collective-permute-start(bf16[80,384]{1,0:T(8,128)(2,1)S(1)} %fusion.1), channel_id=1, source_target_pairs={{0,16},{1,17},{2,18},{3,19},{4,20},{5,21},{6,22},{7,23},{8,24},{9,... | collective-permute-start | bytes 184328 | tf_op jit(solution)/shard_map/ppermute | solution.py:388
  60.9 6.8 %collective-permute-done.10 = bf16[216,384]{1,0:T(8,128)(2,1)S(1)} collective-permute-done((bf16[216,384]{1,0:T(8,128)(2,1)S(1)}, bf16[216,384]{1,0:T(8,128)(2,1)S(1)}, u32[]{:S(2)}, u32[]{:S(2)}) %collective-permute-start.10) | collective-permute-done | bytes 165920 | tf_op jit(solution)/shard_map/ppermute | solution.py:388
  67.7 0.6 collective-permute-done.13
  68.3 0.3 collective-permute-start.12
  68.7 1.0 %collective-permute-start.14 = (bf16[1,80,384]{2,1,0:T(8,128)(2,1)S(1)}, bf16[1,80,384]{2,1,0:T(8,128)(2,1)S(1)}, u32[]{:S(2)}, u32[]{:S(2)}) collective-permute-start(bf16[1,80,384]{2,1,0:T(8,128)(2,1)S(1)} %fusion.2), channel_id=1, source_target_pairs={{0,2},{1,3},{2,0},{3,1},{4,6},{5,7},{6,4},{7,5},{8,10},{9,11},{10,... | collective-permute-start | bytes 184328 | tf_op jit(solution)/shard_map/ppermute | solution.py:388
  69.8 3.2 %collective-permute-done.14 = bf16[1,80,384]{2,1,0:T(8,128)(2,1)S(1)} collective-permute-done((bf16[1,80,384]{2,1,0:T(8,128)(2,1)S(1)}, bf16[1,80,384]{2,1,0:T(8,128)(2,1)S(1)}, u32[]{:S(2)}, u32[]{:S(2)}) %collective-permute-start.14) | collective-permute-done | bytes 61472 | tf_op jit(solution)/shard_map/ppermute | solution.py:388
  73.0 0.7 collective-permute-done.12
  73.7 1.4 %collective-permute-start.15 = (bf16[2,216,384]{2,1,0:T(8,128)(2,1)S(1)}, bf16[2,216,384]{2,1,0:T(8,128)(2,1)S(1)}, u32[]{:S(2)}, u32[]{:S(2)}) collective-permute-start(bf16[2,216,384]{2,1,0:T(8,128)(2,1)S(1)} %pad_maximum_fusion.1), channel_id=1, source_target_pairs={{0,4},{1,3},{2,6},{3,1},{4,0},{5,7},{6,2},{7,5},{8,12},{9,11},{10,... | collective-permute-start | bytes 995336 | tf_op jit(solution)/shard_map/ppermute | solution.py:388
  75.2 1.1 %collective-permute-start.16 = (bf16[2,80,384]{2,1,0:T(8,128)(2,1)S(1)}, bf16[2,80,384]{2,1,0:T(8,128)(2,1)S(1)}, u32[]{:S(2)}, u32[]{:S(2)}) collective-permute-start(bf16[2,80,384]{2,1,0:T(8,128)(2,1)S(1)} %pad_maximum_fusion.3), channel_id=1, source_target_pairs={{0,8},{1,9},{2,10},{3,11},{4,12},{5,13},{6,14},{7,15},{8,0},{9,1},... | collective-permute-start | bytes 368648 | tf_op jit(solution)/shard_map/ppermute | solution.py:388
  76.2 4.1 %collective-permute-done.16 = bf16[2,80,384]{2,1,0:T(8,128)(2,1)S(1)} collective-permute-done((bf16[2,80,384]{2,1,0:T(8,128)(2,1)S(1)}, bf16[2,80,384]{2,1,0:T(8,128)(2,1)S(1)}, u32[]{:S(2)}, u32[]{:S(2)}) %collective-permute-start.16) | collective-permute-done | bytes 122912 | tf_op jit(solution)/shard_map/ppermute | solution.py:388
  80.3 0.6 collective-permute-done.15
  81.0 0.7 collective-permute-start.17
  81.7 1.8 %collective-permute-start.18 = (bf16[4,80,384]{2,1,0:T(8,128)(2,1)S(1)}, bf16[4,80,384]{2,1,0:T(8,128)(2,1)S(1)}, u32[]{:S(2)}, u32[]{:S(2)}) collective-permute-start(bf16[4,80,384]{2,1,0:T(8,128)(2,1)S(1)} %pad_maximum_fusion.2.refs_9_), channel_id=1, source_target_pairs={{0,4},{1,5},{2,6},{3,7},{4,0},{5,1},{6,2},{7,3},{8,12},{9,13},{10,... | collective-permute-start | bytes 737288 | tf_op jit(solution)/shard_map/ppermute | solution.py:388
  83.5 0.3 collective-permute-start.20
  83.8 3.0 %collective-permute-start.21 = (bf16[3,3,8,384]{3,2,1,0:T(8,128)(2,1)S(1)}, bf16[3,3,8,384]{3,2,1,0:T(8,128)(2,1)S(1)}, u32[]{:S(2)}, u32[]{:S(2)}) collective-permute-start(bf16[3,3,8,384]{3,2,1,0:T(8,128)(2,1)S(1)} %get-tuple-element.100), channel_id=1, source_target_pairs={{0,5},{1,6},{2,7},{3,4},{4,9},{5,10},{6,11},{7,8},{8,13},{9,14},{1... | collective-permute-start | bytes 165896 | tf_op jit(solution)/shard_map/ppermute | solution.py:347
  86.8 0.9 collective-permute-done.19.refs_2_
  87.8 3.3 %collective-permute-done.20.refs_3_ = bf16[3,3,8,384]{3,2,1,0:T(8,128)(2,1)S(1)} collective-permute-done((bf16[3,3,8,384]{3,2,1,0:T(8,128)(2,1)S(1)}, bf16[3,3,8,384]{3,2,1,0:T(8,128)(2,1)S(1)}, u32[]{:S(2)}, u32[]{:S(2)}) %collective-permute-start.20) | collective-permute-done | bytes 55328 | tf_op jit(solution)/shard_map/ppermute | solution.py:347
  91.0 2.1 %collective-permute-done.21.refs_4_ = bf16[3,3,8,384]{3,2,1,0:T(8,128)(2,1)S(1)} collective-permute-done((bf16[3,3,8,384]{3,2,1,0:T(8,128)(2,1)S(1)}, bf16[3,3,8,384]{3,2,1,0:T(8,128)(2,1)S(1)}, u32[]{:S(2)}, u32[]{:S(2)}) %collective-permute-start.21) | collective-permute-done | bytes 55328 | tf_op jit(solution)/shard_map/ppermute | solution.py:347
  93.2 0.5 collective-permute-start.24
  93.8 1.9 %collective-permute-done.24.refs_11_ = bf16[4,80,384]{2,1,0:T(8,128)(2,1)S(1)} collective-permute-done((bf16[4,80,384]{2,1,0:T(8,128)(2,1)S(1)}, bf16[4,80,384]{2,1,0:T(8,128)(2,1)S(1)}, u32[]{:S(2)}, u32[]{:S(2)}) %collective-permute-start.24) | collective-permute-done | bytes 245792 | tf_op jit(solution)/shard_map/ppermute | solution.py:388
  95.6 0.3 collective-permute-done.25.refs_12_
  96.0 3.8 %shard_map.165 = (bf16[6,6,8,384]{3,2,1,0:T(8,128)(2,1)}, f32[384]{0:T(512)}, bf16[16,24,1152]{2,1,0:T(8,128)(2,1)}, bf16[16,24,384]{2,1,0:T(8,128)(2,1)}, f32[3...) custom-call(s32[5]{0:T(128)S(1)} %stack.29.refs_0_.me, ...), custom_call_target="tpu_custom_call" | custom-call | flops 589824 | bytes 7627796 | tf_op jit(solution)/shard_map/pallas_call | solution.py:329
  (47 shorter events, 1.3 us)
Async XLA Ops:
  0.6 13.5 %copy-start = (bf16[6,6,8,384]{3,2,1,0:T(8,128)(2,1)S(1)}, bf16[6,6,8,384]{3,2,1,0:T(8,128)(2,1)}, u32[]{:S(2)}) copy-start(bf16[6,6,8,384]{3,2,1,0:T(8,128)(2,1)} %tok.1) | copy-start | bytes 663556
  0.6 13.5 %copy-start.1 = (bf16[6,6,8,384]{3,2,1,0:T(8,128)(2,1)S(1)}, bf16[6,6,8,384]{3,2,1,0:T(8,128)(2,1)}, u32[]{:S(2)}) copy-start(bf16[6,6,8,384]{3,2,1,0:T(8,128)(2,1)} %up_own.1) | copy-start | bytes 663556
  0.7 13.5 %copy-start.2 = (f32[384]{0:T(512)S(1)}, f32[384]{0:T(512)}, u32[]{:S(2)}) copy-start(f32[384]{0:T(512)} %gain1.3) | copy-start | bytes 4612
  0.7 13.5 %copy-start.4 = (f32[384]{0:T(512)S(1)}, f32[384]{0:T(512)}, u32[]{:S(2)}) copy-start(f32[384]{0:T(512)} %gain2.1) | copy-start | bytes 4612
  0.7 13.5 %copy-start.3 = (f32[1536]{0:T(1024)S(1)}, f32[1536]{0:T(1024)}, u32[]{:S(2)}) copy-start(f32[1536]{0:T(1024)} %b_fc1.1) | copy-start | bytes 18436
  1.8 10.8 %collective-permute-start = (bf16[2,3,3,8,384]{4,3,2,1,0:T(8,128)(2,1)S(1)}, bf16[2,3,3,8,384]{4,3,2,1,0:T(8,128)(2,1)S(1)}, u32[]{:S(2)}, u32[]{:S(2)}) collective-permute-start(bf16[2,3,3,8,384]{4,3,2,1,0:T(8,128)(2,1)S(1)} %get-tuple-element.124), channel_id=1, source_target_pairs={{0,3},{1,0},{2,1},{3,2},{4,7},{5,4},{6,5},{7,6},{8,11},{9,8},{10,9... | collective-permute-start | bytes 331784 | tf_op jit(solution)/shard_map/ppermute | solution.py:347
  4.2 8.4 %collective-permute-start.1 = (bf16[2,3,3,8,384]{4,3,2,1,0:T(8,128)(2,1)S(1)}, bf16[2,3,3,8,384]{4,3,2,1,0:T(8,128)(2,1)S(1)}, u32[]{:S(2)}, u32[]{:S(2)}) collective-permute-start(bf16[2,3,3,8,384]{4,3,2,1,0:T(8,128)(2,1)S(1)} %get-tuple-element.123), channel_id=1, source_target_pairs={{0,28},{1,29},{2,30},{3,31},{4,0},{5,1},{6,2},{7,3},{8,4},{9,5},{1... | collective-permute-start | bytes 331784 | tf_op jit(solution)/shard_map/ppermute | solution.py:347
  8.8 5.4 %collective-permute-start.2 = (bf16[2,3,3,8,384]{4,3,2,1,0:T(8,128)(2,1)S(1)}, bf16[2,3,3,8,384]{4,3,2,1,0:T(8,128)(2,1)S(1)}, u32[]{:S(2)}, u32[]{:S(2)}) collective-permute-start(bf16[2,3,3,8,384]{4,3,2,1,0:T(8,128)(2,1)S(1)} %get-tuple-element.122), channel_id=1, source_target_pairs={{0,31},{1,28},{2,29},{3,30},{4,3},{5,0},{6,1},{7,2},{8,7},{9,4},{1... | collective-permute-start | bytes 331784 | tf_op jit(solution)/shard_map/ppermute | solution.py:347
  25.8 3.9 %collective-permute-start.3 = (bf16[8,216,384]{2,1,0:T(8,128)(2,1)S(1)}, bf16[8,216,384]{2,1,0:T(8,128)(2,1)S(1)}, u32[]{:S(2)}, u32[]{:S(2)}) collective-permute-start(bf16[8,216,384]{2,1,0:T(8,128)(2,1)S(1)} %get-tuple-element.75), channel_id=1, source_target_pairs={{0,1},{1,0},{2,3},{3,2},{4,5},{5,4},{6,7},{7,6},{8,9},{9,8},{10,11... | collective-permute-start | bytes 3981320 | tf_op jit(solution)/shard_map/ppermute | solution.py:388
  33.7 2.0 %collective-permute-start.5 = (bf16[8,80,384]{2,1,0:T(8,128)(2,1)S(1)}, bf16[8,80,384]{2,1,0:T(8,128)(2,1)S(1)}, u32[]{:S(2)}, u32[]{:S(2)}) collective-permute-start(bf16[8,80,384]{2,1,0:T(8,128)(2,1)S(1)} %get-tuple-element.81), channel_id=1, source_target_pairs={{0,1},{1,0},{2,3},{3,2},{4,5},{5,4},{6,7},{7,6},{8,9},{9,8},{10,11... | collective-permute-start | bytes 1474568 | tf_op jit(solution)/shard_map/ppermute | solution.py:388
  34.3 10.7 %collective-permute-start.4 = (bf16[4,216,384]{2,1,0:T(8,128)(2,1)S(1)}, bf16[4,216,384]{2,1,0:T(8,128)(2,1)S(1)}, u32[]{:S(2)}, u32[]{:S(2)}) collective-permute-start(bf16[4,216,384]{2,1,0:T(8,128)(2,1)S(1)} %get-tuple-element.115), channel_id=1, source_target_pairs={{0,2},{1,9},{2,0},{3,11},{4,6},{5,13},{6,4},{7,15},{8,10},{9,1},{1... | collective-permute-start | bytes 1990664 | tf_op jit(solution)/shard_map/ppermute | solution.py:388
  35.9 9.3 %collective-permute-start.7 = (bf16[4,80,384]{2,1,0:T(8,128)(2,1)S(1)}, bf16[4,80,384]{2,1,0:T(8,128)(2,1)S(1)}, u32[]{:S(2)}, u32[]{:S(2)}) collective-permute-start(bf16[4,80,384]{2,1,0:T(8,128)(2,1)S(1)} %get-tuple-element.119), channel_id=1, source_target_pairs={{0,4},{1,5},{2,6},{3,7},{4,0},{5,1},{6,2},{7,3},{8,12},{9,13},{10,... | collective-permute-start | bytes 737288 | tf_op jit(solution)/shard_map/ppermute | solution.py:388
  45.1 7.2 %collective-permute-start.6 = (bf16[2,216,384]{2,1,0:T(8,128)(2,1)S(1)}, bf16[2,216,384]{2,1,0:T(8,128)(2,1)S(1)}, u32[]{:S(2)}, u32[]{:S(2)}) collective-permute-start(bf16[2,216,384]{2,1,0:T(8,128)(2,1)S(1)} %get-tuple-element.116), channel_id=1, source_target_pairs={{0,4},{1,3},{2,6},{3,1},{4,0},{5,7},{6,2},{7,5},{8,12},{9,11},{10,... | collective-permute-start | bytes 995336 | tf_op jit(solution)/shard_map/ppermute | solution.py:388
  45.3 7.2 %collective-permute-start.9 = (bf16[2,80,384]{2,1,0:T(8,128)(2,1)S(1)}, bf16[2,80,384]{2,1,0:T(8,128)(2,1)S(1)}, u32[]{:S(2)}, u32[]{:S(2)}) collective-permute-start(bf16[2,80,384]{2,1,0:T(8,128)(2,1)S(1)} %get-tuple-element.121), channel_id=1, source_target_pairs={{0,8},{1,9},{2,10},{3,11},{4,12},{5,13},{6,14},{7,15},{8,0},{9,1},... | collective-permute-start | bytes 368648 | tf_op jit(solution)/shard_map/ppermute | solution.py:388
  52.3 5.4 %collective-permute-start.8 = (bf16[1,216,384]{2,1,0:T(8,128)(2,1)S(1)}, bf16[1,216,384]{2,1,0:T(8,128)(2,1)S(1)}, u32[]{:S(2)}, u32[]{:S(2)}) collective-permute-start(bf16[1,216,384]{2,1,0:T(8,128)(2,1)S(1)} %add_convert_fusion.8), channel_id=1, source_target_pairs={{0,8},{1,5},{2,10},{3,7},{4,12},{5,1},{6,14},{7,3},{8,0},{9,13},{1... | collective-permute-start | bytes 497672 | tf_op jit(solution)/shard_map/ppermute | solution.py:388
  52.5 7.1 %collective-permute-start.11 = (bf16[1,80,384]{2,1,0:T(8,128)(2,1)S(1)}, bf16[1,80,384]{2,1,0:T(8,128)(2,1)S(1)}, u32[]{:S(2)}, u32[]{:S(2)}) collective-permute-start(bf16[1,80,384]{2,1,0:T(8,128)(2,1)S(1)} %add_convert_fusion.15), channel_id=1, source_target_pairs={{0,2},{1,3},{2,0},{3,1},{4,6},{5,7},{6,4},{7,5},{8,10},{9,11},{10,... | collective-permute-start | bytes 184328 | tf_op jit(solution)/shard_map/ppermute | solution.py:388
  57.8 9.9 %collective-permute-start.10 = (bf16[216,384]{1,0:T(8,128)(2,1)S(1)}, bf16[216,384]{1,0:T(8,128)(2,1)S(1)}, u32[]{:S(2)}, u32[]{:S(2)}) collective-permute-start(bf16[216,384]{1,0:T(8,128)(2,1)S(1)} %fusion), channel_id=1, source_target_pairs={{0,16},{1,17},{2,18},{3,19},{4,20},{5,21},{6,22},{7,23},{8,24},{9,... | collective-permute-start | bytes 497672 | tf_op jit(solution)/shard_map/ppermute | solution.py:388
  59.6 8.8 %collective-permute-start.13 = (bf16[80,384]{1,0:T(8,128)(2,1)S(1)}, bf16[80,384]{1,0:T(8,128)(2,1)S(1)}, u32[]{:S(2)}, u32[]{:S(2)}) collective-permute-start(bf16[80,384]{1,0:T(8,128)(2,1)S(1)} %fusion.1), channel_id=1, source_target_pairs={{0,16},{1,17},{2,18},{3,19},{4,20},{5,21},{6,22},{7,23},{8,24},{9,... | collective-permute-start | bytes 184328 | tf_op jit(solution)/shard_map/ppermute | solution.py:388
  68.3 5.3 %collective-permute-start.12 = (bf16[1,216,384]{2,1,0:T(8,128)(2,1)S(1)}, bf16[1,216,384]{2,1,0:T(8,128)(2,1)S(1)}, u32[]{:S(2)}, u32[]{:S(2)}) collective-permute-start(bf16[1,216,384]{2,1,0:T(8,128)(2,1)S(1)} %bitcast.17), channel_id=1, source_target_pairs={{0,8},{1,5},{2,10},{3,7},{4,12},{5,1},{6,14},{7,3},{8,0},{9,13},{1... | collective-permute-start | bytes 497672 | tf_op jit(solution)/shard_map/ppermute | solution.py:388
  68.7 4.3 %collective-permute-start.14 = (bf16[1,80,384]{2,1,0:T(8,128)(2,1)S(1)}, bf16[1,80,384]{2,1,0:T(8,128)(2,1)S(1)}, u32[]{:S(2)}, u32[]{:S(2)}) collective-permute-start(bf16[1,80,384]{2,1,0:T(8,128)(2,1)S(1)} %fusion.2), channel_id=1, source_target_pairs={{0,2},{1,3},{2,0},{3,1},{4,6},{5,7},{6,4},{7,5},{8,10},{9,11},{10,... | collective-permute-start | bytes 184328 | tf_op jit(solution)/shard_map/ppermute | solution.py:388
  73.7 7.2 %collective-permute-start.15 = (bf16[2,216,384]{2,1,0:T(8,128)(2,1)S(1)}, bf16[2,216,384]{2,1,0:T(8,128)(2,1)S(1)}, u32[]{:S(2)}, u32[]{:S(2)}) collective-permute-start(bf16[2,216,384]{2,1,0:T(8,128)(2,1)S(1)} %pad_maximum_fusion.1), channel_id=1, source_target_pairs={{0,4},{1,3},{2,6},{3,1},{4,0},{5,7},{6,2},{7,5},{8,12},{9,11},{10,... | collective-permute-start | bytes 995336 | tf_op jit(solution)/shard_map/ppermute | solution.py:388
  75.2 5.1 %collective-permute-start.16 = (bf16[2,80,384]{2,1,0:T(8,128)(2,1)S(1)}, bf16[2,80,384]{2,1,0:T(8,128)(2,1)S(1)}, u32[]{:S(2)}, u32[]{:S(2)}) collective-permute-start(bf16[2,80,384]{2,1,0:T(8,128)(2,1)S(1)} %pad_maximum_fusion.3), channel_id=1, source_target_pairs={{0,8},{1,9},{2,10},{3,11},{4,12},{5,13},{6,14},{7,15},{8,0},{9,1},... | collective-permute-start | bytes 368648 | tf_op jit(solution)/shard_map/ppermute | solution.py:388
  81.0 12.2 %collective-permute-start.17 = (bf16[4,216,384]{2,1,0:T(8,128)(2,1)S(1)}, bf16[4,216,384]{2,1,0:T(8,128)(2,1)S(1)}, u32[]{:S(2)}, u32[]{:S(2)}) collective-permute-start(bf16[4,216,384]{2,1,0:T(8,128)(2,1)S(1)} %pad_maximum_fusion.refs_5_), channel_id=1, source_target_pairs={{0,2},{1,9},{2,0},{3,11},{4,6},{5,13},{6,4},{7,15},{8,10},{9,1},{1... | collective-permute-start | bytes 1990664 | tf_op jit(solution)/shard_map/ppermute | solution.py:388
  81.7 11.5 %collective-permute-start.18 = (bf16[4,80,384]{2,1,0:T(8,128)(2,1)S(1)}, bf16[4,80,384]{2,1,0:T(8,128)(2,1)S(1)}, u32[]{:S(2)}, u32[]{:S(2)}) collective-permute-start(bf16[4,80,384]{2,1,0:T(8,128)(2,1)S(1)} %pad_maximum_fusion.2.refs_9_), channel_id=1, source_target_pairs={{0,4},{1,5},{2,6},{3,7},{4,0},{5,1},{6,2},{7,3},{8,12},{9,13},{10,... | collective-permute-start | bytes 737288 | tf_op jit(solution)/shard_map/ppermute | solution.py:388
  83.5 4.2 %collective-permute-start.19 = (bf16[3,3,8,384]{3,2,1,0:T(8,128)(2,1)S(1)}, bf16[3,3,8,384]{3,2,1,0:T(8,128)(2,1)S(1)}, u32[]{:S(2)}, u32[]{:S(2)}) collective-permute-start(bf16[3,3,8,384]{3,2,1,0:T(8,128)(2,1)S(1)} %get-tuple-element.98), channel_id=1, source_target_pairs={{0,1},{1,2},{2,3},{3,0},{4,5},{5,6},{6,7},{7,4},{8,9},{9,10},{10,1... | collective-permute-start | bytes 165896 | tf_op jit(solution)/shard_map/ppermute | solution.py:347
  83.5 7.5 %collective-permute-start.20 = (bf16[3,3,8,384]{3,2,1,0:T(8,128)(2,1)S(1)}, bf16[3,3,8,384]{3,2,1,0:T(8,128)(2,1)S(1)}, u32[]{:S(2)}, u32[]{:S(2)}) collective-permute-start(bf16[3,3,8,384]{3,2,1,0:T(8,128)(2,1)S(1)} %get-tuple-element.99), channel_id=1, source_target_pairs={{0,4},{1,5},{2,6},{3,7},{4,8},{5,9},{6,10},{7,11},{8,12},{9,13},{1... | collective-permute-start | bytes 165896 | tf_op jit(solution)/shard_map/ppermute | solution.py:347
  83.8 9.4 %collective-permute-start.21 = (bf16[3,3,8,384]{3,2,1,0:T(8,128)(2,1)S(1)}, bf16[3,3,8,384]{3,2,1,0:T(8,128)(2,1)S(1)}, u32[]{:S(2)}, u32[]{:S(2)}) collective-permute-start(bf16[3,3,8,384]{3,2,1,0:T(8,128)(2,1)S(1)} %get-tuple-element.100), channel_id=1, source_target_pairs={{0,5},{1,6},{2,7},{3,4},{4,9},{5,10},{6,11},{7,8},{8,13},{9,14},{1... | collective-permute-start | bytes 165896 | tf_op jit(solution)/shard_map/ppermute | solution.py:347
  87.8 7.9 %collective-permute-start.22 = (bf16[4,216,384]{2,1,0:T(8,128)(2,1)S(1)}, bf16[4,216,384]{2,1,0:T(8,128)(2,1)S(1)}, u32[]{:S(2)}, u32[]{:S(2)}) collective-permute-start(bf16[4,216,384]{2,1,0:T(8,128)(2,1)S(1)} %pad_maximum_fusion.refs_5_), channel_id=1, source_target_pairs={{0,1},{1,0},{2,3},{3,2},{4,5},{5,4},{6,7},{7,6},{8,9},{9,8},{10,11... | collective-permute-start | bytes 1990664 | tf_op jit(solution)/shard_map/ppermute | solution.py:388
  93.2 2.8 %collective-permute-start.23 = (bf16[4,216,384]{2,1,0:T(8,128)(2,1)S(1)}, bf16[4,216,384]{2,1,0:T(8,128)(2,1)S(1)}, u32[]{:S(2)}, u32[]{:S(2)}) collective-permute-start(bf16[4,216,384]{2,1,0:T(8,128)(2,1)S(1)} %collective-permute-done.17.refs_6_), channel_id=1, source_target_pairs={{0,1},{1,0},{2,3},{3,2},{4,5},{5,4},{6,7},{7,6},{8,9},{9,8},{10,11... | collective-permute-start | bytes 1990664 | tf_op jit(solution)/shard_map/ppermute | solution.py:388
  93.2 2.5 %collective-permute-start.24 = (bf16[4,80,384]{2,1,0:T(8,128)(2,1)S(1)}, bf16[4,80,384]{2,1,0:T(8,128)(2,1)S(1)}, u32[]{:S(2)}, u32[]{:S(2)}) collective-permute-start(bf16[4,80,384]{2,1,0:T(8,128)(2,1)S(1)} %pad_maximum_fusion.2.refs_9_), channel_id=1, source_target_pairs={{0,1},{1,0},{2,3},{3,2},{4,5},{5,4},{6,7},{7,6},{8,9},{9,8},{10,11... | collective-permute-start | bytes 737288 | tf_op jit(solution)/shard_map/ppermute | solution.py:388
  93.7 2.3 %collective-permute-start.25 = (bf16[4,80,384]{2,1,0:T(8,128)(2,1)S(1)}, bf16[4,80,384]{2,1,0:T(8,128)(2,1)S(1)}, u32[]{:S(2)}, u32[]{:S(2)}) collective-permute-start(bf16[4,80,384]{2,1,0:T(8,128)(2,1)S(1)} %collective-permute-done.18.refs_10_), channel_id=1, source_target_pairs={{0,1},{1,0},{2,3},{3,2},{4,5},{5,4},{6,7},{7,6},{8,9},{9,8},{10,11... | collective-permute-start | bytes 737288 | tf_op jit(solution)/shard_map/ppermute | solution.py:388

commit v4 on v3

--- a/solution.py
+++ b/solution.py
@@ -18,7 +18,6 @@
 PIECES = 16
 BLOCKS = 4
 EXTRA = 8
-EARLY = 2
 KERNEL_VMEM = 40 << 20
 F32 = jnp.float32
 BF16 = jnp.bfloat16
@@ -112,6 +111,7 @@
         copy.start()
     width = w_proj.shape[0]
     heads = width // HD
+    rows = allowed.shape[0]
     each = PIECES // BLOCKS
     piece = each * width * BLOCKS // (PIECES * each)
     parts = (part_b, part_c, part_d)
@@ -123,17 +123,24 @@
     qkv[...] = dot(h1, w_qkv[...]).astype(BF16)
     allowed[...] = (code_col[...] == code_row[...]).astype(F32)
 
-    for head in range(heads):
-        lo, sub, mine, q, k, v = head_columns(qkv, head, width)
-        scores = dot_last(jnp.where(mine, q, jnp.zeros_like(q)), k)
-        scores = jnp.where(allowed[...] > 0.0, scores, -1e30)
+    together = 4
+    for first in range(0, heads, together):
+        masks = []
+        for head in range(first, first + together):
+            lo, sub, mine, q, k, v = head_columns(qkv, head, width)
+            masks.append(mine)
+        stacked = jnp.concatenate([jnp.where(mine, q, jnp.zeros_like(q)) for mine in masks], axis=0)
+        scores = dot_last(stacked, k).reshape(together, rows, rows)
+        scores = jnp.where(allowed[...][None] > 0.0, scores, -1e30)
         highest = jnp.max(scores, axis=-1, keepdims=True)
         weight = jnp.exp2((scores - highest) * (HD ** (-0.5) * LOG2_E))
         total = jnp.sum(weight, axis=-1, keepdims=True)
         prob = (weight * (1.0 / total)).astype(BF16)
-        probs[head] = prob
-        part = dot(prob, v)
-        mix[:, lo : lo + LANES] = part if sub == 0 else jnp.where(mine, part, mix[:, lo : lo + LANES])
+        probs[first : first + together] = prob
+        part = dot(prob.reshape(together * rows, rows), v).reshape(together, rows, LANES)
+        for i, mine in enumerate(masks):
+            old = mix[:, lo : lo + LANES] if (first + i) % (LANES // HD) else None
+            mix[:, lo : lo + LANES] = part[i] if old is None else jnp.where(mine, part[i], old)
 
     for copy in fetch:
         copy.wait()
@@ -174,41 +181,42 @@
         put_block(stage, grad[:, j * width : (j + 1) * width], me, 0, piece, j * each, each)
     back2, s_ln2 = norm_back(t2, normed2, inv2, gain2[...][None, :])
     small[0:1, :] = s_ln2
-    grad_res = up + back2
-    grad_mid[...] = grad_res
-    grad_proj = dot_first(mix_low, grad_res.astype(BF16)).astype(BF16)
-    put_block(stage, grad_proj, me, 0, 2 * piece)
+    grad_mid[...] = up + back2
     hand_out(stage, keep, send)
 
 
-def heads_back(groups, qkv, probs, mix, dmix, dqkv):
+def heads_back(qkv, probs, mix, dmix, dqkv):
     width = mix.shape[1]
     score_scale = HD ** (-0.5)
     per_group = LANES // HD
-    for group in groups:
+    for group in range(width // LANES):
         sums = None
-        for head in range(group * per_group, (group + 1) * per_group):
-            lo, sub, mine, q, k, v = head_columns(qkv, head, width)
-            do = dmix[:, lo : lo + LANES]
-            do_mine = jnp.where(mine, do, jnp.zeros_like(do))
-            delta = jnp.sum(do_mine.astype(F32) * mix[:, lo : lo + LANES], axis=-1, keepdims=True)
-            prob = probs[head]
-            ds = (prob.astype(F32) * (dot_last(do_mine, v) - delta)).astype(BF16)
-            parts = (dot(ds, k) * score_scale, dot_first(ds, q) * score_scale, dot_first(prob, do))
-            sums = parts if sums is None else [jnp.where(mine, a, b) for a, b in zip(parts, sums)]
+        together = 4
+        for first in range(group * per_group, (group + 1) * per_group, together):
+            masks, deltas, dos = [], [], []
+            for head in range(first, first + together):
+                lo, sub, mine, q, k, v = head_columns(qkv, head, width)
+                do = dmix[:, lo : lo + LANES]
+                do_mine = jnp.where(mine, do, jnp.zeros_like(do))
+                deltas.append(jnp.sum(do_mine.astype(F32) * mix[:, lo : lo + LANES], axis=-1, keepdims=True))
+                masks.append(mine)
+                dos.append(do_mine)
+            rows = do.shape[0]
+            prob = probs[first : first + together]
+            dp = dot_last(jnp.concatenate(dos, axis=0), v).reshape(together, rows, rows)
+            ds = (prob.astype(F32) * (dp - jnp.stack(deltas))).astype(BF16)
+            dq = dot(ds.reshape(together * rows, rows), k).reshape(together, rows, LANES)
+            for i, mine in enumerate(masks):
+                parts = (dq[i] * score_scale, dot_first(ds[i], q) * score_scale, dot_first(prob[i], do))
+                sums = parts if sums is None else [jnp.where(mine, a, b) for a, b in zip(parts, sums)]
         for i, part in enumerate(sums):
             dqkv[:, i * width + lo : i * width + lo + LANES] = part.astype(BF16)
 
 
-def first_back_kernel(me, grad_mid, qkv, probs, mix, w_proj, dmix, dqkv):
-    dmix[...] = dot_last(grad_mid[...].astype(BF16), w_proj[...]).astype(BF16)
-    heads_back(range(EARLY), qkv, probs, mix, dmix, dqkv)
-
-
-def second_back_kernel(
-    me, small, grad_mid, normed1, inv1, qkv, probs, mix, dmix, dqkv_early, gain1, w_qkv,
+def backward_kernel(
+    me, small, grad_mid, normed1, inv1, qkv, probs, mix, gain1, w_qkv, w_proj,
     out_a, out_b, out_c, out_d, keep_t, send_t,
-    dqkv, stage_t,
+    dmix, dqkv, stage_t,
 ):
     width = mix.shape[1]
     pieces, rows, _ = stage_t.shape
@@ -216,13 +224,13 @@
     extra = [me[0] * (PIECES // 2) + low_slot(i, me, 1) for i in range(BLOCKS + 2)]
     for i in range(BLOCKS + 1):
         stage_t[extra[i + 1], rows - EXTRA : rows - EXTRA + 1] = small[i : i + 1, :].astype(BF16)
-    heads_back(range(EARLY, width // LANES), qkv, probs, mix, dmix, dqkv)
+    grad_attn = grad_mid[...].astype(BF16)
+    dmix[...] = dot_last(grad_attn, w_proj[...]).astype(BF16)
+    heads_back(qkv, probs, mix, dmix, dqkv)
+    grad_proj = dot_first(mix[...].astype(BF16), grad_attn).astype(BF16)
+    put_block(stage_t, grad_proj, me, 1, 3 * width // PIECES)
     normed = normed1[...]
     h1 = (normed * gain1[...][None, :]).astype(BF16)
-    early = EARLY * LANES
-    for j in range(3):
-        lo = j * width
-        dqkv[:, lo : lo + early] = dqkv_early[:, lo : lo + early]
     grad = dot_first(h1, dqkv[...]).astype(BF16)
     for j in range(3):
         put_block(stage_t, grad[:, j * width : (j + 1) * width], me, 1, j * width // PIECES)
@@ -281,20 +289,20 @@
                     piece, down, across = spot(core, 0, slot)
                     fc2[pl.ds(pl.multiple_of(piece * rows, rows), rows), :] = value[:rows]
                     fc1[down, across] = value[rows : 2 * rows]
-                    proj[piece] = value[2 * rows :]
                 else:
                     value = ref[j].astype(F32) * factor
                     piece, down, across = spot(core, 1, slot)
                     for part in range(3):
                         at = slice(part * width, (part + 1) * width)
                         qkv[piece, :, at] = value[part * thin : (part + 1) * thin].astype(BF16)
-                    smalls[piece] = value[3 * thin :]
+                    proj[piece] = value[3 * thin : 4 * thin].astype(BF16)
+                    smalls[piece] = value[4 * thin :]
         if kind == 0:
             leave(fc2, g_fc2)
             leave(fc1, g_fc1)
-            leave(proj, g_proj)
         else:
             leave(qkv, g_qkv)
+            leave(proj, g_proj)
     g_ln1[...] = smalls[0, 0]
     g_ln2[...] = smalls[1, 0]
     for j in range(BLOCKS):
@@ -481,7 +489,7 @@
     me = place()
     piece = BLOCKS * width // PIECES
     thin = width // PIECES
-    rows_f, rows_t = 2 * piece + thin, 3 * thin + EXTRA
+    rows_f, rows_t = 2 * piece, 4 * thin + EXTRA
     half = shape((PIECES // 2, rows_f, width), BF16)
     half_t = shape((PIECES // 2, rows_t, width), BF16)
     weights = (w_qkv, w_proj)
@@ -506,26 +514,21 @@
     quarter = shape(parts[0].shape[1:], BF16)
     small, grad_mid, normed1, inv1, qkv, probs, mix = saved
     got = swap(send, CORE)
-    dmix, dqkv = call(
-        first_back_kernel,
-        (shape((rows, width), BF16), shape((rows, 3 * width), BF16)),
-        [],
-        2 * rows * width * width + 8 * EARLY * (LANES // HD) * rows * rows * LANES,
+    *done, keep_t, send_t = call(
+        backward_kernel,
+        (quarter,) * 4 + (half_t, half_t),
+        [
+            pltpu.VMEM((rows, width), BF16),
+            pltpu.VMEM((rows, 3 * width), BF16),
+            pltpu.VMEM((PIECES, rows_t, width), BF16),
+        ],
+        2 * rows * width * 8 * width + 8 * heads * rows * rows * LANES,
         me,
-        (grad_mid, qkv, probs, mix, w_proj),
-    )
-    got, = after([got], dmix)
+        (small, grad_mid, normed1, inv1, qkv, probs, mix, ln1_gain, w_qkv, w_proj),
+    )
+    got, = after([got], keep_t)
     keep, send = fold(keep, got)
     got = swap(send, ORDERS[0][0])
-    dmix, = after([dmix], send)
-    *done, keep_t, send_t = call(
-        second_back_kernel,
-        (quarter,) * 4 + (half_t, half_t),
-        [pltpu.VMEM((rows, 3 * width), BF16), pltpu.VMEM((PIECES, rows_t, width), BF16)],
-        2 * rows * width * 7 * width + 8 * (heads - EARLY * (LANES // HD)) * rows * rows * LANES,
-        me,
-        (small, grad_mid, normed1, inv1, qkv, probs, mix, dmix, dqkv, ln1_gain, w_qkv),
-    )
     back, slots = reduce_all(keep, send, got, keep_t, send_t, done[1:])
     result, g_ln1, g_qkv, g_proj, g_ln2, g_fc1, g_bfc1, g_fc2 = call(
         finish_kernel,

time: 100 us -> 94.3 us (0.943)
  Pallas kernels: 24.7 us -> 19.2 us
  waiting for transfers between devices: 46.2 us -> 40.7 us
  starting transfers between devices: 24.1 us -> 29.2 us
    ppermute x20, starting transfers between devices: 13.5 us -> 19.8 us  [swap(): return lax.ppermute(shard, ('gx', 'gy'), pairs)]
    pallas_call x5 -> x4, Pallas kernels: 24.7 us -> 19.2 us  [call(): pl.pallas_call(kernel, out_shape=outs, in_specs=[SMEM] + [VMEM] * len(nea...]
    ppermute x20, waiting for transfers between devices: 38.3 us -> 33.5 us  [swap(): return lax.ppermute(shard, ('gx', 'gy'), pairs)]
    ppermute x6, starting transfers between devices: 10.6 us -> 9.4 us  [neighbour(): return lax.ppermute(shard, ('gx', 'gy'), pairs)]
  transfers between devices with their start and end apart: 26 -> 26, of which waited for: 16 -> 14; matrix products, arithmetic and copies ran while one was open for 2% -> 3% of each run, Pallas kernels for 6% -> 8%
where the time goes in v4:
time: 94.3 us; the launch traced here: 94.1 us
  waiting for transfers between devices  40.7 us (43%)
  starting transfers between devices  29.2 us (31%)
  Pallas kernels  19.2 us (20%)
  other arithmetic  3.34 us (4%)
  between operations  1.04 us (1%)
    ppermute x20, waiting for transfers between devices, swap(): return lax.ppermute(shard, ('gx', 'gy'), pairs)  33.5 us
    ppermute x20, starting transfers between devices, swap(): return lax.ppermute(shard, ('gx', 'gy'), pairs)  19.8 us
    pallas_call x4, Pallas kernels, call(): pl.pallas_call(kernel, out_shape=outs, in_specs=[SMEM] + [VMEM] * len(nea...  19.2 us
    ppermute x6, starting transfers between devices, neighbour(): return lax.ppermute(shard, ('gx', 'gy'), pairs)  9.4 us
    ppermute x6, waiting for transfers between devices, neighbour(): return lax.ppermute(shard, ('gx', 'gy'), pairs)  7.24 us
  transfers between devices with their start and end apart: 26, of which 14 were waited for; matrix products, arithmetic and copies ran while one was open for 3% of the time, Pallas kernels for 8%

profile of v4, /device:TPU:0, one launch (start us, length us, event | category | flops | bytes accessed | tf_op | source)
XLA Modules:
  0.0 94.1 jit_solution(10518844089472640633)
XLA Ops:
  0.7 1.1 %pad_maximum_fusion.4 = (bf16[2,3,3,8,384]{4,3,2,1,0:T(8,128)(2,1)S(1)}, bf16[2,3,3,8,384]{4,3,2,1,0:T(8,128)(2,1)S(1)}, bf16[2,3,3,8,384]{4,3,2,1,0:T(8,128)(2,1)S(1)}) fusion(bf16[1,6,6,8,384]{4,3,2,1,0:T(8,128)(2,1)} %bitcast.16, bf16[1,6,6,8,384]{4,3,2,1,0:T(8,128)(2,1)} %bitcast.15), kind=kLoop, calls=%fused_computation.21 | loop fusion | flops 165888 | bytes 774144 | tf_op jit(solution)/shard_map/stack | solution.py:486
  1.8 6.4 %collective-permute-start.2 = (bf16[2,3,3,8,384]{4,3,2,1,0:T(8,128)(2,1)S(1)}, bf16[2,3,3,8,384]{4,3,2,1,0:T(8,128)(2,1)S(1)}, u32[]{:S(2)}, u32[]{:S(2)}) collective-permute-start(bf16[2,3,3,8,384]{4,3,2,1,0:T(8,128)(2,1)S(1)} %get-tuple-element.116), channel_id=1, source_target_pairs={{0,31},{1,28},{2,29},{3,30},{4,3},{5,0},{6,1},{7,2},{8,7},{9,4},{1... | collective-permute-start | bytes 331784 | tf_op jit(solution)/shard_map/ppermute | solution.py:355
  8.2 0.5 collective-permute-start.1
  8.7 0.6 collective-permute-start
  9.3 0.8 add_add_fusion
  10.2 0.1 reshape.59
  10.3 0.1 reshape.60
  10.4 0.1 reshape.62
  10.5 0.1 reshape.61
  10.7 0.1 broadcast_in_dim.19.code_col
  10.8 0.1 stack.29.refs_0_.me
  10.9 1.8 %shard_map.161 = (bf16[384,1152]{1,0:T(8,128)(2,1)S(1)}, bf16[384,384]{1,0:T(8,128)(2,1)S(1)}) custom-call(s32[5]{0:T(128)S(1)} %stack.29.refs_0_.me, bf16[384,1152]{1,0:T(8,128)(2,1)} %refs_1_.1, bf16[384,384]{1,0:T(8,128)(2,1)} %refs_2_.1), custom_call_target="tpu_custom_call" | custom-call | bytes 2359316 | tf_op jit(solution)/shard_map/pallas_call | solution.py:337
  12.7 0.4 collective-permute-done.1.part_c
  13.1 8.2 %shard_map.162 = (bf16[8,192,384]{2,1,0:T(8,128)(2,1)S(1)}, bf16[8,192,384]{2,1,0:T(8,128)(2,1)S(1)}, f32[5,384]{1,0:T(8,128)S(1)}, f32[288,384]{1,0:T(8,128)S(1...) custom-call(s32[5]{0:T(128)S(1)} %stack.29.refs_0_.me, ...), custom_call_target="tpu_custom_call" | custom-call | flops 2548039680 | bytes 10674068 | tf_op jit(solution)/shard_map/pallas_call | solution.py:337
  21.4 5.4 %shard_map.163 = (bf16[3,3,8,384]{3,2,1,0:T(8,128)(2,1)S(1)}, bf16[3,3,8,384]{3,2,1,0:T(8,128)(2,1)S(1)}, bf16[3,3,8,384]{3,2,1,0:T(8,128)(2,1)S(1)}, bf16[3,3,8...) custom-call(s32[5]{0:T(128)S(1)} %stack.29.refs_0_.me, ...), custom_call_target="tpu_custom_call" | custom-call | flops 1698693120 | bytes 6670484 | tf_op jit(solution)/shard_map/pallas_call | solution.py:337
  26.8 0.6 collective-permute-start.5
  27.4 0.5 add_convert_fusion
  27.9 1.5 %collective-permute-start.4 = (bf16[4,192,384]{2,1,0:T(8,128)(2,1)S(1)}, bf16[4,192,384]{2,1,0:T(8,128)(2,1)S(1)}, u32[]{:S(2)}, u32[]{:S(2)}) collective-permute-start(bf16[4,192,384]{2,1,0:T(8,128)(2,1)S(1)} %get-tuple-element.108), channel_id=1, source_target_pairs={{0,2},{1,9},{2,0},{3,11},{4,6},{5,13},{6,4},{7,15},{8,10},{9,1},{1... | collective-permute-start | bytes 1769480 | tf_op jit(solution)/shard_map/ppermute | solution.py:396
  29.4 0.2 add_convert_fusion.2
  29.5 1.0 %collective-permute-start.7 = (bf16[4,104,384]{2,1,0:T(8,128)(2,1)S(1)}, bf16[4,104,384]{2,1,0:T(8,128)(2,1)S(1)}, u32[]{:S(2)}, u32[]{:S(2)}) collective-permute-start(bf16[4,104,384]{2,1,0:T(8,128)(2,1)S(1)} %get-tuple-element.111), channel_id=1, source_target_pairs={{0,4},{1,5},{2,6},{3,7},{4,0},{5,1},{6,2},{7,3},{8,12},{9,13},{10,... | collective-permute-start | bytes 958472 | tf_op jit(solution)/shard_map/ppermute | solution.py:396
  30.5 7.3 %collective-permute-done.4 = bf16[4,192,384]{2,1,0:T(8,128)(2,1)S(1)} collective-permute-done((bf16[4,192,384]{2,1,0:T(8,128)(2,1)S(1)}, bf16[4,192,384]{2,1,0:T(8,128)(2,1)S(1)}, u32[]{:S(2)}, u32[]{:S(2)}) %collective-permute-start.4) | collective-permute-done | bytes 589856 | tf_op jit(solution)/shard_map/ppermute | solution.py:396
  37.8 0.2 add_convert_fusion.4
  38.0 1.3 %collective-permute-start.6 = (bf16[2,192,384]{2,1,0:T(8,128)(2,1)S(1)}, bf16[2,192,384]{2,1,0:T(8,128)(2,1)S(1)}, u32[]{:S(2)}, u32[]{:S(2)}) collective-permute-start(bf16[2,192,384]{2,1,0:T(8,128)(2,1)S(1)} %get-tuple-element.112), channel_id=1, source_target_pairs={{0,4},{1,3},{2,6},{3,1},{4,0},{5,7},{6,2},{7,5},{8,12},{9,11},{10,... | collective-permute-start | bytes 884744 | tf_op jit(solution)/shard_map/ppermute | solution.py:396
  39.3 0.8 collective-permute-start.9
  40.1 4.6 %collective-permute-done.6 = bf16[2,192,384]{2,1,0:T(8,128)(2,1)S(1)} collective-permute-done((bf16[2,192,384]{2,1,0:T(8,128)(2,1)S(1)}, bf16[2,192,384]{2,1,0:T(8,128)(2,1)S(1)}, u32[]{:S(2)}, u32[]{:S(2)}) %collective-permute-start.6) | collective-permute-done | bytes 294944 | tf_op jit(solution)/shard_map/ppermute | solution.py:396
  44.9 1.9 %collective-permute-start.11 = (bf16[1,104,384]{2,1,0:T(8,128)(2,1)S(1)}, bf16[1,104,384]{2,1,0:T(8,128)(2,1)S(1)}, u32[]{:S(2)}, u32[]{:S(2)}) collective-permute-start(bf16[1,104,384]{2,1,0:T(8,128)(2,1)S(1)} %add_convert_fusion.15), channel_id=1, source_target_pairs={{0,2},{1,3},{2,0},{3,1},{4,6},{5,7},{6,4},{7,5},{8,10},{9,11},{10,... | collective-permute-start | bytes 239624 | tf_op jit(solution)/shard_map/ppermute | solution.py:396
  46.8 3.2 %collective-permute-done.8 = bf16[1,192,384]{2,1,0:T(8,128)(2,1)S(1)} collective-permute-done((bf16[1,192,384]{2,1,0:T(8,128)(2,1)S(1)}, bf16[1,192,384]{2,1,0:T(8,128)(2,1)S(1)}, u32[]{:S(2)}, u32[]{:S(2)}) %collective-permute-start.8) | collective-permute-done | bytes 147488 | tf_op jit(solution)/shard_map/ppermute | solution.py:396
  50.1 2.3 %collective-permute-start.10 = (bf16[192,384]{1,0:T(8,128)(2,1)S(1)}, bf16[192,384]{1,0:T(8,128)(2,1)S(1)}, u32[]{:S(2)}, u32[]{:S(2)}) collective-permute-start(bf16[192,384]{1,0:T(8,128)(2,1)S(1)} %fusion), channel_id=1, source_target_pairs={{0,16},{1,17},{2,18},{3,19},{4,20},{5,21},{6,22},{7,23},{8,24},{9,... | collective-permute-start | bytes 442376 | tf_op jit(solution)/shard_map/ppermute | solution.py:396
  52.4 1.3 %collective-permute-start.13 = (bf16[104,384]{1,0:T(8,128)(2,1)S(1)}, bf16[104,384]{1,0:T(8,128)(2,1)S(1)}, u32[]{:S(2)}, u32[]{:S(2)}) collective-permute-start(bf16[104,384]{1,0:T(8,128)(2,1)S(1)} %fusion.1), channel_id=1, source_target_pairs={{0,16},{1,17},{2,18},{3,19},{4,20},{5,21},{6,22},{7,23},{8,24},{9,... | collective-permute-start | bytes 239624 | tf_op jit(solution)/shard_map/ppermute | solution.py:396
  53.8 6.3 %collective-permute-done.10 = bf16[192,384]{1,0:T(8,128)(2,1)S(1)} collective-permute-done((bf16[192,384]{1,0:T(8,128)(2,1)S(1)}, bf16[192,384]{1,0:T(8,128)(2,1)S(1)}, u32[]{:S(2)}, u32[]{:S(2)}) %collective-permute-start.10) | collective-permute-done | bytes 147488 | tf_op jit(solution)/shard_map/ppermute | solution.py:396
  60.1 0.8 collective-permute-done.13
  60.9 0.7 collective-permute-start.12
  61.7 1.8 %collective-permute-start.14 = (bf16[1,104,384]{2,1,0:T(8,128)(2,1)S(1)}, bf16[1,104,384]{2,1,0:T(8,128)(2,1)S(1)}, u32[]{:S(2)}, u32[]{:S(2)}) collective-permute-start(bf16[1,104,384]{2,1,0:T(8,128)(2,1)S(1)} %fusion.2), channel_id=1, source_target_pairs={{0,2},{1,3},{2,0},{3,1},{4,6},{5,7},{6,4},{7,5},{8,10},{9,11},{10,... | collective-permute-start | bytes 239624 | tf_op jit(solution)/shard_map/ppermute | solution.py:396
  63.5 2.7 %collective-permute-done.14 = bf16[1,104,384]{2,1,0:T(8,128)(2,1)S(1)} collective-permute-done((bf16[1,104,384]{2,1,0:T(8,128)(2,1)S(1)}, bf16[1,104,384]{2,1,0:T(8,128)(2,1)S(1)}, u32[]{:S(2)}, u32[]{:S(2)}) %collective-permute-start.14) | collective-permute-done | bytes 79904 | tf_op jit(solution)/shard_map/ppermute | solution.py:396
  66.2 2.6 %collective-permute-start.15 = (bf16[2,192,384]{2,1,0:T(8,128)(2,1)S(1)}, bf16[2,192,384]{2,1,0:T(8,128)(2,1)S(1)}, u32[]{:S(2)}, u32[]{:S(2)}) collective-permute-start(bf16[2,192,384]{2,1,0:T(8,128)(2,1)S(1)} %pad_maximum_fusion.2), channel_id=1, source_target_pairs={{0,4},{1,3},{2,6},{3,1},{4,0},{5,7},{6,2},{7,5},{8,12},{9,11},{10,... | collective-permute-start | bytes 884744 | tf_op jit(solution)/shard_map/ppermute | solution.py:396
  68.8 0.7 collective-permute-start.16
  69.5 6.1 %collective-permute-done.16 = bf16[2,104,384]{2,1,0:T(8,128)(2,1)S(1)} collective-permute-done((bf16[2,104,384]{2,1,0:T(8,128)(2,1)S(1)}, bf16[2,104,384]{2,1,0:T(8,128)(2,1)S(1)}, u32[]{:S(2)}, u32[]{:S(2)}) %collective-permute-start.16) | collective-permute-done | bytes 159776 | tf_op jit(solution)/shard_map/ppermute | solution.py:396
  75.6 2.1 %collective-permute-start.17 = (bf16[4,192,384]{2,1,0:T(8,128)(2,1)S(1)}, bf16[4,192,384]{2,1,0:T(8,128)(2,1)S(1)}, u32[]{:S(2)}, u32[]{:S(2)}) collective-permute-start(bf16[4,192,384]{2,1,0:T(8,128)(2,1)S(1)} %pad_maximum_fusion.refs_5_), channel_id=1, source_target_pairs={{0,2},{1,9},{2,0},{3,11},{4,6},{5,13},{6,4},{7,15},{8,10},{9,1},{1... | collective-permute-start | bytes 1769480 | tf_op jit(solution)/shard_map/ppermute | solution.py:396
  77.8 0.6 collective-permute-start.18
  78.3 1.5 %collective-permute-start.20 = (bf16[3,3,8,384]{3,2,1,0:T(8,128)(2,1)S(1)}, bf16[3,3,8,384]{3,2,1,0:T(8,128)(2,1)S(1)}, u32[]{:S(2)}, u32[]{:S(2)}) collective-permute-start(bf16[3,3,8,384]{3,2,1,0:T(8,128)(2,1)S(1)} %get-tuple-element.93), channel_id=1, source_target_pairs={{0,4},{1,5},{2,6},{3,7},{4,8},{5,9},{6,10},{7,11},{8,12},{9,13},{1... | collective-permute-start | bytes 165896 | tf_op jit(solution)/shard_map/ppermute | solution.py:355
  79.9 0.4 collective-permute-start.21
  80.2 2.3 %collective-permute-done.19.refs_2_ = bf16[3,3,8,384]{3,2,1,0:T(8,128)(2,1)S(1)} collective-permute-done((bf16[3,3,8,384]{3,2,1,0:T(8,128)(2,1)S(1)}, bf16[3,3,8,384]{3,2,1,0:T(8,128)(2,1)S(1)}, u32[]{:S(2)}, u32[]{:S(2)}) %collective-permute-start.19) | collective-permute-done | bytes 55328 | tf_op jit(solution)/shard_map/ppermute | solution.py:355
  82.6 2.9 %collective-permute-done.20.refs_3_ = bf16[3,3,8,384]{3,2,1,0:T(8,128)(2,1)S(1)} collective-permute-done((bf16[3,3,8,384]{3,2,1,0:T(8,128)(2,1)S(1)}, bf16[3,3,8,384]{3,2,1,0:T(8,128)(2,1)S(1)}, u32[]{:S(2)}, u32[]{:S(2)}) %collective-permute-start.20) | collective-permute-done | bytes 55328 | tf_op jit(solution)/shard_map/ppermute | solution.py:355
  85.5 1.7 %collective-permute-done.21.refs_4_ = bf16[3,3,8,384]{3,2,1,0:T(8,128)(2,1)S(1)} collective-permute-done((bf16[3,3,8,384]{3,2,1,0:T(8,128)(2,1)S(1)}, bf16[3,3,8,384]{3,2,1,0:T(8,128)(2,1)S(1)}, u32[]{:S(2)}, u32[]{:S(2)}) %collective-permute-start.21) | collective-permute-done | bytes 55328 | tf_op jit(solution)/shard_map/ppermute | solution.py:355
  87.2 0.5 collective-permute-start.24
  87.7 1.9 %collective-permute-done.24.refs_11_ = bf16[4,104,384]{2,1,0:T(8,128)(2,1)S(1)} collective-permute-done((bf16[4,104,384]{2,1,0:T(8,128)(2,1)S(1)}, bf16[4,104,384]{2,1,0:T(8,128)(2,1)S(1)}, u32[]{:S(2)}, u32[]{:S(2)}) %collective-permute-start.24) | collective-permute-done | bytes 319520 | tf_op jit(solution)/shard_map/ppermute | solution.py:396
  89.7 0.5 collective-permute-done.25.refs_12_
  90.1 3.8 %shard_map.164 = (bf16[6,6,8,384]{3,2,1,0:T(8,128)(2,1)}, f32[384]{0:T(512)}, bf16[16,24,1152]{2,1,0:T(8,128)(2,1)}, bf16[16,24,384]{2,1,0:T(8,128)(2,1)}, f32[3...) custom-call(s32[5]{0:T(128)S(1)} %stack.29.refs_0_.me, ...), custom_call_target="tpu_custom_call" | custom-call | flops 589824 | bytes 7627796 | tf_op jit(solution)/shard_map/pallas_call | solution.py:337
  (46 shorter events, 1.0 us)
Async XLA Ops:
  0.6 12.4 %copy-start = (bf16[6,6,8,384]{3,2,1,0:T(8,128)(2,1)S(1)}, bf16[6,6,8,384]{3,2,1,0:T(8,128)(2,1)}, u32[]{:S(2)}) copy-start(bf16[6,6,8,384]{3,2,1,0:T(8,128)(2,1)} %tok.1) | copy-start | bytes 663556
  0.6 12.4 %copy-start.1 = (bf16[6,6,8,384]{3,2,1,0:T(8,128)(2,1)S(1)}, bf16[6,6,8,384]{3,2,1,0:T(8,128)(2,1)}, u32[]{:S(2)}) copy-start(bf16[6,6,8,384]{3,2,1,0:T(8,128)(2,1)} %up_own.1) | copy-start | bytes 663556
  0.7 12.4 %copy-start.2 = (f32[1536]{0:T(1024)S(1)}, f32[1536]{0:T(1024)}, u32[]{:S(2)}) copy-start(f32[1536]{0:T(1024)} %b_fc1.1) | copy-start | bytes 18436
  0.7 12.4 %copy-start.3 = (f32[384]{0:T(512)S(1)}, f32[384]{0:T(512)}, u32[]{:S(2)}) copy-start(f32[384]{0:T(512)} %gain2.1) | copy-start | bytes 4612
  0.7 12.4 %copy-start.4 = (f32[384]{0:T(512)S(1)}, f32[384]{0:T(512)}, u32[]{:S(2)}) copy-start(f32[384]{0:T(512)} %gain1.3) | copy-start | bytes 4612
  1.8 10.9 %collective-permute-start.2 = (bf16[2,3,3,8,384]{4,3,2,1,0:T(8,128)(2,1)S(1)}, bf16[2,3,3,8,384]{4,3,2,1,0:T(8,128)(2,1)S(1)}, u32[]{:S(2)}, u32[]{:S(2)}) collective-permute-start(bf16[2,3,3,8,384]{4,3,2,1,0:T(8,128)(2,1)S(1)} %get-tuple-element.116), channel_id=1, source_target_pairs={{0,31},{1,28},{2,29},{3,30},{4,3},{5,0},{6,1},{7,2},{8,7},{9,4},{1... | collective-permute-start | bytes 331784 | tf_op jit(solution)/shard_map/ppermute | solution.py:355
  8.2 4.9 %collective-permute-start.1 = (bf16[2,3,3,8,384]{4,3,2,1,0:T(8,128)(2,1)S(1)}, bf16[2,3,3,8,384]{4,3,2,1,0:T(8,128)(2,1)S(1)}, u32[]{:S(2)}, u32[]{:S(2)}) collective-permute-start(bf16[2,3,3,8,384]{4,3,2,1,0:T(8,128)(2,1)S(1)} %get-tuple-element.117), channel_id=1, source_target_pairs={{0,28},{1,29},{2,30},{3,31},{4,0},{5,1},{6,2},{7,3},{8,4},{9,5},{1... | collective-permute-start | bytes 331784 | tf_op jit(solution)/shard_map/ppermute | solution.py:355
  8.7 4.4 %collective-permute-start = (bf16[2,3,3,8,384]{4,3,2,1,0:T(8,128)(2,1)S(1)}, bf16[2,3,3,8,384]{4,3,2,1,0:T(8,128)(2,1)S(1)}, u32[]{:S(2)}, u32[]{:S(2)}) collective-permute-start(bf16[2,3,3,8,384]{4,3,2,1,0:T(8,128)(2,1)S(1)} %get-tuple-element.118), channel_id=1, source_target_pairs={{0,3},{1,0},{2,1},{3,2},{4,7},{5,4},{6,5},{7,6},{8,11},{9,8},{10,9... | collective-permute-start | bytes 331784 | tf_op jit(solution)/shard_map/ppermute | solution.py:355
  21.3 6.1 %collective-permute-start.3 = (bf16[8,192,384]{2,1,0:T(8,128)(2,1)S(1)}, bf16[8,192,384]{2,1,0:T(8,128)(2,1)S(1)}, u32[]{:S(2)}, u32[]{:S(2)}) collective-permute-start(bf16[8,192,384]{2,1,0:T(8,128)(2,1)S(1)} %get-tuple-element.72), channel_id=1, source_target_pairs={{0,1},{1,0},{2,3},{3,2},{4,5},{5,4},{6,7},{7,6},{8,9},{9,8},{10,11... | collective-permute-start | bytes 3538952 | tf_op jit(solution)/shard_map/ppermute | solution.py:396
  26.8 2.6 %collective-permute-start.5 = (bf16[8,104,384]{2,1,0:T(8,128)(2,1)S(1)}, bf16[8,104,384]{2,1,0:T(8,128)(2,1)S(1)}, u32[]{:S(2)}, u32[]{:S(2)}) collective-permute-start(bf16[8,104,384]{2,1,0:T(8,128)(2,1)S(1)} %get-tuple-element.75), channel_id=1, source_target_pairs={{0,1},{1,0},{2,3},{3,2},{4,5},{5,4},{6,7},{7,6},{8,9},{9,8},{10,11... | collective-permute-start | bytes 1916936 | tf_op jit(solution)/shard_map/ppermute | solution.py:396
  27.9 9.9 %collective-permute-start.4 = (bf16[4,192,384]{2,1,0:T(8,128)(2,1)S(1)}, bf16[4,192,384]{2,1,0:T(8,128)(2,1)S(1)}, u32[]{:S(2)}, u32[]{:S(2)}) collective-permute-start(bf16[4,192,384]{2,1,0:T(8,128)(2,1)S(1)} %get-tuple-element.108), channel_id=1, source_target_pairs={{0,2},{1,9},{2,0},{3,11},{4,6},{5,13},{6,4},{7,15},{8,10},{9,1},{1... | collective-permute-start | bytes 1769480 | tf_op jit(solution)/shard_map/ppermute | solution.py:396
  29.5 9.7 %collective-permute-start.7 = (bf16[4,104,384]{2,1,0:T(8,128)(2,1)S(1)}, bf16[4,104,384]{2,1,0:T(8,128)(2,1)S(1)}, u32[]{:S(2)}, u32[]{:S(2)}) collective-permute-start(bf16[4,104,384]{2,1,0:T(8,128)(2,1)S(1)} %get-tuple-element.111), channel_id=1, source_target_pairs={{0,4},{1,5},{2,6},{3,7},{4,0},{5,1},{6,2},{7,3},{8,12},{9,13},{10,... | collective-permute-start | bytes 958472 | tf_op jit(solution)/shard_map/ppermute | solution.py:396
  38.0 6.8 %collective-permute-start.6 = (bf16[2,192,384]{2,1,0:T(8,128)(2,1)S(1)}, bf16[2,192,384]{2,1,0:T(8,128)(2,1)S(1)}, u32[]{:S(2)}, u32[]{:S(2)}) collective-permute-start(bf16[2,192,384]{2,1,0:T(8,128)(2,1)S(1)} %get-tuple-element.112), channel_id=1, source_target_pairs={{0,4},{1,3},{2,6},{3,1},{4,0},{5,7},{6,2},{7,5},{8,12},{9,11},{10,... | collective-permute-start | bytes 884744 | tf_op jit(solution)/shard_map/ppermute | solution.py:396
  39.3 5.6 %collective-permute-start.9 = (bf16[2,104,384]{2,1,0:T(8,128)(2,1)S(1)}, bf16[2,104,384]{2,1,0:T(8,128)(2,1)S(1)}, u32[]{:S(2)}, u32[]{:S(2)}) collective-permute-start(bf16[2,104,384]{2,1,0:T(8,128)(2,1)S(1)} %get-tuple-element.115), channel_id=1, source_target_pairs={{0,8},{1,9},{2,10},{3,11},{4,12},{5,13},{6,14},{7,15},{8,0},{9,1},... | collective-permute-start | bytes 479240 | tf_op jit(solution)/shard_map/ppermute | solution.py:396
  44.8 5.2 %collective-permute-start.8 = (bf16[1,192,384]{2,1,0:T(8,128)(2,1)S(1)}, bf16[1,192,384]{2,1,0:T(8,128)(2,1)S(1)}, u32[]{:S(2)}, u32[]{:S(2)}) collective-permute-start(bf16[1,192,384]{2,1,0:T(8,128)(2,1)S(1)} %add_convert_fusion.10), channel_id=1, source_target_pairs={{0,8},{1,5},{2,10},{3,7},{4,12},{5,1},{6,14},{7,3},{8,0},{9,13},{1... | collective-permute-start | bytes 442376 | tf_op jit(solution)/shard_map/ppermute | solution.py:396
  44.9 7.5 %collective-permute-start.11 = (bf16[1,104,384]{2,1,0:T(8,128)(2,1)S(1)}, bf16[1,104,384]{2,1,0:T(8,128)(2,1)S(1)}, u32[]{:S(2)}, u32[]{:S(2)}) collective-permute-start(bf16[1,104,384]{2,1,0:T(8,128)(2,1)S(1)} %add_convert_fusion.15), channel_id=1, source_target_pairs={{0,2},{1,3},{2,0},{3,1},{4,6},{5,7},{6,4},{7,5},{8,10},{9,11},{10,... | collective-permute-start | bytes 239624 | tf_op jit(solution)/shard_map/ppermute | solution.py:396
  50.1 10.0 %collective-permute-start.10 = (bf16[192,384]{1,0:T(8,128)(2,1)S(1)}, bf16[192,384]{1,0:T(8,128)(2,1)S(1)}, u32[]{:S(2)}, u32[]{:S(2)}) collective-permute-start(bf16[192,384]{1,0:T(8,128)(2,1)S(1)} %fusion), channel_id=1, source_target_pairs={{0,16},{1,17},{2,18},{3,19},{4,20},{5,21},{6,22},{7,23},{8,24},{9,... | collective-permute-start | bytes 442376 | tf_op jit(solution)/shard_map/ppermute | solution.py:396
  52.4 8.5 %collective-permute-start.13 = (bf16[104,384]{1,0:T(8,128)(2,1)S(1)}, bf16[104,384]{1,0:T(8,128)(2,1)S(1)}, u32[]{:S(2)}, u32[]{:S(2)}) collective-permute-start(bf16[104,384]{1,0:T(8,128)(2,1)S(1)} %fusion.1), channel_id=1, source_target_pairs={{0,16},{1,17},{2,18},{3,19},{4,20},{5,21},{6,22},{7,23},{8,24},{9,... | collective-permute-start | bytes 239624 | tf_op jit(solution)/shard_map/ppermute | solution.py:396
  60.9 5.2 %collective-permute-start.12 = (bf16[1,192,384]{2,1,0:T(8,128)(2,1)S(1)}, bf16[1,192,384]{2,1,0:T(8,128)(2,1)S(1)}, u32[]{:S(2)}, u32[]{:S(2)}) collective-permute-start(bf16[1,192,384]{2,1,0:T(8,128)(2,1)S(1)} %bitcast.17), channel_id=1, source_target_pairs={{0,8},{1,5},{2,10},{3,7},{4,12},{5,1},{6,14},{7,3},{8,0},{9,13},{1... | collective-permute-start | bytes 442376 | tf_op jit(solution)/shard_map/ppermute | solution.py:396
  61.7 4.5 %collective-permute-start.14 = (bf16[1,104,384]{2,1,0:T(8,128)(2,1)S(1)}, bf16[1,104,384]{2,1,0:T(8,128)(2,1)S(1)}, u32[]{:S(2)}, u32[]{:S(2)}) collective-permute-start(bf16[1,104,384]{2,1,0:T(8,128)(2,1)S(1)} %fusion.2), channel_id=1, source_target_pairs={{0,2},{1,3},{2,0},{3,1},{4,6},{5,7},{6,4},{7,5},{8,10},{9,11},{10,... | collective-permute-start | bytes 239624 | tf_op jit(solution)/shard_map/ppermute | solution.py:396
  66.2 9.4 %collective-permute-start.15 = (bf16[2,192,384]{2,1,0:T(8,128)(2,1)S(1)}, bf16[2,192,384]{2,1,0:T(8,128)(2,1)S(1)}, u32[]{:S(2)}, u32[]{:S(2)}) collective-permute-start(bf16[2,192,384]{2,1,0:T(8,128)(2,1)S(1)} %pad_maximum_fusion.2), channel_id=1, source_target_pairs={{0,4},{1,3},{2,6},{3,1},{4,0},{5,7},{6,2},{7,5},{8,12},{9,11},{10,... | collective-permute-start | bytes 884744 | tf_op jit(solution)/shard_map/ppermute | solution.py:396
  68.8 6.7 %collective-permute-start.16 = (bf16[2,104,384]{2,1,0:T(8,128)(2,1)S(1)}, bf16[2,104,384]{2,1,0:T(8,128)(2,1)S(1)}, u32[]{:S(2)}, u32[]{:S(2)}) collective-permute-start(bf16[2,104,384]{2,1,0:T(8,128)(2,1)S(1)} %pad_maximum_fusion.3), channel_id=1, source_target_pairs={{0,8},{1,9},{2,10},{3,11},{4,12},{5,13},{6,14},{7,15},{8,0},{9,1},... | collective-permute-start | bytes 479240 | tf_op jit(solution)/shard_map/ppermute | solution.py:396
  75.6 11.6 %collective-permute-start.17 = (bf16[4,192,384]{2,1,0:T(8,128)(2,1)S(1)}, bf16[4,192,384]{2,1,0:T(8,128)(2,1)S(1)}, u32[]{:S(2)}, u32[]{:S(2)}) collective-permute-start(bf16[4,192,384]{2,1,0:T(8,128)(2,1)S(1)} %pad_maximum_fusion.refs_5_), channel_id=1, source_target_pairs={{0,2},{1,9},{2,0},{3,11},{4,6},{5,13},{6,4},{7,15},{8,10},{9,1},{1... | collective-permute-start | bytes 1769480 | tf_op jit(solution)/shard_map/ppermute | solution.py:396
  77.8 9.4 %collective-permute-start.18 = (bf16[4,104,384]{2,1,0:T(8,128)(2,1)S(1)}, bf16[4,104,384]{2,1,0:T(8,128)(2,1)S(1)}, u32[]{:S(2)}, u32[]{:S(2)}) collective-permute-start(bf16[4,104,384]{2,1,0:T(8,128)(2,1)S(1)} %pad_maximum_fusion.1.refs_9_), channel_id=1, source_target_pairs={{0,4},{1,5},{2,6},{3,7},{4,0},{5,1},{6,2},{7,3},{8,12},{9,13},{10,... | collective-permute-start | bytes 958472 | tf_op jit(solution)/shard_map/ppermute | solution.py:396
  78.3 4.2 %collective-permute-start.19 = (bf16[3,3,8,384]{3,2,1,0:T(8,128)(2,1)S(1)}, bf16[3,3,8,384]{3,2,1,0:T(8,128)(2,1)S(1)}, u32[]{:S(2)}, u32[]{:S(2)}) collective-permute-start(bf16[3,3,8,384]{3,2,1,0:T(8,128)(2,1)S(1)} %get-tuple-element.92), channel_id=1, source_target_pairs={{0,1},{1,2},{2,3},{3,0},{4,5},{5,6},{6,7},{7,4},{8,9},{9,10},{10,1... | collective-permute-start | bytes 165896 | tf_op jit(solution)/shard_map/ppermute | solution.py:355
  78.3 7.1 %collective-permute-start.20 = (bf16[3,3,8,384]{3,2,1,0:T(8,128)(2,1)S(1)}, bf16[3,3,8,384]{3,2,1,0:T(8,128)(2,1)S(1)}, u32[]{:S(2)}, u32[]{:S(2)}) collective-permute-start(bf16[3,3,8,384]{3,2,1,0:T(8,128)(2,1)S(1)} %get-tuple-element.93), channel_id=1, source_target_pairs={{0,4},{1,5},{2,6},{3,7},{4,8},{5,9},{6,10},{7,11},{8,12},{9,13},{1... | collective-permute-start | bytes 165896 | tf_op jit(solution)/shard_map/ppermute | solution.py:355
  79.9 7.3 %collective-permute-start.21 = (bf16[3,3,8,384]{3,2,1,0:T(8,128)(2,1)S(1)}, bf16[3,3,8,384]{3,2,1,0:T(8,128)(2,1)S(1)}, u32[]{:S(2)}, u32[]{:S(2)}) collective-permute-start(bf16[3,3,8,384]{3,2,1,0:T(8,128)(2,1)S(1)} %get-tuple-element.94), channel_id=1, source_target_pairs={{0,5},{1,6},{2,7},{3,4},{4,9},{5,10},{6,11},{7,8},{8,13},{9,14},{1... | collective-permute-start | bytes 165896 | tf_op jit(solution)/shard_map/ppermute | solution.py:355
  82.6 7.1 %collective-permute-start.22 = (bf16[4,192,384]{2,1,0:T(8,128)(2,1)S(1)}, bf16[4,192,384]{2,1,0:T(8,128)(2,1)S(1)}, u32[]{:S(2)}, u32[]{:S(2)}) collective-permute-start(bf16[4,192,384]{2,1,0:T(8,128)(2,1)S(1)} %pad_maximum_fusion.refs_5_), channel_id=1, source_target_pairs={{0,1},{1,0},{2,3},{3,2},{4,5},{5,4},{6,7},{7,6},{8,9},{9,8},{10,11... | collective-permute-start | bytes 1769480 | tf_op jit(solution)/shard_map/ppermute | solution.py:396
  87.2 2.9 %collective-permute-start.23 = (bf16[4,192,384]{2,1,0:T(8,128)(2,1)S(1)}, bf16[4,192,384]{2,1,0:T(8,128)(2,1)S(1)}, u32[]{:S(2)}, u32[]{:S(2)}) collective-permute-start(bf16[4,192,384]{2,1,0:T(8,128)(2,1)S(1)} %collective-permute-done.17.refs_6_), channel_id=1, source_target_pairs={{0,1},{1,0},{2,3},{3,2},{4,5},{5,4},{6,7},{7,6},{8,9},{9,8},{10,11... | collective-permute-start | bytes 1769480 | tf_op jit(solution)/shard_map/ppermute | solution.py:396
  87.2 2.5 %collective-permute-start.24 = (bf16[4,104,384]{2,1,0:T(8,128)(2,1)S(1)}, bf16[4,104,384]{2,1,0:T(8,128)(2,1)S(1)}, u32[]{:S(2)}, u32[]{:S(2)}) collective-permute-start(bf16[4,104,384]{2,1,0:T(8,128)(2,1)S(1)} %pad_maximum_fusion.1.refs_9_), channel_id=1, source_target_pairs={{0,1},{1,0},{2,3},{3,2},{4,5},{5,4},{6,7},{7,6},{8,9},{9,8},{10,11... | collective-permute-start | bytes 958472 | tf_op jit(solution)/shard_map/ppermute | solution.py:396
  87.7 2.4 %collective-permute-start.25 = (bf16[4,104,384]{2,1,0:T(8,128)(2,1)S(1)}, bf16[4,104,384]{2,1,0:T(8,128)(2,1)S(1)}, u32[]{:S(2)}, u32[]{:S(2)}) collective-permute-start(bf16[4,104,384]{2,1,0:T(8,128)(2,1)S(1)} %collective-permute-done.18.refs_10_), channel_id=1, source_target_pairs={{0,1},{1,0},{2,3},{3,2},{4,5},{5,4},{6,7},{7,6},{8,9},{9,8},{10,11... | collective-permute-start | bytes 958472 | tf_op jit(solution)/shard_map/ppermute | solution.py:396

commit v5 on v4

--- a/solution.py
+++ b/solution.py
@@ -450,9 +450,14 @@
     order, order_t = ORDERS
     got_t, = after([swap(send_t, CORE)], send)
     keep_t, send_t = fold(keep_t, got_t)
+    homes, back = ((0, 1), (1, 0), (1, 1)), []
     for step in range(3):
         got_t = swap(send_t, order_t[step])
-        got, = after([got], send_t)
+        if step < 2:
+            got, home = after([got, neighbour(away[step], *homes[step])], send_t)
+            back.append(home)
+        else:
+            got, = after([got], send_t)
         if step < 2:
             keep, send = fold(keep, got)
             got = swap(send, order[step + 1])
@@ -464,15 +469,16 @@
             low_t = add(keep_t[0], got_t[0]).astype(BF16)
     for flips in spares():
         got, got_t = swap(low, flips), swap(low_t, flips)
+        if len(back) == 2:
+            got, home = lax.optimization_barrier((got, neighbour(away[2], *homes[2])))
+            back.append(home)
         low = add(low, after([got], low_t)[0]).astype(BF16)
         low_t = add(low_t, after([got_t], low)[0]).astype(BF16)
     parts, parts_t = low[None], low_t[None]
     for step in (2, 1, 0):
         more, more_t = swap(parts, order[step]), swap(parts_t, order_t[step])
         if step == 0:
-            away = after(away, parts)
-            back = [neighbour(away[0], 0, 1), neighbour(away[1], 1, 0), neighbour(away[2], 1, 1)]
-            more, more_t, *back = lax.optimization_barrier((more, more_t, *back))
+            more, more_t = lax.optimization_barrier((more, more_t))
             break
         more, more_t = lax.optimization_barrier((more, more_t))
         parts, parts_t = jnp.concatenate([parts, more]), jnp.concatenate([parts_t, more_t])

time: 94.3 us -> 92.5 us (0.981)
  starting transfers between devices: 29.2 us -> 27.1 us
    ppermute x6, waiting for transfers between devices: 7.24 us -> 9.35 us  [neighbour(): return lax.ppermute(shard, ('gx', 'gy'), pairs)]
    ppermute x20, waiting for transfers between devices: 33.5 us -> 31.6 us  [swap(): return lax.ppermute(shard, ('gx', 'gy'), pairs)]
    ppermute x6, starting transfers between devices: 9.4 us -> 8.33 us  [neighbour(): return lax.ppermute(shard, ('gx', 'gy'), pairs)]
    ppermute x20, starting transfers between devices: 19.8 us -> 18.8 us  [swap(): return lax.ppermute(shard, ('gx', 'gy'), pairs)]
where the time goes in v5:
time: 92.5 us; the launch traced here: 92.2 us
  waiting for transfers between devices  41 us (44%)
  starting transfers between devices  27.1 us (29%)
  Pallas kernels  19.2 us (21%)
  other arithmetic  3.34 us (4%)
  between operations  1.03 us (1%)
    ppermute x20, waiting for transfers between devices, swap(): return lax.ppermute(shard, ('gx', 'gy'), pairs)  31.6 us
    pallas_call x4, Pallas kernels, call(): pl.pallas_call(kernel, out_shape=outs, in_specs=[SMEM] + [VMEM] * len(nea...  19.2 us
    ppermute x20, starting transfers between devices, swap(): return lax.ppermute(shard, ('gx', 'gy'), pairs)  18.8 us
    ppermute x6, waiting for transfers between devices, neighbour(): return lax.ppermute(shard, ('gx', 'gy'), pairs)  9.35 us
    ppermute x6, starting transfers between devices, neighbour(): return lax.ppermute(shard, ('gx', 'gy'), pairs)  8.33 us
  transfers between devices with their start and end apart: 26, of which 14 were waited for; matrix products, arithmetic and copies ran while one was open for 3% of the time, Pallas kernels for 8%

profile of v5, /device:TPU:0, one launch (start us, length us, event | category | flops | bytes accessed | tf_op | source)
XLA Modules:
  0.0 92.2 jit_solution(2900488442801968996)
XLA Ops:
  0.7 1.1 %pad_maximum_fusion.4 = (bf16[2,3,3,8,384]{4,3,2,1,0:T(8,128)(2,1)S(1)}, bf16[2,3,3,8,384]{4,3,2,1,0:T(8,128)(2,1)S(1)}, bf16[2,3,3,8,384]{4,3,2,1,0:T(8,128)(2,1)S(1)}) fusion(bf16[1,6,6,8,384]{4,3,2,1,0:T(8,128)(2,1)} %bitcast.16, bf16[1,6,6,8,384]{4,3,2,1,0:T(8,128)(2,1)} %bitcast.15), kind=kLoop, calls=%fused_computation.21 | loop fusion | flops 165888 | bytes 774144 | tf_op jit(solution)/shard_map/stack | solution.py:492
  1.8 6.4 %collective-permute-start.2 = (bf16[2,3,3,8,384]{4,3,2,1,0:T(8,128)(2,1)S(1)}, bf16[2,3,3,8,384]{4,3,2,1,0:T(8,128)(2,1)S(1)}, u32[]{:S(2)}, u32[]{:S(2)}) collective-permute-start(bf16[2,3,3,8,384]{4,3,2,1,0:T(8,128)(2,1)S(1)} %get-tuple-element.112), channel_id=1, source_target_pairs={{0,31},{1,28},{2,29},{3,30},{4,3},{5,0},{6,1},{7,2},{8,7},{9,4},{1... | collective-permute-start | bytes 331784 | tf_op jit(solution)/shard_map/ppermute | solution.py:355
  8.2 0.5 collective-permute-start.1
  8.7 0.6 collective-permute-start
  9.3 0.8 add_add_fusion
  10.2 0.1 reshape.59
  10.3 0.1 reshape.60
  10.4 0.1 reshape.62
  10.5 0.1 reshape.61
  10.7 0.1 broadcast_in_dim.19.code_col
  10.8 0.1 stack.29.refs_0_.me
  10.9 1.8 %shard_map.161 = (bf16[384,1152]{1,0:T(8,128)(2,1)S(1)}, bf16[384,384]{1,0:T(8,128)(2,1)S(1)}) custom-call(s32[5]{0:T(128)S(1)} %stack.29.refs_0_.me, bf16[384,1152]{1,0:T(8,128)(2,1)} %refs_1_.1, bf16[384,384]{1,0:T(8,128)(2,1)} %refs_2_.1), custom_call_target="tpu_custom_call" | custom-call | bytes 2359316 | tf_op jit(solution)/shard_map/pallas_call | solution.py:337
  12.7 0.4 collective-permute-done.1.part_c
  13.1 8.2 %shard_map.162 = (bf16[8,192,384]{2,1,0:T(8,128)(2,1)S(1)}, bf16[8,192,384]{2,1,0:T(8,128)(2,1)S(1)}, f32[5,384]{1,0:T(8,128)S(1)}, f32[288,384]{1,0:T(8,128)S(1...) custom-call(s32[5]{0:T(128)S(1)} %stack.29.refs_0_.me, ...), custom_call_target="tpu_custom_call" | custom-call | flops 2548039680 | bytes 10674068 | tf_op jit(solution)/shard_map/pallas_call | solution.py:337
  21.4 5.4 %shard_map.163 = (bf16[3,3,8,384]{3,2,1,0:T(8,128)(2,1)S(1)}, bf16[3,3,8,384]{3,2,1,0:T(8,128)(2,1)S(1)}, bf16[3,3,8,384]{3,2,1,0:T(8,128)(2,1)S(1)}, bf16[3,3,8...) custom-call(s32[5]{0:T(128)S(1)} %stack.29.refs_0_.me, ...), custom_call_target="tpu_custom_call" | custom-call | flops 1698693120 | bytes 6670484 | tf_op jit(solution)/shard_map/pallas_call | solution.py:337
  26.8 0.6 collective-permute-start.6
  27.4 0.5 add_convert_fusion
  27.9 1.5 %collective-permute-start.4 = (bf16[4,192,384]{2,1,0:T(8,128)(2,1)S(1)}, bf16[4,192,384]{2,1,0:T(8,128)(2,1)S(1)}, u32[]{:S(2)}, u32[]{:S(2)}) collective-permute-start(bf16[4,192,384]{2,1,0:T(8,128)(2,1)S(1)} %get-tuple-element.105), channel_id=1, source_target_pairs={{0,2},{1,9},{2,0},{3,11},{4,6},{5,13},{6,4},{7,15},{8,10},{9,1},{1... | collective-permute-start | bytes 1769480 | tf_op jit(solution)/shard_map/ppermute | solution.py:396
  29.4 0.2 add_convert_fusion.2
  29.5 0.9 %collective-permute-start.9 = (bf16[4,104,384]{2,1,0:T(8,128)(2,1)S(1)}, bf16[4,104,384]{2,1,0:T(8,128)(2,1)S(1)}, u32[]{:S(2)}, u32[]{:S(2)}) collective-permute-start(bf16[4,104,384]{2,1,0:T(8,128)(2,1)S(1)} %get-tuple-element.107), channel_id=1, source_target_pairs={{0,4},{1,5},{2,6},{3,7},{4,0},{5,1},{6,2},{7,3},{8,12},{9,13},{10,... | collective-permute-start | bytes 958472 | tf_op jit(solution)/shard_map/ppermute | solution.py:396
  30.5 3.0 %collective-permute-done.5.refs_2_ = bf16[3,3,8,384]{3,2,1,0:T(8,128)(2,1)S(1)} collective-permute-done((bf16[3,3,8,384]{3,2,1,0:T(8,128)(2,1)S(1)}, bf16[3,3,8,384]{3,2,1,0:T(8,128)(2,1)S(1)}, u32[]{:S(2)}, u32[]{:S(2)}) %collective-permute-start.5) | collective-permute-done | bytes 55328 | tf_op jit(solution)/shard_map/ppermute | solution.py:355
  33.5 4.9 %collective-permute-done.4 = bf16[4,192,384]{2,1,0:T(8,128)(2,1)S(1)} collective-permute-done((bf16[4,192,384]{2,1,0:T(8,128)(2,1)S(1)}, bf16[4,192,384]{2,1,0:T(8,128)(2,1)S(1)}, u32[]{:S(2)}, u32[]{:S(2)}) %collective-permute-start.4) | collective-permute-done | bytes 589856 | tf_op jit(solution)/shard_map/ppermute | solution.py:396
  38.4 0.2 add_convert_fusion.4
  38.6 1.3 %collective-permute-start.7 = (bf16[2,192,384]{2,1,0:T(8,128)(2,1)S(1)}, bf16[2,192,384]{2,1,0:T(8,128)(2,1)S(1)}, u32[]{:S(2)}, u32[]{:S(2)}) collective-permute-start(bf16[2,192,384]{2,1,0:T(8,128)(2,1)S(1)} %get-tuple-element.109), channel_id=1, source_target_pairs={{0,4},{1,3},{2,6},{3,1},{4,0},{5,7},{6,2},{7,5},{8,12},{9,11},{10,... | collective-permute-start | bytes 884744 | tf_op jit(solution)/shard_map/ppermute | solution.py:396
  39.8 0.8 collective-permute-start.8
  40.8 6.0 %collective-permute-done.8.refs_3_ = bf16[3,3,8,384]{3,2,1,0:T(8,128)(2,1)S(1)} collective-permute-done((bf16[3,3,8,384]{3,2,1,0:T(8,128)(2,1)S(1)}, bf16[3,3,8,384]{3,2,1,0:T(8,128)(2,1)S(1)}, u32[]{:S(2)}, u32[]{:S(2)}) %collective-permute-start.8) | collective-permute-done | bytes 55328 | tf_op jit(solution)/shard_map/ppermute | solution.py:355
  46.8 0.9 %collective-permute-start.10 = (bf16[1,192,384]{2,1,0:T(8,128)(2,1)S(1)}, bf16[1,192,384]{2,1,0:T(8,128)(2,1)S(1)}, u32[]{:S(2)}, u32[]{:S(2)}) collective-permute-start(bf16[1,192,384]{2,1,0:T(8,128)(2,1)S(1)} %add_convert_fusion.10), channel_id=1, source_target_pairs={{0,8},{1,5},{2,10},{3,7},{4,12},{5,1},{6,14},{7,3},{8,0},{9,13},{1... | collective-permute-start | bytes 442376 | tf_op jit(solution)/shard_map/ppermute | solution.py:396
  47.8 1.1 %collective-permute-start.14 = (bf16[1,104,384]{2,1,0:T(8,128)(2,1)S(1)}, bf16[1,104,384]{2,1,0:T(8,128)(2,1)S(1)}, u32[]{:S(2)}, u32[]{:S(2)}) collective-permute-start(bf16[1,104,384]{2,1,0:T(8,128)(2,1)S(1)} %add_convert_fusion.15), channel_id=1, source_target_pairs={{0,2},{1,3},{2,0},{3,1},{4,6},{5,7},{6,4},{7,5},{8,10},{9,11},{10,... | collective-permute-start | bytes 239624 | tf_op jit(solution)/shard_map/ppermute | solution.py:396
  48.8 3.2 %collective-permute-done.10 = bf16[1,192,384]{2,1,0:T(8,128)(2,1)S(1)} collective-permute-done((bf16[1,192,384]{2,1,0:T(8,128)(2,1)S(1)}, bf16[1,192,384]{2,1,0:T(8,128)(2,1)S(1)}, u32[]{:S(2)}, u32[]{:S(2)}) %collective-permute-start.10) | collective-permute-done | bytes 147488 | tf_op jit(solution)/shard_map/ppermute | solution.py:396
  52.1 2.7 %collective-permute-start.12 = (bf16[192,384]{1,0:T(8,128)(2,1)S(1)}, bf16[192,384]{1,0:T(8,128)(2,1)S(1)}, u32[]{:S(2)}, u32[]{:S(2)}) collective-permute-start(bf16[192,384]{1,0:T(8,128)(2,1)S(1)} %fusion), channel_id=1, source_target_pairs={{0,16},{1,17},{2,18},{3,19},{4,20},{5,21},{6,22},{7,23},{8,24},{9,... | collective-permute-start | bytes 442376 | tf_op jit(solution)/shard_map/ppermute | solution.py:396
  54.9 1.3 %collective-permute-start.16 = (bf16[104,384]{1,0:T(8,128)(2,1)S(1)}, bf16[104,384]{1,0:T(8,128)(2,1)S(1)}, u32[]{:S(2)}, u32[]{:S(2)}) collective-permute-start(bf16[104,384]{1,0:T(8,128)(2,1)S(1)} %fusion.1), channel_id=1, source_target_pairs={{0,16},{1,17},{2,18},{3,19},{4,20},{5,21},{6,22},{7,23},{8,24},{9,... | collective-permute-start | bytes 239624 | tf_op jit(solution)/shard_map/ppermute | solution.py:396
  56.2 6.0 %collective-permute-done.12 = bf16[192,384]{1,0:T(8,128)(2,1)S(1)} collective-permute-done((bf16[192,384]{1,0:T(8,128)(2,1)S(1)}, bf16[192,384]{1,0:T(8,128)(2,1)S(1)}, u32[]{:S(2)}, u32[]{:S(2)}) %collective-permute-start.12) | collective-permute-done | bytes 147488 | tf_op jit(solution)/shard_map/ppermute | solution.py:396
  62.2 0.8 collective-permute-done.16
  63.1 0.3 collective-permute-start.15
  63.4 0.9 %collective-permute-start.17 = (bf16[1,104,384]{2,1,0:T(8,128)(2,1)S(1)}, bf16[1,104,384]{2,1,0:T(8,128)(2,1)S(1)}, u32[]{:S(2)}, u32[]{:S(2)}) collective-permute-start(bf16[1,104,384]{2,1,0:T(8,128)(2,1)S(1)} %fusion.2), channel_id=1, source_target_pairs={{0,2},{1,3},{2,0},{3,1},{4,6},{5,7},{6,4},{7,5},{8,10},{9,11},{10,... | collective-permute-start | bytes 239624 | tf_op jit(solution)/shard_map/ppermute | solution.py:396
  64.3 3.6 %collective-permute-done.17 = bf16[1,104,384]{2,1,0:T(8,128)(2,1)S(1)} collective-permute-done((bf16[1,104,384]{2,1,0:T(8,128)(2,1)S(1)}, bf16[1,104,384]{2,1,0:T(8,128)(2,1)S(1)}, u32[]{:S(2)}, u32[]{:S(2)}) %collective-permute-start.17) | collective-permute-done | bytes 79904 | tf_op jit(solution)/shard_map/ppermute | solution.py:396
  67.9 0.3 collective-permute-done.15
  68.2 1.7 %collective-permute-start.18 = (bf16[2,192,384]{2,1,0:T(8,128)(2,1)S(1)}, bf16[2,192,384]{2,1,0:T(8,128)(2,1)S(1)}, u32[]{:S(2)}, u32[]{:S(2)}) collective-permute-start(bf16[2,192,384]{2,1,0:T(8,128)(2,1)S(1)} %pad_maximum_fusion.2), channel_id=1, source_target_pairs={{0,4},{1,3},{2,6},{3,1},{4,0},{5,7},{6,2},{7,5},{8,12},{9,11},{10,... | collective-permute-start | bytes 884744 | tf_op jit(solution)/shard_map/ppermute | solution.py:396
  70.0 1.7 %collective-permute-start.19 = (bf16[2,104,384]{2,1,0:T(8,128)(2,1)S(1)}, bf16[2,104,384]{2,1,0:T(8,128)(2,1)S(1)}, u32[]{:S(2)}, u32[]{:S(2)}) collective-permute-start(bf16[2,104,384]{2,1,0:T(8,128)(2,1)S(1)} %pad_maximum_fusion.3), channel_id=1, source_target_pairs={{0,8},{1,9},{2,10},{3,11},{4,12},{5,13},{6,14},{7,15},{8,0},{9,1},... | collective-permute-start | bytes 479240 | tf_op jit(solution)/shard_map/ppermute | solution.py:396
  71.7 3.6 %collective-permute-done.19 = bf16[2,104,384]{2,1,0:T(8,128)(2,1)S(1)} collective-permute-done((bf16[2,104,384]{2,1,0:T(8,128)(2,1)S(1)}, bf16[2,104,384]{2,1,0:T(8,128)(2,1)S(1)}, u32[]{:S(2)}, u32[]{:S(2)}) %collective-permute-start.19) | collective-permute-done | bytes 159776 | tf_op jit(solution)/shard_map/ppermute | solution.py:396
  75.4 1.6 %collective-permute-start.20 = (bf16[4,192,384]{2,1,0:T(8,128)(2,1)S(1)}, bf16[4,192,384]{2,1,0:T(8,128)(2,1)S(1)}, u32[]{:S(2)}, u32[]{:S(2)}) collective-permute-start(bf16[4,192,384]{2,1,0:T(8,128)(2,1)S(1)} %pad_maximum_fusion.refs_5_), channel_id=1, source_target_pairs={{0,2},{1,9},{2,0},{3,11},{4,6},{5,13},{6,4},{7,15},{8,10},{9,1},{1... | collective-permute-start | bytes 1769480 | tf_op jit(solution)/shard_map/ppermute | solution.py:396
  77.1 1.4 %collective-permute-start.21 = (bf16[4,104,384]{2,1,0:T(8,128)(2,1)S(1)}, bf16[4,104,384]{2,1,0:T(8,128)(2,1)S(1)}, u32[]{:S(2)}, u32[]{:S(2)}) collective-permute-start(bf16[4,104,384]{2,1,0:T(8,128)(2,1)S(1)} %pad_maximum_fusion.1.refs_9_), channel_id=1, source_target_pairs={{0,4},{1,5},{2,6},{3,7},{4,0},{5,1},{6,2},{7,3},{8,12},{9,13},{10,... | collective-permute-start | bytes 958472 | tf_op jit(solution)/shard_map/ppermute | solution.py:396
  78.5 5.6 %collective-permute-done.21.refs_10_ = bf16[4,104,384]{2,1,0:T(8,128)(2,1)S(1)} collective-permute-done((bf16[4,104,384]{2,1,0:T(8,128)(2,1)S(1)}, bf16[4,104,384]{2,1,0:T(8,128)(2,1)S(1)}, u32[]{:S(2)}, u32[]{:S(2)}) %collective-permute-start.21) | collective-permute-done | bytes 319520 | tf_op jit(solution)/shard_map/ppermute | solution.py:396
  84.2 1.2 %collective-permute-done.20.refs_6_ = bf16[4,192,384]{2,1,0:T(8,128)(2,1)S(1)} collective-permute-done((bf16[4,192,384]{2,1,0:T(8,128)(2,1)S(1)}, bf16[4,192,384]{2,1,0:T(8,128)(2,1)S(1)}, u32[]{:S(2)}, u32[]{:S(2)}) %collective-permute-start.20) | collective-permute-done | bytes 589856 | tf_op jit(solution)/shard_map/ppermute | solution.py:396
  85.4 0.5 collective-permute-start.24
  85.9 1.9 %collective-permute-done.24.refs_11_ = bf16[4,104,384]{2,1,0:T(8,128)(2,1)S(1)} collective-permute-done((bf16[4,104,384]{2,1,0:T(8,128)(2,1)S(1)}, bf16[4,104,384]{2,1,0:T(8,128)(2,1)S(1)}, u32[]{:S(2)}, u32[]{:S(2)}) %collective-permute-start.24) | collective-permute-done | bytes 319520 | tf_op jit(solution)/shard_map/ppermute | solution.py:396
  87.8 0.5 collective-permute-done.25.refs_12_
  88.3 3.8 %shard_map.164 = (bf16[6,6,8,384]{3,2,1,0:T(8,128)(2,1)}, f32[384]{0:T(512)}, bf16[16,24,1152]{2,1,0:T(8,128)(2,1)}, bf16[16,24,384]{2,1,0:T(8,128)(2,1)}, f32[3...) custom-call(s32[5]{0:T(128)S(1)} %stack.29.refs_0_.me, ...), custom_call_target="tpu_custom_call" | custom-call | flops 589824 | bytes 7627796 | tf_op jit(solution)/shard_map/pallas_call | solution.py:337
  (46 shorter events, 0.9 us)
Async XLA Ops:
  0.6 12.4 %copy-start = (bf16[6,6,8,384]{3,2,1,0:T(8,128)(2,1)S(1)}, bf16[6,6,8,384]{3,2,1,0:T(8,128)(2,1)}, u32[]{:S(2)}) copy-start(bf16[6,6,8,384]{3,2,1,0:T(8,128)(2,1)} %tok.1) | copy-start | bytes 663556
  0.6 12.4 %copy-start.1 = (bf16[6,6,8,384]{3,2,1,0:T(8,128)(2,1)S(1)}, bf16[6,6,8,384]{3,2,1,0:T(8,128)(2,1)}, u32[]{:S(2)}) copy-start(bf16[6,6,8,384]{3,2,1,0:T(8,128)(2,1)} %up_own.1) | copy-start | bytes 663556
  0.7 12.4 %copy-start.2 = (f32[1536]{0:T(1024)S(1)}, f32[1536]{0:T(1024)}, u32[]{:S(2)}) copy-start(f32[1536]{0:T(1024)} %b_fc1.1) | copy-start | bytes 18436
  0.7 12.4 %copy-start.3 = (f32[384]{0:T(512)S(1)}, f32[384]{0:T(512)}, u32[]{:S(2)}) copy-start(f32[384]{0:T(512)} %gain2.1) | copy-start | bytes 4612
  0.7 12.4 %copy-start.4 = (f32[384]{0:T(512)S(1)}, f32[384]{0:T(512)}, u32[]{:S(2)}) copy-start(f32[384]{0:T(512)} %gain1.3) | copy-start | bytes 4612
  1.8 10.9 %collective-permute-start.2 = (bf16[2,3,3,8,384]{4,3,2,1,0:T(8,128)(2,1)S(1)}, bf16[2,3,3,8,384]{4,3,2,1,0:T(8,128)(2,1)S(1)}, u32[]{:S(2)}, u32[]{:S(2)}) collective-permute-start(bf16[2,3,3,8,384]{4,3,2,1,0:T(8,128)(2,1)S(1)} %get-tuple-element.112), channel_id=1, source_target_pairs={{0,31},{1,28},{2,29},{3,30},{4,3},{5,0},{6,1},{7,2},{8,7},{9,4},{1... | collective-permute-start | bytes 331784 | tf_op jit(solution)/shard_map/ppermute | solution.py:355
  8.2 4.9 %collective-permute-start.1 = (bf16[2,3,3,8,384]{4,3,2,1,0:T(8,128)(2,1)S(1)}, bf16[2,3,3,8,384]{4,3,2,1,0:T(8,128)(2,1)S(1)}, u32[]{:S(2)}, u32[]{:S(2)}) collective-permute-start(bf16[2,3,3,8,384]{4,3,2,1,0:T(8,128)(2,1)S(1)} %get-tuple-element.113), channel_id=1, source_target_pairs={{0,28},{1,29},{2,30},{3,31},{4,0},{5,1},{6,2},{7,3},{8,4},{9,5},{1... | collective-permute-start | bytes 331784 | tf_op jit(solution)/shard_map/ppermute | solution.py:355
  8.7 4.4 %collective-permute-start = (bf16[2,3,3,8,384]{4,3,2,1,0:T(8,128)(2,1)S(1)}, bf16[2,3,3,8,384]{4,3,2,1,0:T(8,128)(2,1)S(1)}, u32[]{:S(2)}, u32[]{:S(2)}) collective-permute-start(bf16[2,3,3,8,384]{4,3,2,1,0:T(8,128)(2,1)S(1)} %get-tuple-element.114), channel_id=1, source_target_pairs={{0,3},{1,0},{2,1},{3,2},{4,7},{5,4},{6,5},{7,6},{8,11},{9,8},{10,9... | collective-permute-start | bytes 331784 | tf_op jit(solution)/shard_map/ppermute | solution.py:355
  21.3 6.1 %collective-permute-start.3 = (bf16[8,192,384]{2,1,0:T(8,128)(2,1)S(1)}, bf16[8,192,384]{2,1,0:T(8,128)(2,1)S(1)}, u32[]{:S(2)}, u32[]{:S(2)}) collective-permute-start(bf16[8,192,384]{2,1,0:T(8,128)(2,1)S(1)} %get-tuple-element.70), channel_id=1, source_target_pairs={{0,1},{1,0},{2,3},{3,2},{4,5},{5,4},{6,7},{7,6},{8,9},{9,8},{10,11... | collective-permute-start | bytes 3538952 | tf_op jit(solution)/shard_map/ppermute | solution.py:396
  26.8 2.6 %collective-permute-start.6 = (bf16[8,104,384]{2,1,0:T(8,128)(2,1)S(1)}, bf16[8,104,384]{2,1,0:T(8,128)(2,1)S(1)}, u32[]{:S(2)}, u32[]{:S(2)}) collective-permute-start(bf16[8,104,384]{2,1,0:T(8,128)(2,1)S(1)} %get-tuple-element.74), channel_id=1, source_target_pairs={{0,1},{1,0},{2,3},{3,2},{4,5},{5,4},{6,7},{7,6},{8,9},{9,8},{10,11... | collective-permute-start | bytes 1916936 | tf_op jit(solution)/shard_map/ppermute | solution.py:396
  27.9 10.5 %collective-permute-start.4 = (bf16[4,192,384]{2,1,0:T(8,128)(2,1)S(1)}, bf16[4,192,384]{2,1,0:T(8,128)(2,1)S(1)}, u32[]{:S(2)}, u32[]{:S(2)}) collective-permute-start(bf16[4,192,384]{2,1,0:T(8,128)(2,1)S(1)} %get-tuple-element.105), channel_id=1, source_target_pairs={{0,2},{1,9},{2,0},{3,11},{4,6},{5,13},{6,4},{7,15},{8,10},{9,1},{1... | collective-permute-start | bytes 1769480 | tf_op jit(solution)/shard_map/ppermute | solution.py:396
  29.4 4.2 %collective-permute-start.5 = (bf16[3,3,8,384]{3,2,1,0:T(8,128)(2,1)S(1)}, bf16[3,3,8,384]{3,2,1,0:T(8,128)(2,1)S(1)}, u32[]{:S(2)}, u32[]{:S(2)}) collective-permute-start(bf16[3,3,8,384]{3,2,1,0:T(8,128)(2,1)S(1)} %get-tuple-element.73), channel_id=1, source_target_pairs={{0,1},{1,2},{2,3},{3,0},{4,5},{5,6},{6,7},{7,4},{8,9},{9,10},{10,1... | collective-permute-start | bytes 165896 | tf_op jit(solution)/shard_map/ppermute | solution.py:355
  29.5 11.1 %collective-permute-start.9 = (bf16[4,104,384]{2,1,0:T(8,128)(2,1)S(1)}, bf16[4,104,384]{2,1,0:T(8,128)(2,1)S(1)}, u32[]{:S(2)}, u32[]{:S(2)}) collective-permute-start(bf16[4,104,384]{2,1,0:T(8,128)(2,1)S(1)} %get-tuple-element.107), channel_id=1, source_target_pairs={{0,4},{1,5},{2,6},{3,7},{4,0},{5,1},{6,2},{7,3},{8,12},{9,13},{10,... | collective-permute-start | bytes 958472 | tf_op jit(solution)/shard_map/ppermute | solution.py:396
  38.6 8.2 %collective-permute-start.7 = (bf16[2,192,384]{2,1,0:T(8,128)(2,1)S(1)}, bf16[2,192,384]{2,1,0:T(8,128)(2,1)S(1)}, u32[]{:S(2)}, u32[]{:S(2)}) collective-permute-start(bf16[2,192,384]{2,1,0:T(8,128)(2,1)S(1)} %get-tuple-element.109), channel_id=1, source_target_pairs={{0,4},{1,3},{2,6},{3,1},{4,0},{5,7},{6,2},{7,5},{8,12},{9,11},{10,... | collective-permute-start | bytes 884744 | tf_op jit(solution)/shard_map/ppermute | solution.py:396
  39.8 7.0 %collective-permute-start.8 = (bf16[3,3,8,384]{3,2,1,0:T(8,128)(2,1)S(1)}, bf16[3,3,8,384]{3,2,1,0:T(8,128)(2,1)S(1)}, u32[]{:S(2)}, u32[]{:S(2)}) collective-permute-start(bf16[3,3,8,384]{3,2,1,0:T(8,128)(2,1)S(1)} %get-tuple-element.78), channel_id=1, source_target_pairs={{0,4},{1,5},{2,6},{3,7},{4,8},{5,9},{6,10},{7,11},{8,12},{9,13},{1... | collective-permute-start | bytes 165896 | tf_op jit(solution)/shard_map/ppermute | solution.py:355
  40.6 15.5 %collective-permute-start.13 = (bf16[3,3,8,384]{3,2,1,0:T(8,128)(2,1)S(1)}, bf16[3,3,8,384]{3,2,1,0:T(8,128)(2,1)S(1)}, u32[]{:S(2)}, u32[]{:S(2)}) collective-permute-start(bf16[3,3,8,384]{3,2,1,0:T(8,128)(2,1)S(1)} %get-tuple-element.84), channel_id=1, source_target_pairs={{0,5},{1,6},{2,7},{3,4},{4,9},{5,10},{6,11},{7,8},{8,13},{9,14},{1... | collective-permute-start | bytes 165896 | tf_op jit(solution)/shard_map/ppermute | solution.py:355
  40.7 7.0 %collective-permute-start.11 = (bf16[2,104,384]{2,1,0:T(8,128)(2,1)S(1)}, bf16[2,104,384]{2,1,0:T(8,128)(2,1)S(1)}, u32[]{:S(2)}, u32[]{:S(2)}) collective-permute-start(bf16[2,104,384]{2,1,0:T(8,128)(2,1)S(1)} %get-tuple-element.111), channel_id=1, source_target_pairs={{0,8},{1,9},{2,10},{3,11},{4,12},{5,13},{6,14},{7,15},{8,0},{9,1},... | collective-permute-start | bytes 479240 | tf_op jit(solution)/shard_map/ppermute | solution.py:396
  46.8 5.2 %collective-permute-start.10 = (bf16[1,192,384]{2,1,0:T(8,128)(2,1)S(1)}, bf16[1,192,384]{2,1,0:T(8,128)(2,1)S(1)}, u32[]{:S(2)}, u32[]{:S(2)}) collective-permute-start(bf16[1,192,384]{2,1,0:T(8,128)(2,1)S(1)} %add_convert_fusion.10), channel_id=1, source_target_pairs={{0,8},{1,5},{2,10},{3,7},{4,12},{5,1},{6,14},{7,3},{8,0},{9,13},{1... | collective-permute-start | bytes 442376 | tf_op jit(solution)/shard_map/ppermute | solution.py:396
  47.8 7.1 %collective-permute-start.14 = (bf16[1,104,384]{2,1,0:T(8,128)(2,1)S(1)}, bf16[1,104,384]{2,1,0:T(8,128)(2,1)S(1)}, u32[]{:S(2)}, u32[]{:S(2)}) collective-permute-start(bf16[1,104,384]{2,1,0:T(8,128)(2,1)S(1)} %add_convert_fusion.15), channel_id=1, source_target_pairs={{0,2},{1,3},{2,0},{3,1},{4,6},{5,7},{6,4},{7,5},{8,10},{9,11},{10,... | collective-permute-start | bytes 239624 | tf_op jit(solution)/shard_map/ppermute | solution.py:396
  52.1 10.1 %collective-permute-start.12 = (bf16[192,384]{1,0:T(8,128)(2,1)S(1)}, bf16[192,384]{1,0:T(8,128)(2,1)S(1)}, u32[]{:S(2)}, u32[]{:S(2)}) collective-permute-start(bf16[192,384]{1,0:T(8,128)(2,1)S(1)} %fusion), channel_id=1, source_target_pairs={{0,16},{1,17},{2,18},{3,19},{4,20},{5,21},{6,22},{7,23},{8,24},{9,... | collective-permute-start | bytes 442376 | tf_op jit(solution)/shard_map/ppermute | solution.py:396
  54.9 8.2 %collective-permute-start.16 = (bf16[104,384]{1,0:T(8,128)(2,1)S(1)}, bf16[104,384]{1,0:T(8,128)(2,1)S(1)}, u32[]{:S(2)}, u32[]{:S(2)}) collective-permute-start(bf16[104,384]{1,0:T(8,128)(2,1)S(1)} %fusion.1), channel_id=1, source_target_pairs={{0,16},{1,17},{2,18},{3,19},{4,20},{5,21},{6,22},{7,23},{8,24},{9,... | collective-permute-start | bytes 239624 | tf_op jit(solution)/shard_map/ppermute | solution.py:396
  63.1 5.1 %collective-permute-start.15 = (bf16[1,192,384]{2,1,0:T(8,128)(2,1)S(1)}, bf16[1,192,384]{2,1,0:T(8,128)(2,1)S(1)}, u32[]{:S(2)}, u32[]{:S(2)}) collective-permute-start(bf16[1,192,384]{2,1,0:T(8,128)(2,1)S(1)} %bitcast.17), channel_id=1, source_target_pairs={{0,8},{1,5},{2,10},{3,7},{4,12},{5,1},{6,14},{7,3},{8,0},{9,13},{1... | collective-permute-start | bytes 442376 | tf_op jit(solution)/shard_map/ppermute | solution.py:396
  63.4 4.5 %collective-permute-start.17 = (bf16[1,104,384]{2,1,0:T(8,128)(2,1)S(1)}, bf16[1,104,384]{2,1,0:T(8,128)(2,1)S(1)}, u32[]{:S(2)}, u32[]{:S(2)}) collective-permute-start(bf16[1,104,384]{2,1,0:T(8,128)(2,1)S(1)} %fusion.2), channel_id=1, source_target_pairs={{0,2},{1,3},{2,0},{3,1},{4,6},{5,7},{6,4},{7,5},{8,10},{9,11},{10,... | collective-permute-start | bytes 239624 | tf_op jit(solution)/shard_map/ppermute | solution.py:396
  68.2 7.1 %collective-permute-start.18 = (bf16[2,192,384]{2,1,0:T(8,128)(2,1)S(1)}, bf16[2,192,384]{2,1,0:T(8,128)(2,1)S(1)}, u32[]{:S(2)}, u32[]{:S(2)}) collective-permute-start(bf16[2,192,384]{2,1,0:T(8,128)(2,1)S(1)} %pad_maximum_fusion.2), channel_id=1, source_target_pairs={{0,4},{1,3},{2,6},{3,1},{4,0},{5,7},{6,2},{7,5},{8,12},{9,11},{10,... | collective-permute-start | bytes 884744 | tf_op jit(solution)/shard_map/ppermute | solution.py:396
  70.0 5.3 %collective-permute-start.19 = (bf16[2,104,384]{2,1,0:T(8,128)(2,1)S(1)}, bf16[2,104,384]{2,1,0:T(8,128)(2,1)S(1)}, u32[]{:S(2)}, u32[]{:S(2)}) collective-permute-start(bf16[2,104,384]{2,1,0:T(8,128)(2,1)S(1)} %pad_maximum_fusion.3), channel_id=1, source_target_pairs={{0,8},{1,9},{2,10},{3,11},{4,12},{5,13},{6,14},{7,15},{8,0},{9,1},... | collective-permute-start | bytes 479240 | tf_op jit(solution)/shard_map/ppermute | solution.py:396
  75.4 9.9 %collective-permute-start.20 = (bf16[4,192,384]{2,1,0:T(8,128)(2,1)S(1)}, bf16[4,192,384]{2,1,0:T(8,128)(2,1)S(1)}, u32[]{:S(2)}, u32[]{:S(2)}) collective-permute-start(bf16[4,192,384]{2,1,0:T(8,128)(2,1)S(1)} %pad_maximum_fusion.refs_5_), channel_id=1, source_target_pairs={{0,2},{1,9},{2,0},{3,11},{4,6},{5,13},{6,4},{7,15},{8,10},{9,1},{1... | collective-permute-start | bytes 1769480 | tf_op jit(solution)/shard_map/ppermute | solution.py:396
  77.1 7.1 %collective-permute-start.21 = (bf16[4,104,384]{2,1,0:T(8,128)(2,1)S(1)}, bf16[4,104,384]{2,1,0:T(8,128)(2,1)S(1)}, u32[]{:S(2)}, u32[]{:S(2)}) collective-permute-start(bf16[4,104,384]{2,1,0:T(8,128)(2,1)S(1)} %pad_maximum_fusion.1.refs_9_), channel_id=1, source_target_pairs={{0,4},{1,5},{2,6},{3,7},{4,0},{5,1},{6,2},{7,3},{8,12},{9,13},{10,... | collective-permute-start | bytes 958472 | tf_op jit(solution)/shard_map/ppermute | solution.py:396
  78.5 9.3 %collective-permute-start.22 = (bf16[4,192,384]{2,1,0:T(8,128)(2,1)S(1)}, bf16[4,192,384]{2,1,0:T(8,128)(2,1)S(1)}, u32[]{:S(2)}, u32[]{:S(2)}) collective-permute-start(bf16[4,192,384]{2,1,0:T(8,128)(2,1)S(1)} %pad_maximum_fusion.refs_5_), channel_id=1, source_target_pairs={{0,1},{1,0},{2,3},{3,2},{4,5},{5,4},{6,7},{7,6},{8,9},{9,8},{10,11... | collective-permute-start | bytes 1769480 | tf_op jit(solution)/shard_map/ppermute | solution.py:396
  85.4 2.9 %collective-permute-start.23 = (bf16[4,192,384]{2,1,0:T(8,128)(2,1)S(1)}, bf16[4,192,384]{2,1,0:T(8,128)(2,1)S(1)}, u32[]{:S(2)}, u32[]{:S(2)}) collective-permute-start(bf16[4,192,384]{2,1,0:T(8,128)(2,1)S(1)} %collective-permute-done.20.refs_6_), channel_id=1, source_target_pairs={{0,1},{1,0},{2,3},{3,2},{4,5},{5,4},{6,7},{7,6},{8,9},{9,8},{10,11... | collective-permute-start | bytes 1769480 | tf_op jit(solution)/shard_map/ppermute | solution.py:396
  85.4 2.5 %collective-permute-start.24 = (bf16[4,104,384]{2,1,0:T(8,128)(2,1)S(1)}, bf16[4,104,384]{2,1,0:T(8,128)(2,1)S(1)}, u32[]{:S(2)}, u32[]{:S(2)}) collective-permute-start(bf16[4,104,384]{2,1,0:T(8,128)(2,1)S(1)} %pad_maximum_fusion.1.refs_9_), channel_id=1, source_target_pairs={{0,1},{1,0},{2,3},{3,2},{4,5},{5,4},{6,7},{7,6},{8,9},{9,8},{10,11... | collective-permute-start | bytes 958472 | tf_op jit(solution)/shard_map/ppermute | solution.py:396
  85.9 2.4 %collective-permute-start.25 = (bf16[4,104,384]{2,1,0:T(8,128)(2,1)S(1)}, bf16[4,104,384]{2,1,0:T(8,128)(2,1)S(1)}, u32[]{:S(2)}, u32[]{:S(2)}) collective-permute-start(bf16[4,104,384]{2,1,0:T(8,128)(2,1)S(1)} %collective-permute-done.21.refs_10_), channel_id=1, source_target_pairs={{0,1},{1,0},{2,3},{3,2},{4,5},{5,4},{6,7},{7,6},{8,9},{9,8},{10,11... | collective-permute-start | bytes 958472 | tf_op jit(solution)/shard_map/ppermute | solution.py:396

commit v6 on v5

--- a/solution.py
+++ b/solution.py
@@ -279,16 +279,18 @@
         left = pl.multiple_of(piece // per_block * width, width)
         return piece, pl.ds(top, rows), pl.ds(left, width)
 
-    for kind in range(2):
-        for i, ref in enumerate(parts[4 * kind : 4 * kind + 4]):
+    for kind in range(3):
+        for i, ref in enumerate(parts[4 * (kind // 2) : 4 * (kind // 2) + 4]):
             core = me[0] ^ (i // 2)
             for j in range(ref.shape[0]):
                 slot = i % 2 * ref.shape[0] + j
                 if kind == 0:
-                    value = (ref[j].astype(F32) * factor).astype(BF16)
-                    piece, down, across = spot(core, 0, slot)
-                    fc2[pl.ds(pl.multiple_of(piece * rows, rows), rows), :] = value[:rows]
-                    fc1[down, across] = value[rows : 2 * rows]
+                    piece, _, _ = spot(core, 0, slot)
+                    value = (ref[j, :rows].astype(F32) * factor).astype(BF16)
+                    fc2[pl.ds(pl.multiple_of(piece * rows, rows), rows), :] = value
+                elif kind == 1:
+                    _, down, across = spot(core, 0, slot)
+                    fc1[down, across] = (ref[j, rows:].astype(F32) * factor).astype(BF16)
                 else:
                     value = ref[j].astype(F32) * factor
                     piece, down, across = spot(core, 1, slot)
@@ -299,6 +301,7 @@
                     smalls[piece] = value[4 * thin :]
         if kind == 0:
             leave(fc2, g_fc2)
+        elif kind == 1:
             leave(fc1, g_fc1)
         else:
             leave(qkv, g_qkv)

time: 92.5 us -> 92.4 us (level)
  no operation moved by 1% of the time
where the time goes in v6:
time: 92.4 us; the launch traced here: 92.2 us
  waiting for transfers between devices  41 us (44%)
  starting transfers between devices  27.1 us (29%)
  Pallas kernels  19.1 us (21%)
  other arithmetic  3.34 us (4%)
  between operations  1.03 us (1%)
    ppermute x20, waiting for transfers between devices, swap(): return lax.ppermute(shard, ('gx', 'gy'), pairs)  31.6 us
    pallas_call x4, Pallas kernels, call(): pl.pallas_call(kernel, out_shape=outs, in_specs=[SMEM] + [VMEM] * len(nea...  19.1 us
    ppermute x20, starting transfers between devices, swap(): return lax.ppermute(shard, ('gx', 'gy'), pairs)  18.8 us
    ppermute x6, waiting for transfers between devices, neighbour(): return lax.ppermute(shard, ('gx', 'gy'), pairs)  9.35 us
    ppermute x6, starting transfers between devices, neighbour(): return lax.ppermute(shard, ('gx', 'gy'), pairs)  8.33 us
  transfers between devices with their start and end apart: 26, of which 14 were waited for; matrix products, arithmetic and copies ran while one was open for 3% of the time, Pallas kernels for 8%

profile of v6, /device:TPU:0, one launch (start us, length us, event | category | flops | bytes accessed | tf_op | source)
XLA Modules:
  0.0 92.2 jit_solution(12875576345139570611)
XLA Ops:
  0.7 1.1 %pad_maximum_fusion.4 = (bf16[2,3,3,8,384]{4,3,2,1,0:T(8,128)(2,1)S(1)}, bf16[2,3,3,8,384]{4,3,2,1,0:T(8,128)(2,1)S(1)}, bf16[2,3,3,8,384]{4,3,2,1,0:T(8,128)(2,1)S(1)}) fusion(bf16[1,6,6,8,384]{4,3,2,1,0:T(8,128)(2,1)} %bitcast.16, bf16[1,6,6,8,384]{4,3,2,1,0:T(8,128)(2,1)} %bitcast.15), kind=kLoop, calls=%fused_computation.21 | loop fusion | flops 165888 | bytes 774144 | tf_op jit(solution)/shard_map/stack | solution.py:495
  1.8 6.4 %collective-permute-start.2 = (bf16[2,3,3,8,384]{4,3,2,1,0:T(8,128)(2,1)S(1)}, bf16[2,3,3,8,384]{4,3,2,1,0:T(8,128)(2,1)S(1)}, u32[]{:S(2)}, u32[]{:S(2)}) collective-permute-start(bf16[2,3,3,8,384]{4,3,2,1,0:T(8,128)(2,1)S(1)} %get-tuple-element.112), channel_id=1, source_target_pairs={{0,31},{1,28},{2,29},{3,30},{4,3},{5,0},{6,1},{7,2},{8,7},{9,4},{1... | collective-permute-start | bytes 331784 | tf_op jit(solution)/shard_map/ppermute | solution.py:358
  8.2 0.5 collective-permute-start.1
  8.7 0.6 collective-permute-start
  9.3 0.8 add_add_fusion
  10.2 0.1 reshape.59
  10.3 0.1 reshape.60
  10.4 0.1 reshape.62
  10.5 0.1 reshape.61
  10.7 0.1 broadcast_in_dim.19.code_col
  10.8 0.1 stack.29.refs_0_.me
  10.9 1.8 %shard_map.161 = (bf16[384,1152]{1,0:T(8,128)(2,1)S(1)}, bf16[384,384]{1,0:T(8,128)(2,1)S(1)}) custom-call(s32[5]{0:T(128)S(1)} %stack.29.refs_0_.me, bf16[384,1152]{1,0:T(8,128)(2,1)} %refs_1_.1, bf16[384,384]{1,0:T(8,128)(2,1)} %refs_2_.1), custom_call_target="tpu_custom_call" | custom-call | bytes 2359316 | tf_op jit(solution)/shard_map/pallas_call | solution.py:340
  12.7 0.4 collective-permute-done.1.part_c
  13.1 8.2 %shard_map.162 = (bf16[8,192,384]{2,1,0:T(8,128)(2,1)S(1)}, bf16[8,192,384]{2,1,0:T(8,128)(2,1)S(1)}, f32[5,384]{1,0:T(8,128)S(1)}, f32[288,384]{1,0:T(8,128)S(1...) custom-call(s32[5]{0:T(128)S(1)} %stack.29.refs_0_.me, ...), custom_call_target="tpu_custom_call" | custom-call | flops 2548039680 | bytes 10674068 | tf_op jit(solution)/shard_map/pallas_call | solution.py:340
  21.4 5.4 %shard_map.163 = (bf16[3,3,8,384]{3,2,1,0:T(8,128)(2,1)S(1)}, bf16[3,3,8,384]{3,2,1,0:T(8,128)(2,1)S(1)}, bf16[3,3,8,384]{3,2,1,0:T(8,128)(2,1)S(1)}, bf16[3,3,8...) custom-call(s32[5]{0:T(128)S(1)} %stack.29.refs_0_.me, ...), custom_call_target="tpu_custom_call" | custom-call | flops 1698693120 | bytes 6670484 | tf_op jit(solution)/shard_map/pallas_call | solution.py:340
  26.8 0.6 collective-permute-start.6
  27.4 0.5 add_convert_fusion
  27.9 1.5 %collective-permute-start.4 = (bf16[4,192,384]{2,1,0:T(8,128)(2,1)S(1)}, bf16[4,192,384]{2,1,0:T(8,128)(2,1)S(1)}, u32[]{:S(2)}, u32[]{:S(2)}) collective-permute-start(bf16[4,192,384]{2,1,0:T(8,128)(2,1)S(1)} %get-tuple-element.105), channel_id=1, source_target_pairs={{0,2},{1,9},{2,0},{3,11},{4,6},{5,13},{6,4},{7,15},{8,10},{9,1},{1... | collective-permute-start | bytes 1769480 | tf_op jit(solution)/shard_map/ppermute | solution.py:399
  29.4 0.2 add_convert_fusion.2
  29.5 0.9 %collective-permute-start.9 = (bf16[4,104,384]{2,1,0:T(8,128)(2,1)S(1)}, bf16[4,104,384]{2,1,0:T(8,128)(2,1)S(1)}, u32[]{:S(2)}, u32[]{:S(2)}) collective-permute-start(bf16[4,104,384]{2,1,0:T(8,128)(2,1)S(1)} %get-tuple-element.107), channel_id=1, source_target_pairs={{0,4},{1,5},{2,6},{3,7},{4,0},{5,1},{6,2},{7,3},{8,12},{9,13},{10,... | collective-permute-start | bytes 958472 | tf_op jit(solution)/shard_map/ppermute | solution.py:399
  30.5 3.0 %collective-permute-done.5.refs_2_ = bf16[3,3,8,384]{3,2,1,0:T(8,128)(2,1)S(1)} collective-permute-done((bf16[3,3,8,384]{3,2,1,0:T(8,128)(2,1)S(1)}, bf16[3,3,8,384]{3,2,1,0:T(8,128)(2,1)S(1)}, u32[]{:S(2)}, u32[]{:S(2)}) %collective-permute-start.5) | collective-permute-done | bytes 55328 | tf_op jit(solution)/shard_map/ppermute | solution.py:358
  33.5 4.9 %collective-permute-done.4 = bf16[4,192,384]{2,1,0:T(8,128)(2,1)S(1)} collective-permute-done((bf16[4,192,384]{2,1,0:T(8,128)(2,1)S(1)}, bf16[4,192,384]{2,1,0:T(8,128)(2,1)S(1)}, u32[]{:S(2)}, u32[]{:S(2)}) %collective-permute-start.4) | collective-permute-done | bytes 589856 | tf_op jit(solution)/shard_map/ppermute | solution.py:399
  38.4 0.2 add_convert_fusion.4
  38.6 1.3 %collective-permute-start.7 = (bf16[2,192,384]{2,1,0:T(8,128)(2,1)S(1)}, bf16[2,192,384]{2,1,0:T(8,128)(2,1)S(1)}, u32[]{:S(2)}, u32[]{:S(2)}) collective-permute-start(bf16[2,192,384]{2,1,0:T(8,128)(2,1)S(1)} %get-tuple-element.109), channel_id=1, source_target_pairs={{0,4},{1,3},{2,6},{3,1},{4,0},{5,7},{6,2},{7,5},{8,12},{9,11},{10,... | collective-permute-start | bytes 884744 | tf_op jit(solution)/shard_map/ppermute | solution.py:399
  39.8 0.8 collective-permute-start.8
  40.8 6.0 %collective-permute-done.8.refs_3_ = bf16[3,3,8,384]{3,2,1,0:T(8,128)(2,1)S(1)} collective-permute-done((bf16[3,3,8,384]{3,2,1,0:T(8,128)(2,1)S(1)}, bf16[3,3,8,384]{3,2,1,0:T(8,128)(2,1)S(1)}, u32[]{:S(2)}, u32[]{:S(2)}) %collective-permute-start.8) | collective-permute-done | bytes 55328 | tf_op jit(solution)/shard_map/ppermute | solution.py:358
  46.8 0.9 %collective-permute-start.10 = (bf16[1,192,384]{2,1,0:T(8,128)(2,1)S(1)}, bf16[1,192,384]{2,1,0:T(8,128)(2,1)S(1)}, u32[]{:S(2)}, u32[]{:S(2)}) collective-permute-start(bf16[1,192,384]{2,1,0:T(8,128)(2,1)S(1)} %add_convert_fusion.10), channel_id=1, source_target_pairs={{0,8},{1,5},{2,10},{3,7},{4,12},{5,1},{6,14},{7,3},{8,0},{9,13},{1... | collective-permute-start | bytes 442376 | tf_op jit(solution)/shard_map/ppermute | solution.py:399
  47.8 1.1 %collective-permute-start.14 = (bf16[1,104,384]{2,1,0:T(8,128)(2,1)S(1)}, bf16[1,104,384]{2,1,0:T(8,128)(2,1)S(1)}, u32[]{:S(2)}, u32[]{:S(2)}) collective-permute-start(bf16[1,104,384]{2,1,0:T(8,128)(2,1)S(1)} %add_convert_fusion.15), channel_id=1, source_target_pairs={{0,2},{1,3},{2,0},{3,1},{4,6},{5,7},{6,4},{7,5},{8,10},{9,11},{10,... | collective-permute-start | bytes 239624 | tf_op jit(solution)/shard_map/ppermute | solution.py:399
  48.8 3.2 %collective-permute-done.10 = bf16[1,192,384]{2,1,0:T(8,128)(2,1)S(1)} collective-permute-done((bf16[1,192,384]{2,1,0:T(8,128)(2,1)S(1)}, bf16[1,192,384]{2,1,0:T(8,128)(2,1)S(1)}, u32[]{:S(2)}, u32[]{:S(2)}) %collective-permute-start.10) | collective-permute-done | bytes 147488 | tf_op jit(solution)/shard_map/ppermute | solution.py:399
  52.1 2.7 %collective-permute-start.12 = (bf16[192,384]{1,0:T(8,128)(2,1)S(1)}, bf16[192,384]{1,0:T(8,128)(2,1)S(1)}, u32[]{:S(2)}, u32[]{:S(2)}) collective-permute-start(bf16[192,384]{1,0:T(8,128)(2,1)S(1)} %fusion), channel_id=1, source_target_pairs={{0,16},{1,17},{2,18},{3,19},{4,20},{5,21},{6,22},{7,23},{8,24},{9,... | collective-permute-start | bytes 442376 | tf_op jit(solution)/shard_map/ppermute | solution.py:399
  54.9 1.3 %collective-permute-start.16 = (bf16[104,384]{1,0:T(8,128)(2,1)S(1)}, bf16[104,384]{1,0:T(8,128)(2,1)S(1)}, u32[]{:S(2)}, u32[]{:S(2)}) collective-permute-start(bf16[104,384]{1,0:T(8,128)(2,1)S(1)} %fusion.1), channel_id=1, source_target_pairs={{0,16},{1,17},{2,18},{3,19},{4,20},{5,21},{6,22},{7,23},{8,24},{9,... | collective-permute-start | bytes 239624 | tf_op jit(solution)/shard_map/ppermute | solution.py:399
  56.2 6.0 %collective-permute-done.12 = bf16[192,384]{1,0:T(8,128)(2,1)S(1)} collective-permute-done((bf16[192,384]{1,0:T(8,128)(2,1)S(1)}, bf16[192,384]{1,0:T(8,128)(2,1)S(1)}, u32[]{:S(2)}, u32[]{:S(2)}) %collective-permute-start.12) | collective-permute-done | bytes 147488 | tf_op jit(solution)/shard_map/ppermute | solution.py:399
  62.2 0.8 collective-permute-done.16
  63.1 0.3 collective-permute-start.15
  63.4 0.9 %collective-permute-start.17 = (bf16[1,104,384]{2,1,0:T(8,128)(2,1)S(1)}, bf16[1,104,384]{2,1,0:T(8,128)(2,1)S(1)}, u32[]{:S(2)}, u32[]{:S(2)}) collective-permute-start(bf16[1,104,384]{2,1,0:T(8,128)(2,1)S(1)} %fusion.2), channel_id=1, source_target_pairs={{0,2},{1,3},{2,0},{3,1},{4,6},{5,7},{6,4},{7,5},{8,10},{9,11},{10,... | collective-permute-start | bytes 239624 | tf_op jit(solution)/shard_map/ppermute | solution.py:399
  64.3 3.6 %collective-permute-done.17 = bf16[1,104,384]{2,1,0:T(8,128)(2,1)S(1)} collective-permute-done((bf16[1,104,384]{2,1,0:T(8,128)(2,1)S(1)}, bf16[1,104,384]{2,1,0:T(8,128)(2,1)S(1)}, u32[]{:S(2)}, u32[]{:S(2)}) %collective-permute-start.17) | collective-permute-done | bytes 79904 | tf_op jit(solution)/shard_map/ppermute | solution.py:399
  67.9 0.3 collective-permute-done.15
  68.2 1.7 %collective-permute-start.18 = (bf16[2,192,384]{2,1,0:T(8,128)(2,1)S(1)}, bf16[2,192,384]{2,1,0:T(8,128)(2,1)S(1)}, u32[]{:S(2)}, u32[]{:S(2)}) collective-permute-start(bf16[2,192,384]{2,1,0:T(8,128)(2,1)S(1)} %pad_maximum_fusion.2), channel_id=1, source_target_pairs={{0,4},{1,3},{2,6},{3,1},{4,0},{5,7},{6,2},{7,5},{8,12},{9,11},{10,... | collective-permute-start | bytes 884744 | tf_op jit(solution)/shard_map/ppermute | solution.py:399
  70.0 1.7 %collective-permute-start.19 = (bf16[2,104,384]{2,1,0:T(8,128)(2,1)S(1)}, bf16[2,104,384]{2,1,0:T(8,128)(2,1)S(1)}, u32[]{:S(2)}, u32[]{:S(2)}) collective-permute-start(bf16[2,104,384]{2,1,0:T(8,128)(2,1)S(1)} %pad_maximum_fusion.3), channel_id=1, source_target_pairs={{0,8},{1,9},{2,10},{3,11},{4,12},{5,13},{6,14},{7,15},{8,0},{9,1},... | collective-permute-start | bytes 479240 | tf_op jit(solution)/shard_map/ppermute | solution.py:399
  71.7 3.6 %collective-permute-done.19 = bf16[2,104,384]{2,1,0:T(8,128)(2,1)S(1)} collective-permute-done((bf16[2,104,384]{2,1,0:T(8,128)(2,1)S(1)}, bf16[2,104,384]{2,1,0:T(8,128)(2,1)S(1)}, u32[]{:S(2)}, u32[]{:S(2)}) %collective-permute-start.19) | collective-permute-done | bytes 159776 | tf_op jit(solution)/shard_map/ppermute | solution.py:399
  75.4 1.6 %collective-permute-start.20 = (bf16[4,192,384]{2,1,0:T(8,128)(2,1)S(1)}, bf16[4,192,384]{2,1,0:T(8,128)(2,1)S(1)}, u32[]{:S(2)}, u32[]{:S(2)}) collective-permute-start(bf16[4,192,384]{2,1,0:T(8,128)(2,1)S(1)} %pad_maximum_fusion.refs_5_), channel_id=1, source_target_pairs={{0,2},{1,9},{2,0},{3,11},{4,6},{5,13},{6,4},{7,15},{8,10},{9,1},{1... | collective-permute-start | bytes 1769480 | tf_op jit(solution)/shard_map/ppermute | solution.py:399
  77.1 1.4 %collective-permute-start.21 = (bf16[4,104,384]{2,1,0:T(8,128)(2,1)S(1)}, bf16[4,104,384]{2,1,0:T(8,128)(2,1)S(1)}, u32[]{:S(2)}, u32[]{:S(2)}) collective-permute-start(bf16[4,104,384]{2,1,0:T(8,128)(2,1)S(1)} %pad_maximum_fusion.1.refs_9_), channel_id=1, source_target_pairs={{0,4},{1,5},{2,6},{3,7},{4,0},{5,1},{6,2},{7,3},{8,12},{9,13},{10,... | collective-permute-start | bytes 958472 | tf_op jit(solution)/shard_map/ppermute | solution.py:399
  78.5 5.6 %collective-permute-done.21.refs_10_ = bf16[4,104,384]{2,1,0:T(8,128)(2,1)S(1)} collective-permute-done((bf16[4,104,384]{2,1,0:T(8,128)(2,1)S(1)}, bf16[4,104,384]{2,1,0:T(8,128)(2,1)S(1)}, u32[]{:S(2)}, u32[]{:S(2)}) %collective-permute-start.21) | collective-permute-done | bytes 319520 | tf_op jit(solution)/shard_map/ppermute | solution.py:399
  84.2 1.2 %collective-permute-done.20.refs_6_ = bf16[4,192,384]{2,1,0:T(8,128)(2,1)S(1)} collective-permute-done((bf16[4,192,384]{2,1,0:T(8,128)(2,1)S(1)}, bf16[4,192,384]{2,1,0:T(8,128)(2,1)S(1)}, u32[]{:S(2)}, u32[]{:S(2)}) %collective-permute-start.20) | collective-permute-done | bytes 589856 | tf_op jit(solution)/shard_map/ppermute | solution.py:399
  85.4 0.5 collective-permute-start.24
  85.9 1.9 %collective-permute-done.24.refs_11_ = bf16[4,104,384]{2,1,0:T(8,128)(2,1)S(1)} collective-permute-done((bf16[4,104,384]{2,1,0:T(8,128)(2,1)S(1)}, bf16[4,104,384]{2,1,0:T(8,128)(2,1)S(1)}, u32[]{:S(2)}, u32[]{:S(2)}) %collective-permute-start.24) | collective-permute-done | bytes 319520 | tf_op jit(solution)/shard_map/ppermute | solution.py:399
  87.8 0.5 collective-permute-done.25.refs_12_
  88.3 3.8 %shard_map.164 = (bf16[6,6,8,384]{3,2,1,0:T(8,128)(2,1)}, f32[384]{0:T(512)}, bf16[16,24,1152]{2,1,0:T(8,128)(2,1)}, bf16[16,24,384]{2,1,0:T(8,128)(2,1)}, f32[3...) custom-call(s32[5]{0:T(128)S(1)} %stack.29.refs_0_.me, ...), custom_call_target="tpu_custom_call" | custom-call | flops 589824 | bytes 7627796 | tf_op jit(solution)/shard_map/pallas_call | solution.py:340
  (46 shorter events, 0.9 us)
Async XLA Ops:
  0.6 12.4 %copy-start = (bf16[6,6,8,384]{3,2,1,0:T(8,128)(2,1)S(1)}, bf16[6,6,8,384]{3,2,1,0:T(8,128)(2,1)}, u32[]{:S(2)}) copy-start(bf16[6,6,8,384]{3,2,1,0:T(8,128)(2,1)} %tok.1) | copy-start | bytes 663556
  0.6 12.4 %copy-start.1 = (bf16[6,6,8,384]{3,2,1,0:T(8,128)(2,1)S(1)}, bf16[6,6,8,384]{3,2,1,0:T(8,128)(2,1)}, u32[]{:S(2)}) copy-start(bf16[6,6,8,384]{3,2,1,0:T(8,128)(2,1)} %up_own.1) | copy-start | bytes 663556
  0.7 12.4 %copy-start.2 = (f32[1536]{0:T(1024)S(1)}, f32[1536]{0:T(1024)}, u32[]{:S(2)}) copy-start(f32[1536]{0:T(1024)} %b_fc1.1) | copy-start | bytes 18436
  0.7 12.4 %copy-start.3 = (f32[384]{0:T(512)S(1)}, f32[384]{0:T(512)}, u32[]{:S(2)}) copy-start(f32[384]{0:T(512)} %gain2.1) | copy-start | bytes 4612
  0.7 12.4 %copy-start.4 = (f32[384]{0:T(512)S(1)}, f32[384]{0:T(512)}, u32[]{:S(2)}) copy-start(f32[384]{0:T(512)} %gain1.3) | copy-start | bytes 4612
  1.8 10.9 %collective-permute-start.2 = (bf16[2,3,3,8,384]{4,3,2,1,0:T(8,128)(2,1)S(1)}, bf16[2,3,3,8,384]{4,3,2,1,0:T(8,128)(2,1)S(1)}, u32[]{:S(2)}, u32[]{:S(2)}) collective-permute-start(bf16[2,3,3,8,384]{4,3,2,1,0:T(8,128)(2,1)S(1)} %get-tuple-element.112), channel_id=1, source_target_pairs={{0,31},{1,28},{2,29},{3,30},{4,3},{5,0},{6,1},{7,2},{8,7},{9,4},{1... | collective-permute-start | bytes 331784 | tf_op jit(solution)/shard_map/ppermute | solution.py:358
  8.2 4.9 %collective-permute-start.1 = (bf16[2,3,3,8,384]{4,3,2,1,0:T(8,128)(2,1)S(1)}, bf16[2,3,3,8,384]{4,3,2,1,0:T(8,128)(2,1)S(1)}, u32[]{:S(2)}, u32[]{:S(2)}) collective-permute-start(bf16[2,3,3,8,384]{4,3,2,1,0:T(8,128)(2,1)S(1)} %get-tuple-element.113), channel_id=1, source_target_pairs={{0,28},{1,29},{2,30},{3,31},{4,0},{5,1},{6,2},{7,3},{8,4},{9,5},{1... | collective-permute-start | bytes 331784 | tf_op jit(solution)/shard_map/ppermute | solution.py:358
  8.7 4.4 %collective-permute-start = (bf16[2,3,3,8,384]{4,3,2,1,0:T(8,128)(2,1)S(1)}, bf16[2,3,3,8,384]{4,3,2,1,0:T(8,128)(2,1)S(1)}, u32[]{:S(2)}, u32[]{:S(2)}) collective-permute-start(bf16[2,3,3,8,384]{4,3,2,1,0:T(8,128)(2,1)S(1)} %get-tuple-element.114), channel_id=1, source_target_pairs={{0,3},{1,0},{2,1},{3,2},{4,7},{5,4},{6,5},{7,6},{8,11},{9,8},{10,9... | collective-permute-start | bytes 331784 | tf_op jit(solution)/shard_map/ppermute | solution.py:358
  21.3 6.1 %collective-permute-start.3 = (bf16[8,192,384]{2,1,0:T(8,128)(2,1)S(1)}, bf16[8,192,384]{2,1,0:T(8,128)(2,1)S(1)}, u32[]{:S(2)}, u32[]{:S(2)}) collective-permute-start(bf16[8,192,384]{2,1,0:T(8,128)(2,1)S(1)} %get-tuple-element.70), channel_id=1, source_target_pairs={{0,1},{1,0},{2,3},{3,2},{4,5},{5,4},{6,7},{7,6},{8,9},{9,8},{10,11... | collective-permute-start | bytes 3538952 | tf_op jit(solution)/shard_map/ppermute | solution.py:399
  26.8 2.6 %collective-permute-start.6 = (bf16[8,104,384]{2,1,0:T(8,128)(2,1)S(1)}, bf16[8,104,384]{2,1,0:T(8,128)(2,1)S(1)}, u32[]{:S(2)}, u32[]{:S(2)}) collective-permute-start(bf16[8,104,384]{2,1,0:T(8,128)(2,1)S(1)} %get-tuple-element.74), channel_id=1, source_target_pairs={{0,1},{1,0},{2,3},{3,2},{4,5},{5,4},{6,7},{7,6},{8,9},{9,8},{10,11... | collective-permute-start | bytes 1916936 | tf_op jit(solution)/shard_map/ppermute | solution.py:399
  27.9 10.5 %collective-permute-start.4 = (bf16[4,192,384]{2,1,0:T(8,128)(2,1)S(1)}, bf16[4,192,384]{2,1,0:T(8,128)(2,1)S(1)}, u32[]{:S(2)}, u32[]{:S(2)}) collective-permute-start(bf16[4,192,384]{2,1,0:T(8,128)(2,1)S(1)} %get-tuple-element.105), channel_id=1, source_target_pairs={{0,2},{1,9},{2,0},{3,11},{4,6},{5,13},{6,4},{7,15},{8,10},{9,1},{1... | collective-permute-start | bytes 1769480 | tf_op jit(solution)/shard_map/ppermute | solution.py:399
  29.4 4.2 %collective-permute-start.5 = (bf16[3,3,8,384]{3,2,1,0:T(8,128)(2,1)S(1)}, bf16[3,3,8,384]{3,2,1,0:T(8,128)(2,1)S(1)}, u32[]{:S(2)}, u32[]{:S(2)}) collective-permute-start(bf16[3,3,8,384]{3,2,1,0:T(8,128)(2,1)S(1)} %get-tuple-element.73), channel_id=1, source_target_pairs={{0,1},{1,2},{2,3},{3,0},{4,5},{5,6},{6,7},{7,4},{8,9},{9,10},{10,1... | collective-permute-start | bytes 165896 | tf_op jit(solution)/shard_map/ppermute | solution.py:358
  29.5 11.1 %collective-permute-start.9 = (bf16[4,104,384]{2,1,0:T(8,128)(2,1)S(1)}, bf16[4,104,384]{2,1,0:T(8,128)(2,1)S(1)}, u32[]{:S(2)}, u32[]{:S(2)}) collective-permute-start(bf16[4,104,384]{2,1,0:T(8,128)(2,1)S(1)} %get-tuple-element.107), channel_id=1, source_target_pairs={{0,4},{1,5},{2,6},{3,7},{4,0},{5,1},{6,2},{7,3},{8,12},{9,13},{10,... | collective-permute-start | bytes 958472 | tf_op jit(solution)/shard_map/ppermute | solution.py:399
  38.6 8.2 %collective-permute-start.7 = (bf16[2,192,384]{2,1,0:T(8,128)(2,1)S(1)}, bf16[2,192,384]{2,1,0:T(8,128)(2,1)S(1)}, u32[]{:S(2)}, u32[]{:S(2)}) collective-permute-start(bf16[2,192,384]{2,1,0:T(8,128)(2,1)S(1)} %get-tuple-element.109), channel_id=1, source_target_pairs={{0,4},{1,3},{2,6},{3,1},{4,0},{5,7},{6,2},{7,5},{8,12},{9,11},{10,... | collective-permute-start | bytes 884744 | tf_op jit(solution)/shard_map/ppermute | solution.py:399
  39.8 7.0 %collective-permute-start.8 = (bf16[3,3,8,384]{3,2,1,0:T(8,128)(2,1)S(1)}, bf16[3,3,8,384]{3,2,1,0:T(8,128)(2,1)S(1)}, u32[]{:S(2)}, u32[]{:S(2)}) collective-permute-start(bf16[3,3,8,384]{3,2,1,0:T(8,128)(2,1)S(1)} %get-tuple-element.78), channel_id=1, source_target_pairs={{0,4},{1,5},{2,6},{3,7},{4,8},{5,9},{6,10},{7,11},{8,12},{9,13},{1... | collective-permute-start | bytes 165896 | tf_op jit(solution)/shard_map/ppermute | solution.py:358
  40.6 15.5 %collective-permute-start.13 = (bf16[3,3,8,384]{3,2,1,0:T(8,128)(2,1)S(1)}, bf16[3,3,8,384]{3,2,1,0:T(8,128)(2,1)S(1)}, u32[]{:S(2)}, u32[]{:S(2)}) collective-permute-start(bf16[3,3,8,384]{3,2,1,0:T(8,128)(2,1)S(1)} %get-tuple-element.84), channel_id=1, source_target_pairs={{0,5},{1,6},{2,7},{3,4},{4,9},{5,10},{6,11},{7,8},{8,13},{9,14},{1... | collective-permute-start | bytes 165896 | tf_op jit(solution)/shard_map/ppermute | solution.py:358
  40.7 7.0 %collective-permute-start.11 = (bf16[2,104,384]{2,1,0:T(8,128)(2,1)S(1)}, bf16[2,104,384]{2,1,0:T(8,128)(2,1)S(1)}, u32[]{:S(2)}, u32[]{:S(2)}) collective-permute-start(bf16[2,104,384]{2,1,0:T(8,128)(2,1)S(1)} %get-tuple-element.111), channel_id=1, source_target_pairs={{0,8},{1,9},{2,10},{3,11},{4,12},{5,13},{6,14},{7,15},{8,0},{9,1},... | collective-permute-start | bytes 479240 | tf_op jit(solution)/shard_map/ppermute | solution.py:399
  46.8 5.2 %collective-permute-start.10 = (bf16[1,192,384]{2,1,0:T(8,128)(2,1)S(1)}, bf16[1,192,384]{2,1,0:T(8,128)(2,1)S(1)}, u32[]{:S(2)}, u32[]{:S(2)}) collective-permute-start(bf16[1,192,384]{2,1,0:T(8,128)(2,1)S(1)} %add_convert_fusion.10), channel_id=1, source_target_pairs={{0,8},{1,5},{2,10},{3,7},{4,12},{5,1},{6,14},{7,3},{8,0},{9,13},{1... | collective-permute-start | bytes 442376 | tf_op jit(solution)/shard_map/ppermute | solution.py:399
  47.8 7.1 %collective-permute-start.14 = (bf16[1,104,384]{2,1,0:T(8,128)(2,1)S(1)}, bf16[1,104,384]{2,1,0:T(8,128)(2,1)S(1)}, u32[]{:S(2)}, u32[]{:S(2)}) collective-permute-start(bf16[1,104,384]{2,1,0:T(8,128)(2,1)S(1)} %add_convert_fusion.15), channel_id=1, source_target_pairs={{0,2},{1,3},{2,0},{3,1},{4,6},{5,7},{6,4},{7,5},{8,10},{9,11},{10,... | collective-permute-start | bytes 239624 | tf_op jit(solution)/shard_map/ppermute | solution.py:399
  52.1 10.1 %collective-permute-start.12 = (bf16[192,384]{1,0:T(8,128)(2,1)S(1)}, bf16[192,384]{1,0:T(8,128)(2,1)S(1)}, u32[]{:S(2)}, u32[]{:S(2)}) collective-permute-start(bf16[192,384]{1,0:T(8,128)(2,1)S(1)} %fusion), channel_id=1, source_target_pairs={{0,16},{1,17},{2,18},{3,19},{4,20},{5,21},{6,22},{7,23},{8,24},{9,... | collective-permute-start | bytes 442376 | tf_op jit(solution)/shard_map/ppermute | solution.py:399
  54.9 8.2 %collective-permute-start.16 = (bf16[104,384]{1,0:T(8,128)(2,1)S(1)}, bf16[104,384]{1,0:T(8,128)(2,1)S(1)}, u32[]{:S(2)}, u32[]{:S(2)}) collective-permute-start(bf16[104,384]{1,0:T(8,128)(2,1)S(1)} %fusion.1), channel_id=1, source_target_pairs={{0,16},{1,17},{2,18},{3,19},{4,20},{5,21},{6,22},{7,23},{8,24},{9,... | collective-permute-start | bytes 239624 | tf_op jit(solution)/shard_map/ppermute | solution.py:399
  63.1 5.1 %collective-permute-start.15 = (bf16[1,192,384]{2,1,0:T(8,128)(2,1)S(1)}, bf16[1,192,384]{2,1,0:T(8,128)(2,1)S(1)}, u32[]{:S(2)}, u32[]{:S(2)}) collective-permute-start(bf16[1,192,384]{2,1,0:T(8,128)(2,1)S(1)} %bitcast.17), channel_id=1, source_target_pairs={{0,8},{1,5},{2,10},{3,7},{4,12},{5,1},{6,14},{7,3},{8,0},{9,13},{1... | collective-permute-start | bytes 442376 | tf_op jit(solution)/shard_map/ppermute | solution.py:399
  63.4 4.5 %collective-permute-start.17 = (bf16[1,104,384]{2,1,0:T(8,128)(2,1)S(1)}, bf16[1,104,384]{2,1,0:T(8,128)(2,1)S(1)}, u32[]{:S(2)}, u32[]{:S(2)}) collective-permute-start(bf16[1,104,384]{2,1,0:T(8,128)(2,1)S(1)} %fusion.2), channel_id=1, source_target_pairs={{0,2},{1,3},{2,0},{3,1},{4,6},{5,7},{6,4},{7,5},{8,10},{9,11},{10,... | collective-permute-start | bytes 239624 | tf_op jit(solution)/shard_map/ppermute | solution.py:399
  68.2 7.1 %collective-permute-start.18 = (bf16[2,192,384]{2,1,0:T(8,128)(2,1)S(1)}, bf16[2,192,384]{2,1,0:T(8,128)(2,1)S(1)}, u32[]{:S(2)}, u32[]{:S(2)}) collective-permute-start(bf16[2,192,384]{2,1,0:T(8,128)(2,1)S(1)} %pad_maximum_fusion.2), channel_id=1, source_target_pairs={{0,4},{1,3},{2,6},{3,1},{4,0},{5,7},{6,2},{7,5},{8,12},{9,11},{10,... | collective-permute-start | bytes 884744 | tf_op jit(solution)/shard_map/ppermute | solution.py:399
  70.0 5.3 %collective-permute-start.19 = (bf16[2,104,384]{2,1,0:T(8,128)(2,1)S(1)}, bf16[2,104,384]{2,1,0:T(8,128)(2,1)S(1)}, u32[]{:S(2)}, u32[]{:S(2)}) collective-permute-start(bf16[2,104,384]{2,1,0:T(8,128)(2,1)S(1)} %pad_maximum_fusion.3), channel_id=1, source_target_pairs={{0,8},{1,9},{2,10},{3,11},{4,12},{5,13},{6,14},{7,15},{8,0},{9,1},... | collective-permute-start | bytes 479240 | tf_op jit(solution)/shard_map/ppermute | solution.py:399
  75.4 9.9 %collective-permute-start.20 = (bf16[4,192,384]{2,1,0:T(8,128)(2,1)S(1)}, bf16[4,192,384]{2,1,0:T(8,128)(2,1)S(1)}, u32[]{:S(2)}, u32[]{:S(2)}) collective-permute-start(bf16[4,192,384]{2,1,0:T(8,128)(2,1)S(1)} %pad_maximum_fusion.refs_5_), channel_id=1, source_target_pairs={{0,2},{1,9},{2,0},{3,11},{4,6},{5,13},{6,4},{7,15},{8,10},{9,1},{1... | collective-permute-start | bytes 1769480 | tf_op jit(solution)/shard_map/ppermute | solution.py:399
  77.1 7.1 %collective-permute-start.21 = (bf16[4,104,384]{2,1,0:T(8,128)(2,1)S(1)}, bf16[4,104,384]{2,1,0:T(8,128)(2,1)S(1)}, u32[]{:S(2)}, u32[]{:S(2)}) collective-permute-start(bf16[4,104,384]{2,1,0:T(8,128)(2,1)S(1)} %pad_maximum_fusion.1.refs_9_), channel_id=1, source_target_pairs={{0,4},{1,5},{2,6},{3,7},{4,0},{5,1},{6,2},{7,3},{8,12},{9,13},{10,... | collective-permute-start | bytes 958472 | tf_op jit(solution)/shard_map/ppermute | solution.py:399
  78.5 9.3 %collective-permute-start.22 = (bf16[4,192,384]{2,1,0:T(8,128)(2,1)S(1)}, bf16[4,192,384]{2,1,0:T(8,128)(2,1)S(1)}, u32[]{:S(2)}, u32[]{:S(2)}) collective-permute-start(bf16[4,192,384]{2,1,0:T(8,128)(2,1)S(1)} %pad_maximum_fusion.refs_5_), channel_id=1, source_target_pairs={{0,1},{1,0},{2,3},{3,2},{4,5},{5,4},{6,7},{7,6},{8,9},{9,8},{10,11... | collective-permute-start | bytes 1769480 | tf_op jit(solution)/shard_map/ppermute | solution.py:399
  85.4 2.9 %collective-permute-start.23 = (bf16[4,192,384]{2,1,0:T(8,128)(2,1)S(1)}, bf16[4,192,384]{2,1,0:T(8,128)(2,1)S(1)}, u32[]{:S(2)}, u32[]{:S(2)}) collective-permute-start(bf16[4,192,384]{2,1,0:T(8,128)(2,1)S(1)} %collective-permute-done.20.refs_6_), channel_id=1, source_target_pairs={{0,1},{1,0},{2,3},{3,2},{4,5},{5,4},{6,7},{7,6},{8,9},{9,8},{10,11... | collective-permute-start | bytes 1769480 | tf_op jit(solution)/shard_map/ppermute | solution.py:399
  85.4 2.5 %collective-permute-start.24 = (bf16[4,104,384]{2,1,0:T(8,128)(2,1)S(1)}, bf16[4,104,384]{2,1,0:T(8,128)(2,1)S(1)}, u32[]{:S(2)}, u32[]{:S(2)}) collective-permute-start(bf16[4,104,384]{2,1,0:T(8,128)(2,1)S(1)} %pad_maximum_fusion.1.refs_9_), channel_id=1, source_target_pairs={{0,1},{1,0},{2,3},{3,2},{4,5},{5,4},{6,7},{7,6},{8,9},{9,8},{10,11... | collective-permute-start | bytes 958472 | tf_op jit(solution)/shard_map/ppermute | solution.py:399
  85.9 2.4 %collective-permute-start.25 = (bf16[4,104,384]{2,1,0:T(8,128)(2,1)S(1)}, bf16[4,104,384]{2,1,0:T(8,128)(2,1)S(1)}, u32[]{:S(2)}, u32[]{:S(2)}) collective-permute-start(bf16[4,104,384]{2,1,0:T(8,128)(2,1)S(1)} %collective-permute-done.21.refs_10_), channel_id=1, source_target_pairs={{0,1},{1,0},{2,3},{3,2},{4,5},{5,4},{6,7},{7,6},{8,9},{9,8},{10,11... | collective-permute-start | bytes 958472 | tf_op jit(solution)/shard_map/ppermute | solution.py:399
